TPU v7x, 32 devices: a whole 2x2x4 slice. The times are simulated.
32 devices in a mesh: cfg: 2 (over x), ctx: 8 (over z, y), tp: 2 (over core).
Axes of the slice: x: 2, y: 2, z: 4, core: 2. Of those that a mesh axis runs over, the one named last changes fastest.
Arguments:
- query_proj: bfloat16 [2, 2048, 3072], P('cfg', 'ctx', 'tp'), may hold values from -8 to 8
- key_proj: bfloat16 [2, 2048, 3072], P('cfg', 'ctx', 'tp'), may hold values from -8 to 8
- value_proj: bfloat16 [2, 2048, 3072], P('cfg', 'ctx', 'tp'), may hold values from -6 to 6
- query_gain: float32 [128], replicated, may hold values from 1 to 8
- key_gain: float32 [128], replicated, may hold values from 1 to 8
- block_input: bfloat16 [2, 2048, 3072], P('cfg', ('ctx', 'tp')), may hold values from -120 to 120
- cached_out: bfloat16 [2, 2048, 3072], P('cfg', ('ctx', 'tp')), may hold values from -120 to 120
- replay_mask: int32 [2, 2048], P('cfg', 'ctx'), may hold values from 0 to 1, as said below
- branch_gate: float32 [2, 3072], P('cfg'), may hold values from 1 to 4
- attn_weight: bfloat16 [3072, 3072], P('tp'), may hold values from -0.109375 to 0.109375
- final_shift: float32 [2, 3072], P('cfg'), may hold values from -4 to 4
- final_scale: float32 [2, 3072], P('cfg'), may hold values from -2 to 2
- patch_weight: bfloat16 [3072, 64], replicated, may hold values from -0.109375 to 0.109375
Outputs:
- block_out: bfloat16 [2, 2048, 3072], P('cfg', ('ctx', 'tp'))
- velocity: float32 [2048, 64], P(('ctx', 'tp'), 'cfg')
Inputs may be any that keep to these rules, and one draw needn't show every extreme that they name: `replay_mask`: in each branch, at most 128 of the 256 rows of one index of ctx have a 0, and some index of ctx has exactly 128.
All inputs are finite; a program needn't handle non-finite values.
Results may differ from a plain program's by a relative error of at most 0.0097.
Values may be sent and summed in bfloat16 or wider, within the bound.
No kernel may reach another device: no remote copies, remote signals or barrier semaphores. Data moves between devices by JAX's collectives and lax.ppermute only.
A program may use at most 128 MiB of HBM per device.

v0:
```python
import functools
import math

import jax
import jax.numpy as jnp
from jax import lax
from jax.experimental import pallas as pl
from jax.experimental.pallas import tpu as pltpu
from jax.sharding import PartitionSpec as P


guidance_scale = 3.0
VMEM = pl.BlockSpec(memory_space=pltpu.VMEM)
HBM = pl.BlockSpec(memory_space=pltpu.HBM)
NT = (((1,), (1,)), ((), ()))


def in_hbm(value):
    return pltpu.with_memory_space_constraint(value, pltpu.HBM)


def dot_f32(a, b):
    return jnp.dot(a, b, preferred_element_type=jnp.float32)


def dot_nt(a, b):
    return lax.dot_general(a, b, NT, preferred_element_type=jnp.float32)


def live_lanes(mask_ref):
    return jnp.where(mask_ref[...] == 1, 0.0, 1.0)


def pick_matrix(mask_ref, live_count):
    live = live_lanes(mask_ref)
    count = live.shape[1]
    rows = lax.broadcasted_iota(jnp.int32, (count, count), 0)
    cols = lax.broadcasted_iota(jnp.int32, (count, count), 1)
    upto = jnp.where(rows <= cols, 1.0, 0.0).astype(jnp.bfloat16)
    wide = jnp.broadcast_to(live, (8, count)).astype(jnp.bfloat16)
    rank = dot_f32(wide, upto)[0:1]
    slot = lax.broadcasted_iota(jnp.int32, (live_count, count), 0).astype(jnp.float32)
    hit = (jnp.broadcast_to(rank, slot.shape) == slot + 1.0) & (jnp.broadcast_to(live, slot.shape) > 0.5)
    return jnp.where(hit, 1.0, 0.0).astype(jnp.bfloat16)


def place_matrix(mask_ref, live_count, first, share):
    live = live_lanes(mask_ref)
    count = live.shape[1]
    wide = jnp.broadcast_to(live, (live_count, count)).astype(jnp.bfloat16)
    rows = lax.broadcasted_iota(jnp.int32, (share, count), 0) + first
    cols = lax.broadcasted_iota(jnp.int32, (share, count), 1)
    rank = dot_nt(jnp.where(cols <= rows, 1.0, 0.0).astype(jnp.bfloat16), wide)
    alive = dot_nt(jnp.where(cols == rows, 1.0, 0.0).astype(jnp.bfloat16), wide)
    slot = lax.broadcasted_iota(jnp.int32, (share, live_count), 1).astype(jnp.float32)
    hit = (rank == slot + 1.0) & (alive > 0.5)
    return jnp.where(hit, 1.0, 0.0).astype(jnp.bfloat16)


def ring_place(members):
    return lax.rem(lax.axis_index("ctx"), members)


def unit_rows(raw, gain):
    lifted = raw.astype(jnp.float32)
    mean_square = jnp.mean(lifted * lifted, axis=-1, keepdims=True)
    return (lifted * lax.rsqrt(mean_square + 1e-06) * gain).astype(jnp.bfloat16)


def split_kernel(dims, k_hbm, v_hbm, *refs):
    members, width, depth = dims
    outs, sems = refs[:members], refs[members]
    count = k_hbm.shape[0]
    position = ring_place(members)
    copies = []
    for b in [b for b in range(1, members)] + [0]:
        columns = pl.ds(pl.multiple_of(lax.rem(position + b, members) * width, depth), width)
        for n, source in enumerate((k_hbm, v_hbm)):
            target = outs[b].at[pl.ds(n * count, count), :]
            copies.append(pltpu.make_async_copy(source.at[:, columns], target, sems.at[n, b]))
    for copy in copies:
        copy.start()
    for copy in copies:
        copy.wait()


def ask_kernel(dims, mask_hbm, gain_hbm, q_hbm, *refs):
    members, own_heads, depth, live_count = dims
    asks = refs[1 : members + 1]
    mask_ref, gain_ref, q_ref, small_sems, q_sems = refs[members + 1 :]
    width = own_heads * depth
    position = ring_place(members)
    small = [
        pltpu.make_async_copy(mask_hbm, mask_ref, small_sems.at[0]),
        pltpu.make_async_copy(gain_hbm, gain_ref, small_sems.at[1]),
    ]
    for copy in small:
        copy.start()
    order = [b for b in range(1, members)] + [0]
    loads = {}
    for b in order:
        columns = pl.ds(pl.multiple_of(lax.rem(position + b, members) * width, depth), width)
        loads[b] = pltpu.make_async_copy(q_hbm.at[:, columns], q_ref.at[b], q_sems.at[b])
        loads[b].start()
    for copy in small:
        copy.wait()
    picks = pick_matrix(mask_ref, live_count)
    gain = gain_ref[...]
    for b in order:
        loads[b].wait()
        picked = dot_f32(picks, q_ref[b])
        for h in range(own_heads):
            columns = slice(h * depth, (h + 1) * depth)
            asks[b][:, columns] = unit_rows(picked[:, columns], gain)


def unit_kernel(depth, gain_ref, *refs):
    pairs, out_ref = refs[:-1], refs[-1]
    count = out_ref.shape[0] // len(pairs)
    gain = gain_ref[...]
    for b, ref in enumerate(pairs):
        for first in range(0, out_ref.shape[1], depth):
            columns = slice(first, first + depth)
            out_ref[pl.ds(b * count, count), columns] = unit_rows(ref[pl.ds(0, count), columns], gain)


def fetch_kernel(dims, *refs):
    n, live_count, parts = dims
    sources, targets, places_ref, sems = refs[:n], refs[n + 1 : 2 * n + 1], refs[2 * n + 1], refs[2 * n + 2]
    copies = [pltpu.make_async_copy(s, t, sems.at[i]) for i, (s, t) in enumerate(zip(sources, targets))]
    for copy in copies:
        copy.start()
    mask_ref = targets[0]
    copies[0].wait()
    share = places_ref.shape[1]
    for s in range(parts):
        first = lax.rem(lax.axis_index("tp") + s, parts) * share
        places_ref[s] = place_matrix(mask_ref, live_count, first, share)
    for copy in copies[1:]:
        copy.wait()


def attend_kernel(dims, *refs):
    members, partial, own_heads, depth, live_count, count, stat_rows, sources = dims
    pairs, units_ref = refs[1 : members + 1], refs[members + 1]
    asks = refs[members + 2 : members + 2 + sources]
    outs, stats = refs[members + 2 + sources : -1], refs[-1]
    factor = depth ** (-0.5)
    power = factor * math.log2(math.e)
    lanes = lax.broadcasted_iota(jnp.int32, (live_count, stats.shape[2]), 1)
    if partial:
        stats[...] = jnp.zeros_like(stats)
    batch = 2 if sources % 2 == 0 else 1

    def one_head(h, carry):
        columns = pl.ds(pl.multiple_of(h * depth, depth), depth)
        keys = [units_ref[pl.ds(b * count, count), columns] for b in range(members)]
        values = [ref[pl.ds(count, count), columns] for ref in pairs]
        for first in range(0, sources, batch):
            chosen = range(first, first + batch)
            parts = [asks[s][:, columns] for s in chosen]
            queries = jnp.concatenate(parts, axis=0) if batch > 1 else parts[0]
            scores = [dot_nt(queries, k) for k in keys]
            biggest = functools.reduce(jnp.maximum, scores)
            biggest = jnp.max(biggest, axis=-1, keepdims=True)
            weights = [jnp.exp2((s - biggest) * power) for s in scores]
            totals = jnp.sum(functools.reduce(jnp.add, weights), axis=-1, keepdims=True)
            summed = functools.reduce(jnp.add, [dot_f32(w.astype(jnp.bfloat16), v) for w, v in zip(weights, values)])
            attended = (summed / totals).astype(jnp.bfloat16)
            logged = biggest * factor + jnp.log(totals)
            for n, s in enumerate(chosen):
                rows = slice(n * live_count, (n + 1) * live_count)
                outs[s][pl.ds(pl.multiple_of(h * live_count, live_count), live_count), :] = attended[rows]
                if partial:
                    rest = logged[rows]
                    for piece in range(3):
                        rounded = rest.astype(jnp.bfloat16).astype(jnp.float32)
                        stats[s] = jnp.where(lanes == piece * own_heads + h, rounded, stats[s])
                        rest = rest - rounded
        return carry

    lax.fori_loop(0, own_heads, one_head, 0)
    if partial:
        for s in range(sources):
            turned = jnp.transpose(stats[s])[:stat_rows]
            outs[s][pl.ds(own_heads * live_count, stat_rows), :] = turned.astype(jnp.bfloat16)


def merge_kernel(dims, places_ref, weight_ref, *refs):
    members, groups, own_heads, depth, live_count, stat_rows, parts = dims
    sources = members * groups
    parcels = refs[:sources]
    sends = refs[sources : sources + parts - 1]
    own_ref, attended_ref = refs[sources + parts - 1 :]
    width = own_heads * depth
    position = ring_place(members)
    for b in range(members):
        logged = []
        if groups > 1:
            for a in range(groups):
                stat = parcels[a * members + b][pl.ds(own_heads * live_count, stat_rows), :].astype(jnp.float32)
                full = jnp.concatenate([stat, jnp.zeros((depth - stat_rows, live_count), jnp.float32)], axis=0)
                turned = jnp.transpose(full)
                pieces = [turned[:, n : n + 1] for n in range(3 * own_heads)]
                logged.append(
                    [pieces[h] + pieces[own_heads + h] + pieces[2 * own_heads + h] for h in range(own_heads)]
                )
        for h in range(own_heads):
            rows = pl.ds(h * live_count, live_count)
            held = [parcels[a * members + b][rows, :] for a in range(groups)]
            if groups > 1:
                biggest = functools.reduce(jnp.maximum, [l[h] for l in logged])
                shares = [jnp.exp(l[h] - biggest) for l in logged]
                total = functools.reduce(jnp.add, shares)
                mixed = functools.reduce(jnp.add, [w * o.astype(jnp.float32) for w, o in zip(shares, held)])
                value = (mixed / total).astype(jnp.bfloat16)
            else:
                value = held[0]
            base = lax.rem(position + b, members) * width + h * depth
            attended_ref[:, pl.ds(pl.multiple_of(base, depth), depth)] = value
    attended = attended_ref[...]
    for s in list(range(1, parts)) + [0]:
        placed = dot_f32(places_ref[s], attended).astype(jnp.bfloat16)
        if s == 0:
            own_ref[...] = placed
        else:
            project(placed, weight_ref, sends[s - 1])


def project(rows, weight_ref, out_ref):
    features = weight_ref.shape[1]
    tile = 512 if features % 512 == 0 else features
    for first in range(0, features, tile):
        columns = pl.ds(first, tile)
        out_ref[:, columns] = dot_f32(rows, weight_ref[:, columns]).astype(out_ref.dtype)


def project_kernel(rows_ref, weight_ref, out_ref):
    project(rows_ref[...], weight_ref, out_ref)


def tail_kernel(parts, mask_ref, own_ref, *refs):
    arrived = refs[: parts - 1]
    input_ref, cached_ref, gate_ref, shift_ref, scale_ref, patch_ref, block_ref, kept_ref, given_ref = refs[
        parts - 1 :
    ]
    projected = own_ref[...]
    for ref in arrived:
        projected = projected + ref[...].astype(jnp.float32)
    share = projected.shape[0]
    count = mask_ref.shape[1]
    first = lax.axis_index("tp") * share
    rows = lax.broadcasted_iota(jnp.int32, (share, count), 0) + first
    cols = lax.broadcasted_iota(jnp.int32, (share, count), 1)
    replayed = jnp.where((cols == rows) & (jnp.broadcast_to(mask_ref[...], rows.shape) == 1), 1.0, 0.0)
    replayed = jnp.sum(replayed, axis=-1, keepdims=True) > 0.5
    mixed = input_ref[...].astype(jnp.float32) + gate_ref[...] * projected
    block = jnp.where(replayed, cached_ref[...].astype(jnp.float32), mixed).astype(jnp.bfloat16)
    block_ref[...] = block
    lifted = block.astype(jnp.float32)
    centred = lifted - jnp.mean(lifted, axis=-1, keepdims=True)
    spread = jnp.mean(centred * centred, axis=-1, keepdims=True)
    normed = centred * lax.rsqrt(spread + 1e-06) * (1.0 + scale_ref[...]) + shift_ref[...]
    branch = dot_nt(patch_ref[...], normed.astype(jnp.bfloat16))
    half = branch.shape[0] // 2
    first_side = lax.axis_index("cfg") == 0
    kept_ref[...] = jnp.where(first_side, branch[:half], branch[half:])
    given_ref[...] = jnp.where(first_side, branch[half:], branch[:half])


def guide_kernel(kept_ref, partner_ref, out_ref):
    first_side = lax.axis_index("cfg") == 0
    cond = jnp.where(first_side, kept_ref[...], partner_ref[...])
    uncond = jnp.where(first_side, partner_ref[...], kept_ref[...])
    out_ref[...] = uncond + guidance_scale * (cond - uncond)


def shards(
    query_proj,
    key_proj,
    value_proj,
    query_gain,
    key_gain,
    block_input,
    cached_out,
    replay_mask,
    branch_gate,
    attn_weight,
    final_shift,
    final_scale,
    patch_weight,
):
    _, count, width = query_proj.shape
    depth = query_gain.shape[0]
    heads = width // depth
    features = attn_weight.shape[1]
    channels = patch_weight.shape[1]
    live_count = count // 2
    ring = lax.axis_size("ctx")
    parts = lax.axis_size("tp")
    share = count // parts
    members = math.gcd(heads, ring)
    groups = ring // members
    own_heads = heads // members
    own_width = own_heads * depth
    partial = groups > 1
    stat_rows = -(-3 * own_heads // 16) * 16

    def route(a, b, back):
        pairs = []
        for g in range(groups):
            for p in range(members):
                other = ((g + a) % groups) * members + (p + b) % members
                pairs.append((other, g * members + p) if back else (g * members + p, other))
        return pairs

    def call(kernel, inputs, outs, in_specs=None, out_specs=None, scratch=(), limit=24, cost=None):
        return pl.pallas_call(
            kernel,
            out_shape=outs,
            in_specs=in_specs or [VMEM] * len(inputs),
            out_specs=out_specs or [VMEM] * len(outs),
            scratch_shapes=scratch,
            compiler_params=pltpu.CompilerParams(vmem_limit_bytes=limit << 20),
            cost_estimate=cost,
        )(*inputs)

    bf16, f32 = jnp.bfloat16, jnp.float32
    shaped = jax.ShapeDtypeStruct
    pair_shape = shaped((2 * count, own_width), bf16)
    pairs = call(
        functools.partial(split_kernel, (members, own_width, depth)),
        (in_hbm(key_proj[0]), in_hbm(value_proj[0])),
        [pair_shape] * members,
        in_specs=[HBM] * 2,
        scratch=[pltpu.SemaphoreType.DMA((2, members))],
        limit=8,
    )
    pairs = [pairs[0]] + [lax.ppermute(pairs[b], "ctx", route(0, b, False)) for b in range(1, members)]
    asks = call(
        functools.partial(ask_kernel, (members, own_heads, depth, live_count)),
        (*map(in_hbm, (replay_mask, query_gain[None], query_proj[0])), pairs[0]),
        [shaped((live_count, own_width), bf16)] * members,
        in_specs=[HBM] * 3 + [VMEM],
        scratch=[
            pltpu.VMEM((1, count), jnp.int32),
            pltpu.VMEM((1, depth), f32),
            pltpu.VMEM((members, count, own_width), bf16),
            pltpu.SemaphoreType.DMA((2,)),
            pltpu.SemaphoreType.DMA((members,)),
        ],
        limit=16,
    )
    far_asks = [lax.ppermute(asks[b], "ctx", route(a, b, False)) for a in range(1, groups) for b in range(members)]
    near_asks = [asks[0]] + [lax.ppermute(asks[b], "ctx", route(0, b, False)) for b in range(1, members)]

    wanted = (
        replay_mask,
        key_gain[None],
        attn_weight,
        block_input[0],
        cached_out[0],
        branch_gate,
        final_shift,
        final_scale,
        patch_weight.T,
    )
    fetched = call(
        functools.partial(fetch_kernel, (len(wanted), live_count, parts)),
        (*map(in_hbm, wanted), asks[0]),
        [shaped(w.shape, w.dtype) for w in wanted] + [shaped((parts, share, live_count), bf16)],
        in_specs=[HBM] * len(wanted) + [VMEM],
        scratch=[pltpu.SemaphoreType.DMA((len(wanted),))],
        limit=16,
        cost=pl.CostEstimate(flops=0, transcendentals=0, bytes_accessed=2 * sum(w.size * w.dtype.itemsize for w in wanted)),
    )
    mask, key_gain_here, weight, inputs_here, cached_here, gate, shift, scale, patch, places = fetched

    parcel_rows = own_heads * live_count + (stat_rows if partial else 0)
    parcel_shape = shaped((parcel_rows, depth), bf16)

    (units,) = call(
        functools.partial(unit_kernel, depth),
        (key_gain_here, *pairs),
        [shaped((members * count, own_width), bf16)],
        cost=pl.CostEstimate(flops=0, transcendentals=0, bytes_accessed=1 << 20),
    )

    def attend(after, asks):
        scores = len(asks) * live_count * members * count * own_heads
        return call(
            functools.partial(
                attend_kernel,
                (members, partial, own_heads, depth, live_count, count, stat_rows, len(asks)),
            ),
            (after, *pairs, units, *asks),
            [parcel_shape] * len(asks),
            scratch=[pltpu.VMEM((len(asks), live_count, live_count), f32)],
            cost=pl.CostEstimate(flops=4 * scores * depth, transcendentals=scores, bytes_accessed=1 << 20),
        )

    after, distant = mask, []
    pieces = 2
    for piece in range(pieces):
        low, high = (piece * len(far_asks) // pieces, (piece + 1) * len(far_asks) // pieces)
        if low == high:
            continue
        far = attend(after, far_asks[low:high])
        after = far[0]
        distant += [
            lax.ppermute(far[n - low], "ctx", route(1 + n // members, n % members, True))
            for n in range(low, high)
        ]
    near = attend(after, near_asks)
    parcels = [near[0]] + [lax.ppermute(near[b], "ctx", route(0, b, True)) for b in range(1, members)] + distant

    merged = call(
        functools.partial(merge_kernel, (members, groups, own_heads, depth, live_count, stat_rows, parts)),
        (places, weight, *parcels),
        [shaped((share, features), bf16)] * (parts - 1) + [shaped((share, width), bf16)],
        scratch=[pltpu.VMEM((live_count, width), bf16)],
    )
    arrived = [
        lax.ppermute(merged[s - 1], "tp", [(i, (i + s) % parts) for i in range(parts)]) for s in range(1, parts)
    ]
    (own,) = call(
        project_kernel,
        (merged[-1], weight),
        [shaped((share, features), f32)],
        cost=pl.CostEstimate(flops=2 * share * width * features, transcendentals=0, bytes_accessed=1 << 20),
    )

    half = channels // 2
    block_out, kept, given = call(
        functools.partial(tail_kernel, parts),
        (mask, own, *arrived, inputs_here, cached_here, gate, shift, scale, patch),
        [shaped((share, features), bf16), shaped((half, share), f32), shaped((half, share), f32)],
    )
    partner = lax.ppermute(given, "cfg", [(0, 1), (1, 0)])
    (velocity,) = call(guide_kernel, (kept, partner), [shaped((half, share), f32)], limit=4)
    return (block_out[None], velocity.T)


def solution(mesh):
    in_specs = (
        P("cfg", "ctx", "tp"),
        P("cfg", "ctx", "tp"),
        P("cfg", "ctx", "tp"),
        P(),
        P(),
        P("cfg", ("ctx", "tp"), None),
        P("cfg", ("ctx", "tp"), None),
        P("cfg", "ctx"),
        P("cfg", None),
        P("tp", None),
        P("cfg", None),
        P("cfg", None),
        P(),
    )
    out_specs = (P("cfg", ("ctx", "tp"), None), P(("ctx", "tp"), "cfg"))
    return jax.shard_map(shards, mesh=mesh, in_specs=in_specs, out_specs=out_specs, check_vma=False)
```

profile of v0, /device:TPU:0, one launch (start us, length us, event | category | flops | bytes accessed | tf_op | source)
XLA Modules:
  0.0 79.4 jit_solution(14695273654657826181)
XLA Ops:
  0.6 1.6 %shard_map.140 = (bf16[512,384]{1,0:T(8,128)(2,1)S(1)}, bf16[512,384]{1,0:T(8,128)(2,1)S(1)}, bf16[512,384]{1,0:T(8,128)(2,1)S(1)}, bf16[512,384]{1,0:T(8,128)(2,1)S(1)}) custom-call(bf16[256,1536]{1,0:T(8,128)(2,1)} %bitcast.12, bf16[256,1536]{1,0:T(8,128)(2,1)} %bitcast.13), custom_call_target="tpu_custom_call" | custom-call | tf_op jit(solution)/shard_map/pallas_call | solution.py:318
  2.2 3.0 %collective-permute-start = (bf16[512,384]{1,0:T(8,128)(2,1)S(1)}, bf16[512,384]{1,0:T(8,128)(2,1)S(1)}, u32[]{:S(2)}, u32[]{:S(2)}) collective-permute-start(bf16[512,384]{1,0:T(8,128)(2,1)S(1)} %get-tuple-element.38), channel_id=1, source_target_pairs={{0,2},{2,4},{4,6},{6,0},{8,10},{10,12},{12,14},{14,8},{1,3},{3,5},... | collective-permute-start | bytes 1179656 | tf_op jit(solution)/shard_map/ppermute | solution.py:339
  5.2 1.6 %collective-permute-start.1 = (bf16[512,384]{1,0:T(8,128)(2,1)S(1)}, bf16[512,384]{1,0:T(8,128)(2,1)S(1)}, u32[]{:S(2)}, u32[]{:S(2)}) collective-permute-start(bf16[512,384]{1,0:T(8,128)(2,1)S(1)} %get-tuple-element.39), channel_id=1, source_target_pairs={{0,4},{2,6},{4,0},{6,2},{8,12},{10,14},{12,8},{14,10},{1,5},{3,7},... | collective-permute-start | bytes 1179656 | tf_op jit(solution)/shard_map/ppermute | solution.py:339
  6.8 1.4 %collective-permute-start.2 = (bf16[512,384]{1,0:T(8,128)(2,1)S(1)}, bf16[512,384]{1,0:T(8,128)(2,1)S(1)}, u32[]{:S(2)}, u32[]{:S(2)}) collective-permute-start(bf16[512,384]{1,0:T(8,128)(2,1)S(1)} %get-tuple-element.40), channel_id=1, source_target_pairs={{0,6},{2,0},{4,2},{6,4},{8,14},{10,8},{12,10},{14,12},{1,7},{3,1},... | collective-permute-start | bytes 1179656 | tf_op jit(solution)/shard_map/ppermute | solution.py:339
  8.2 2.1 %shard_map.141 = (bf16[128,384]{1,0:T(8,128)(2,1)S(1)}, bf16[128,384]{1,0:T(8,128)(2,1)S(1)}, bf16[128,384]{1,0:T(8,128)(2,1)S(1)}, bf16[128,384]{1,0:T(8,128)(2,1)S(1)}) custom-call(s32[1,256]{1,0:T(1,128)} %refs_0_.1, f32[1,128]{1,0:T(1,128)} %bitcast.17, bf16[256,1536]{1,0:T(8,128)(2,1)} %bitcast.14, bf16[512,384]{1,0:T(8,128)(2,1)S(1)} %get-tuple-element.33.refs_0_.refs_1_), custom_call_target="tpu_custom_call" | custom-call | tf_op jit(solution)/shard_map/pallas_call | solution.py:318
  10.4 2.7 %collective-permute-start.4 = (bf16[128,384]{1,0:T(8,128)(2,1)S(1)}, bf16[128,384]{1,0:T(8,128)(2,1)S(1)}, u32[]{:S(2)}, u32[]{:S(2)}) collective-permute-start(bf16[128,384]{1,0:T(8,128)(2,1)S(1)} %get-tuple-element.42), channel_id=1, source_target_pairs={{0,10},{2,12},{4,14},{6,8},{8,2},{10,4},{12,6},{14,0},{1,11},{3,13... | collective-permute-start | bytes 294920 | tf_op jit(solution)/shard_map/ppermute | solution.py:354
  13.1 0.3 collective-permute-start.3
  13.4 16.2 %collective-permute-done.4.refs_7_ = bf16[128,384]{1,0:T(8,128)(2,1)S(1)} collective-permute-done((bf16[128,384]{1,0:T(8,128)(2,1)S(1)}, bf16[128,384]{1,0:T(8,128)(2,1)S(1)}, u32[]{:S(2)}, u32[]{:S(2)}) %collective-permute-start.4) | collective-permute-done | bytes 98336 | tf_op jit(solution)/shard_map/ppermute | solution.py:354
  29.6 2.5 %collective-permute-start.5 = (bf16[128,384]{1,0:T(8,128)(2,1)S(1)}, bf16[128,384]{1,0:T(8,128)(2,1)S(1)}, u32[]{:S(2)}, u32[]{:S(2)}) collective-permute-start(bf16[128,384]{1,0:T(8,128)(2,1)S(1)} %get-tuple-element.44), channel_id=1, source_target_pairs={{0,12},{2,14},{4,8},{6,10},{8,4},{10,6},{12,0},{14,2},{1,13},{3,15... | collective-permute-start | bytes 294920 | tf_op jit(solution)/shard_map/ppermute | solution.py:354
  32.1 0.0 collective-permute-done.3.refs_6_
  32.1 0.0 collective-permute-start.6
  32.1 0.0 collective-permute-done.refs_1_.refs_2_
  32.1 0.3 collective-permute-start.7
  32.4 0.0 collective-permute-done.1.refs_2_.refs_3_
  32.4 3.1 %collective-permute-start.8 = (bf16[128,384]{1,0:T(8,128)(2,1)S(1)}, bf16[128,384]{1,0:T(8,128)(2,1)S(1)}, u32[]{:S(2)}, u32[]{:S(2)}) collective-permute-start(bf16[128,384]{1,0:T(8,128)(2,1)S(1)} %get-tuple-element.44), channel_id=1, source_target_pairs={{0,4},{2,6},{4,0},{6,2},{8,12},{10,14},{12,8},{14,10},{1,5},{3,7},... | collective-permute-start | bytes 294920 | tf_op jit(solution)/shard_map/ppermute | solution.py:355
  35.5 0.0 collective-permute-done.2.refs_3_.refs_4_
  35.5 1.3 %collective-permute-start.9 = (bf16[128,384]{1,0:T(8,128)(2,1)S(1)}, bf16[128,384]{1,0:T(8,128)(2,1)S(1)}, u32[]{:S(2)}, u32[]{:S(2)}) collective-permute-start(bf16[128,384]{1,0:T(8,128)(2,1)S(1)} %get-tuple-element.45), channel_id=1, source_target_pairs={{0,6},{2,0},{4,2},{6,4},{8,14},{10,8},{12,10},{14,12},{1,7},{3,1},... | collective-permute-start | bytes 294920 | tf_op jit(solution)/shard_map/ppermute | solution.py:355
  36.8 4.3 %shard_map.142 = (s32[1,256]{1,0:T(1,128)S(1)}, f32[1,128]{1,0:T(1,128)S(1)}, bf16[1536,3072]{1,0:T(8,128)(2,1)S(1)}, bf16[128,3072]{1,0:T(8,128)(2,1)S(1)}, bf1...) custom-call(s32[1,256]{1,0:T(1,128)} %refs_0_.1, ...), custom_call_target="tpu_custom_call" | custom-call | bytes 22883328 | tf_op jit(solution)/shard_map/pallas_call | solution.py:318
  41.1 0.5 shard_map.143.refs_5_
  41.6 2.0 %shard_map.144 = (bf16[400,128]{1,0:T(8,128)(2,1)S(1)}, bf16[400,128]{1,0:T(8,128)(2,1)S(1)}) custom-call(s32[1,256]{1,0:T(1,128)S(1)} %get-tuple-element.35.refs_0_.mask_ref, bf16[512,384]{1,0:T(8,128)(2,1)S(1)} %get-tuple-element.33.refs_0_.refs_1_, bf16[512,384]{1,0:T(8,128)(2,1)S(1)} %collective-permute-done.refs_1_.refs_2_, ...), custom_call_target="tpu_custom_call" | custom-call | flops 402653184 | bytes 1048576 | tf_op jit(solution)/shard_map/pallas_call | solution.py:318
  43.6 0.0 collective-permute-done.5.refs_6_
  43.7 2.1 %shard_map.145 = (bf16[400,128]{1,0:T(8,128)(2,1)S(1)}, bf16[400,128]{1,0:T(8,128)(2,1)S(1)}) custom-call(bf16[400,128]{1,0:T(8,128)(2,1)S(1)} %get-tuple-element.43.refs_0_, bf16[512,384]{1,0:T(8,128)(2,1)S(1)} %get-tuple-element.33.refs_0_.refs_1_, bf16[512,384]{1,0:T(8,128)(2,1)S(1)} %collective-permute-done.refs_1_.refs_2_, ...), custom_call_target="tpu_custom_call" | custom-call | flops 402653184 | bytes 1048576 | tf_op jit(solution)/shard_map/pallas_call | solution.py:318
  45.7 0.0 collective-permute-done.7.refs_7_
  45.7 0.0 collective-permute-done.8.refs_8_
  45.7 0.0 collective-permute-done.9.refs_9_
  45.8 3.7 %shard_map.146 = (bf16[400,128]{1,0:T(8,128)(2,1)S(1)}, bf16[400,128]{1,0:T(8,128)(2,1)S(1)}, bf16[400,128]{1,0:T(8,128)(2,1)S(1)}, bf16[400,128]{1,0:T(8,128)(2,1)S(1)}) custom-call(bf16[400,128]{1,0:T(8,128)(2,1)S(1)} %get-tuple-element.46.refs_0_, bf16[512,384]{1,0:T(8,128)(2,1)S(1)} %get-tuple-element.33.refs_0_.refs_1_, ...), custom_call_target="tpu_custom_call" | custom-call | flops 805306368 | bytes 1048576 | tf_op jit(solution)/shard_map/pallas_call | solution.py:318
  49.4 0.2 collective-permute-start.10
  49.7 2.0 %collective-permute-start.11 = (bf16[400,128]{1,0:T(8,128)(2,1)S(1)}, bf16[400,128]{1,0:T(8,128)(2,1)S(1)}, u32[]{:S(2)}, u32[]{:S(2)}) collective-permute-start(bf16[400,128]{1,0:T(8,128)(2,1)S(1)} %get-tuple-element.49), channel_id=1, source_target_pairs={{4,0},{6,2},{0,4},{2,6},{12,8},{14,10},{8,12},{10,14},{5,1},{7,3},... | collective-permute-start | bytes 307208 | tf_op jit(solution)/shard_map/ppermute | solution.py:415
  51.6 2.5 %collective-permute-start.15 = (bf16[400,128]{1,0:T(8,128)(2,1)S(1)}, bf16[400,128]{1,0:T(8,128)(2,1)S(1)}, u32[]{:S(2)}, u32[]{:S(2)}) collective-permute-start(bf16[400,128]{1,0:T(8,128)(2,1)S(1)} %get-tuple-element.46.refs_0_), channel_id=1, source_target_pairs={{12,0},{14,2},{8,4},{10,6},{4,8},{6,10},{0,12},{2,14},{13,1},{15,3... | collective-permute-start | bytes 307208 | tf_op jit(solution)/shard_map/ppermute | solution.py:411
  54.1 0.1 collective-permute-start.12
  54.2 2.7 %collective-permute-start.16 = (bf16[400,128]{1,0:T(8,128)(2,1)S(1)}, bf16[400,128]{1,0:T(8,128)(2,1)S(1)}, u32[]{:S(2)}, u32[]{:S(2)}) collective-permute-start(bf16[400,128]{1,0:T(8,128)(2,1)S(1)} %get-tuple-element.52), channel_id=1, source_target_pairs={{14,0},{8,2},{10,4},{12,6},{6,8},{0,10},{2,12},{4,14},{15,1},{9,3}... | collective-permute-start | bytes 307208 | tf_op jit(solution)/shard_map/ppermute | solution.py:411
  56.9 0.0 collective-permute-done.10.refs_1_
  56.9 2.0 %collective-permute-start.14 = (bf16[400,128]{1,0:T(8,128)(2,1)S(1)}, bf16[400,128]{1,0:T(8,128)(2,1)S(1)}, u32[]{:S(2)}, u32[]{:S(2)}) collective-permute-start(bf16[400,128]{1,0:T(8,128)(2,1)S(1)} %get-tuple-element.51), channel_id=1, source_target_pairs={{10,0},{12,2},{14,4},{8,6},{2,8},{4,10},{6,12},{0,14},{11,1},{13,3... | collective-permute-start | bytes 307208 | tf_op jit(solution)/shard_map/ppermute | solution.py:411
  58.9 0.0 collective-permute-done.11.refs_2_
  58.9 0.0 collective-permute-start.13
  58.9 1.5 %collective-permute-done.12.refs_3_ = bf16[400,128]{1,0:T(8,128)(2,1)S(1)} collective-permute-done((bf16[400,128]{1,0:T(8,128)(2,1)S(1)}, bf16[400,128]{1,0:T(8,128)(2,1)S(1)}, u32[]{:S(2)}, u32[]{:S(2)}) %collective-permute-start.12) | collective-permute-done | bytes 102432 | tf_op jit(solution)/shard_map/ppermute | solution.py:415
  60.4 2.1 %collective-permute-done.16.refs_7_ = bf16[400,128]{1,0:T(8,128)(2,1)S(1)} collective-permute-done((bf16[400,128]{1,0:T(8,128)(2,1)S(1)}, bf16[400,128]{1,0:T(8,128)(2,1)S(1)}, u32[]{:S(2)}, u32[]{:S(2)}) %collective-permute-start.16) | collective-permute-done | bytes 102432 | tf_op jit(solution)/shard_map/ppermute | solution.py:411
  62.5 0.0 collective-permute-done.15.refs_6_
  62.5 5.8 %collective-permute-done.14.refs_5_ = bf16[400,128]{1,0:T(8,128)(2,1)S(1)} collective-permute-done((bf16[400,128]{1,0:T(8,128)(2,1)S(1)}, bf16[400,128]{1,0:T(8,128)(2,1)S(1)}, u32[]{:S(2)}, u32[]{:S(2)}) %collective-permute-start.14) | collective-permute-done | bytes 102432 | tf_op jit(solution)/shard_map/ppermute | solution.py:411
  68.3 0.0 collective-permute-done.13.refs_4_
  68.4 2.7 %shard_map.147 = (bf16[128,3072]{1,0:T(8,128)(2,1)S(1)}, bf16[128,1536]{1,0:T(8,128)(2,1)S(1)}) custom-call(bf16[2,128,128]{2,1,0:T(8,128)(2,1)S(1)} %get-tuple-element.36.places_ref, bf16[1536,3072]{1,0:T(8,128)(2,1)S(1)} %get-tuple-element.37.weight_ref, bf16[400,128]{1,0:T(8,128)(2,1)S(1)} %get-tuple-element.47.refs_0_, ...), custom_call_target="tpu_custom_call" | custom-call | tf_op jit(solution)/shard_map/pallas_call | solution.py:318
  71.1 0.1 collective-permute-start.17
  71.2 1.4 %shard_map.148.own_ref = f32[128,3072]{1,0:T(8,128)S(1)} custom-call(bf16[128,1536]{1,0:T(8,128)(2,1)S(1)} %get-tuple-element.53.rows_ref, bf16[1536,3072]{1,0:T(8,128)(2,1)S(1)} %get-tuple-element.37.weight_ref), custom_call_target="tpu_custom_call" | custom-call | flops 1207959552 | bytes 1048576 | tf_op jit(solution)/shard_map/pallas_call | solution.py:318
  72.6 0.9 %collective-permute-done.17.refs_0_ = bf16[128,3072]{1,0:T(8,128)(2,1)S(1)} collective-permute-done((bf16[128,3072]{1,0:T(8,128)(2,1)S(1)}, bf16[128,3072]{1,0:T(8,128)(2,1)S(1)}, u32[]{:S(2)}, u32[]{:S(2)}) %collective-permute-start.17) | collective-permute-done | bytes 786464 | tf_op jit(solution)/shard_map/ppermute | solution.py:424
  73.4 1.6 %shard_map.149 = (bf16[128,3072]{1,0:T(8,128)(2,1)}, f32[32,128]{1,0:T(8,128)S(1)}, f32[32,128]{1,0:T(8,128)S(1)}) custom-call(s32[1,256]{1,0:T(1,128)S(1)} %get-tuple-element.35.refs_0_.mask_ref, f32[128,3072]{1,0:T(8,128)S(1)} %shard_map.148.own_ref, bf16[128,3072]{1,0:T(8,128)(2,1)S(1)} %collective-permute-done.17.refs_0_, ...), custom_call_target="tpu_custom_call" | custom-call | tf_op jit(solution)/shard_map/pallas_call | solution.py:318
  75.0 1.5 %collective-permute-start.18 = (f32[32,128]{1,0:T(8,128)S(1)}, f32[32,128]{1,0:T(8,128)S(1)}, u32[]{:S(2)}, u32[]{:S(2)}) collective-permute-start(f32[32,128]{1,0:T(8,128)S(1)} %get-tuple-element.63), channel_id=1, source_target_pairs={{0,16},{16,0},{1,17},{17,1},{2,18},{18,2},{3,19},{19,3},{4,20},{20... | collective-permute-start | bytes 49160 | tf_op jit(solution)/shard_map/ppermute | solution.py:439
  76.5 2.2 %collective-permute-done.18.partner_ref = f32[32,128]{1,0:T(8,128)S(1)} collective-permute-done((f32[32,128]{1,0:T(8,128)S(1)}, f32[32,128]{1,0:T(8,128)S(1)}, u32[]{:S(2)}, u32[]{:S(2)}) %collective-permute-start.18) | collective-permute-done | bytes 16416 | tf_op jit(solution)/shard_map/ppermute | solution.py:439
  78.8 0.6 shard_map.150
  (1 shorter events, 0.0 us)
Async XLA Ops:
  2.2 29.9 %collective-permute-start = (bf16[512,384]{1,0:T(8,128)(2,1)S(1)}, bf16[512,384]{1,0:T(8,128)(2,1)S(1)}, u32[]{:S(2)}, u32[]{:S(2)}) collective-permute-start(bf16[512,384]{1,0:T(8,128)(2,1)S(1)} %get-tuple-element.38), channel_id=1, source_target_pairs={{0,2},{2,4},{4,6},{6,0},{8,10},{10,12},{12,14},{14,8},{1,3},{3,5},... | collective-permute-start | bytes 1179656 | tf_op jit(solution)/shard_map/ppermute | solution.py:339
  5.2 27.2 %collective-permute-start.1 = (bf16[512,384]{1,0:T(8,128)(2,1)S(1)}, bf16[512,384]{1,0:T(8,128)(2,1)S(1)}, u32[]{:S(2)}, u32[]{:S(2)}) collective-permute-start(bf16[512,384]{1,0:T(8,128)(2,1)S(1)} %get-tuple-element.39), channel_id=1, source_target_pairs={{0,4},{2,6},{4,0},{6,2},{8,12},{10,14},{12,8},{14,10},{1,5},{3,7},... | collective-permute-start | bytes 1179656 | tf_op jit(solution)/shard_map/ppermute | solution.py:339
  6.8 28.7 %collective-permute-start.2 = (bf16[512,384]{1,0:T(8,128)(2,1)S(1)}, bf16[512,384]{1,0:T(8,128)(2,1)S(1)}, u32[]{:S(2)}, u32[]{:S(2)}) collective-permute-start(bf16[512,384]{1,0:T(8,128)(2,1)S(1)} %get-tuple-element.40), channel_id=1, source_target_pairs={{0,6},{2,0},{4,2},{6,4},{8,14},{10,8},{12,10},{14,12},{1,7},{3,1},... | collective-permute-start | bytes 1179656 | tf_op jit(solution)/shard_map/ppermute | solution.py:339
  10.4 19.3 %collective-permute-start.4 = (bf16[128,384]{1,0:T(8,128)(2,1)S(1)}, bf16[128,384]{1,0:T(8,128)(2,1)S(1)}, u32[]{:S(2)}, u32[]{:S(2)}) collective-permute-start(bf16[128,384]{1,0:T(8,128)(2,1)S(1)} %get-tuple-element.42), channel_id=1, source_target_pairs={{0,10},{2,12},{4,14},{6,8},{8,2},{10,4},{12,6},{14,0},{1,11},{3,13... | collective-permute-start | bytes 294920 | tf_op jit(solution)/shard_map/ppermute | solution.py:354
  13.1 19.0 %collective-permute-start.3 = (bf16[128,384]{1,0:T(8,128)(2,1)S(1)}, bf16[128,384]{1,0:T(8,128)(2,1)S(1)}, u32[]{:S(2)}, u32[]{:S(2)}) collective-permute-start(bf16[128,384]{1,0:T(8,128)(2,1)S(1)} %get-tuple-element.34.refs_9_.refs_6_), channel_id=1, source_target_pairs={{0,8},{2,10},{4,12},{6,14},{8,0},{10,2},{12,4},{14,6},{1,9},{3,11}... | collective-permute-start | bytes 294920 | tf_op jit(solution)/shard_map/ppermute | solution.py:354
  29.6 14.0 %collective-permute-start.5 = (bf16[128,384]{1,0:T(8,128)(2,1)S(1)}, bf16[128,384]{1,0:T(8,128)(2,1)S(1)}, u32[]{:S(2)}, u32[]{:S(2)}) collective-permute-start(bf16[128,384]{1,0:T(8,128)(2,1)S(1)} %get-tuple-element.44), channel_id=1, source_target_pairs={{0,12},{2,14},{4,8},{6,10},{8,4},{10,6},{12,0},{14,2},{1,13},{3,15... | collective-permute-start | bytes 294920 | tf_op jit(solution)/shard_map/ppermute | solution.py:354
  32.1 11.5 %collective-permute-start.6 = (bf16[128,384]{1,0:T(8,128)(2,1)S(1)}, bf16[128,384]{1,0:T(8,128)(2,1)S(1)}, u32[]{:S(2)}, u32[]{:S(2)}) collective-permute-start(bf16[128,384]{1,0:T(8,128)(2,1)S(1)} %get-tuple-element.45), channel_id=1, source_target_pairs={{0,14},{2,8},{4,10},{6,12},{8,6},{10,0},{12,2},{14,4},{1,15},{3,9}... | collective-permute-start | bytes 294920 | tf_op jit(solution)/shard_map/ppermute | solution.py:354
  32.1 13.6 %collective-permute-start.7 = (bf16[128,384]{1,0:T(8,128)(2,1)S(1)}, bf16[128,384]{1,0:T(8,128)(2,1)S(1)}, u32[]{:S(2)}, u32[]{:S(2)}) collective-permute-start(bf16[128,384]{1,0:T(8,128)(2,1)S(1)} %get-tuple-element.42), channel_id=1, source_target_pairs={{0,2},{2,4},{4,6},{6,0},{8,10},{10,12},{12,14},{14,8},{1,3},{3,5},... | collective-permute-start | bytes 294920 | tf_op jit(solution)/shard_map/ppermute | solution.py:355
  32.4 13.3 %collective-permute-start.8 = (bf16[128,384]{1,0:T(8,128)(2,1)S(1)}, bf16[128,384]{1,0:T(8,128)(2,1)S(1)}, u32[]{:S(2)}, u32[]{:S(2)}) collective-permute-start(bf16[128,384]{1,0:T(8,128)(2,1)S(1)} %get-tuple-element.44), channel_id=1, source_target_pairs={{0,4},{2,6},{4,0},{6,2},{8,12},{10,14},{12,8},{14,10},{1,5},{3,7},... | collective-permute-start | bytes 294920 | tf_op jit(solution)/shard_map/ppermute | solution.py:355
  35.5 10.2 %collective-permute-start.9 = (bf16[128,384]{1,0:T(8,128)(2,1)S(1)}, bf16[128,384]{1,0:T(8,128)(2,1)S(1)}, u32[]{:S(2)}, u32[]{:S(2)}) collective-permute-start(bf16[128,384]{1,0:T(8,128)(2,1)S(1)} %get-tuple-element.45), channel_id=1, source_target_pairs={{0,6},{2,0},{4,2},{6,4},{8,14},{10,8},{12,10},{14,12},{1,7},{3,1},... | collective-permute-start | bytes 294920 | tf_op jit(solution)/shard_map/ppermute | solution.py:355
  49.4 7.5 %collective-permute-start.10 = (bf16[400,128]{1,0:T(8,128)(2,1)S(1)}, bf16[400,128]{1,0:T(8,128)(2,1)S(1)}, u32[]{:S(2)}, u32[]{:S(2)}) collective-permute-start(bf16[400,128]{1,0:T(8,128)(2,1)S(1)} %get-tuple-element.48), channel_id=1, source_target_pairs={{2,0},{4,2},{6,4},{0,6},{10,8},{12,10},{14,12},{8,14},{3,1},{5,3},... | collective-permute-start | bytes 307208 | tf_op jit(solution)/shard_map/ppermute | solution.py:415
  49.7 9.2 %collective-permute-start.11 = (bf16[400,128]{1,0:T(8,128)(2,1)S(1)}, bf16[400,128]{1,0:T(8,128)(2,1)S(1)}, u32[]{:S(2)}, u32[]{:S(2)}) collective-permute-start(bf16[400,128]{1,0:T(8,128)(2,1)S(1)} %get-tuple-element.49), channel_id=1, source_target_pairs={{4,0},{6,2},{0,4},{2,6},{12,8},{14,10},{8,12},{10,14},{5,1},{7,3},... | collective-permute-start | bytes 307208 | tf_op jit(solution)/shard_map/ppermute | solution.py:415
  51.6 10.8 %collective-permute-start.15 = (bf16[400,128]{1,0:T(8,128)(2,1)S(1)}, bf16[400,128]{1,0:T(8,128)(2,1)S(1)}, u32[]{:S(2)}, u32[]{:S(2)}) collective-permute-start(bf16[400,128]{1,0:T(8,128)(2,1)S(1)} %get-tuple-element.46.refs_0_), channel_id=1, source_target_pairs={{12,0},{14,2},{8,4},{10,6},{4,8},{6,10},{0,12},{2,14},{13,1},{15,3... | collective-permute-start | bytes 307208 | tf_op jit(solution)/shard_map/ppermute | solution.py:411
  54.1 6.3 %collective-permute-start.12 = (bf16[400,128]{1,0:T(8,128)(2,1)S(1)}, bf16[400,128]{1,0:T(8,128)(2,1)S(1)}, u32[]{:S(2)}, u32[]{:S(2)}) collective-permute-start(bf16[400,128]{1,0:T(8,128)(2,1)S(1)} %get-tuple-element.50), channel_id=1, source_target_pairs={{6,0},{0,2},{2,4},{4,6},{14,8},{8,10},{10,12},{12,14},{7,1},{1,3},... | collective-permute-start | bytes 307208 | tf_op jit(solution)/shard_map/ppermute | solution.py:415
  54.2 8.3 %collective-permute-start.16 = (bf16[400,128]{1,0:T(8,128)(2,1)S(1)}, bf16[400,128]{1,0:T(8,128)(2,1)S(1)}, u32[]{:S(2)}, u32[]{:S(2)}) collective-permute-start(bf16[400,128]{1,0:T(8,128)(2,1)S(1)} %get-tuple-element.52), channel_id=1, source_target_pairs={{14,0},{8,2},{10,4},{12,6},{6,8},{0,10},{2,12},{4,14},{15,1},{9,3}... | collective-permute-start | bytes 307208 | tf_op jit(solution)/shard_map/ppermute | solution.py:411
  56.9 11.4 %collective-permute-start.14 = (bf16[400,128]{1,0:T(8,128)(2,1)S(1)}, bf16[400,128]{1,0:T(8,128)(2,1)S(1)}, u32[]{:S(2)}, u32[]{:S(2)}) collective-permute-start(bf16[400,128]{1,0:T(8,128)(2,1)S(1)} %get-tuple-element.51), channel_id=1, source_target_pairs={{10,0},{12,2},{14,4},{8,6},{2,8},{4,10},{6,12},{0,14},{11,1},{13,3... | collective-permute-start | bytes 307208 | tf_op jit(solution)/shard_map/ppermute | solution.py:411
  58.9 9.4 %collective-permute-start.13 = (bf16[400,128]{1,0:T(8,128)(2,1)S(1)}, bf16[400,128]{1,0:T(8,128)(2,1)S(1)}, u32[]{:S(2)}, u32[]{:S(2)}) collective-permute-start(bf16[400,128]{1,0:T(8,128)(2,1)S(1)} %get-tuple-element.43.refs_0_), channel_id=1, source_target_pairs={{8,0},{10,2},{12,4},{14,6},{0,8},{2,10},{4,12},{6,14},{9,1},{11,3}... | collective-permute-start | bytes 307208 | tf_op jit(solution)/shard_map/ppermute | solution.py:411
  71.1 2.4 %collective-permute-start.17 = (bf16[128,3072]{1,0:T(8,128)(2,1)S(1)}, bf16[128,3072]{1,0:T(8,128)(2,1)S(1)}, u32[]{:S(2)}, u32[]{:S(2)}) collective-permute-start(bf16[128,3072]{1,0:T(8,128)(2,1)S(1)} %get-tuple-element.54), channel_id=1, source_target_pairs={{0,1},{1,0},{2,3},{3,2},{4,5},{5,4},{6,7},{7,6},{8,9},{9,8},{10,11... | collective-permute-start | bytes 2359304 | tf_op jit(solution)/shard_map/ppermute | solution.py:424
  75.0 3.7 %collective-permute-start.18 = (f32[32,128]{1,0:T(8,128)S(1)}, f32[32,128]{1,0:T(8,128)S(1)}, u32[]{:S(2)}, u32[]{:S(2)}) collective-permute-start(f32[32,128]{1,0:T(8,128)S(1)} %get-tuple-element.63), channel_id=1, source_target_pairs={{0,16},{16,0},{1,17},{17,1},{2,18},{18,2},{3,19},{19,3},{4,20},{20... | collective-permute-start | bytes 49160 | tf_op jit(solution)/shard_map/ppermute | solution.py:439
where the time goes:
time: 79.5 us; the launch traced here: 79.4 us
  waiting for transfers between devices  28.8 us (36%)
  starting transfers between devices  27.3 us (34%)
  Pallas kernels  22.6 us (28%)
    pallas_call x11, Pallas kernels, call(): pl.pallas_call(kernel, out_shape=outs, in_specs=in_specs or [VMEM] * len(...  22.6 us
    ppermute x4, waiting for transfers between devices, shards(): lax.ppermute(asks[b], 'ctx', route(a, b, False))  16.2 us
    ppermute x4, waiting for transfers between devices, shards(): lax.ppermute(far[n - low], 'ctx', route(1 + n // members, n % members, Tr...  7.97 us
    ppermute x4, starting transfers between devices, shards(): lax.ppermute(far[n - low], 'ctx', route(1 + n // members, n % members, Tr...  7.2 us
    ppermute x3, starting transfers between devices, shards(): lax.ppermute(pairs[b], 'ctx', route(0, b, False))  6.03 us
    ppermute x4, starting transfers between devices, shards(): lax.ppermute(asks[b], 'ctx', route(a, b, False))  5.51 us
    ppermute x3, starting transfers between devices, shards(): lax.ppermute(asks[b], 'ctx', route(0, b, False))  4.67 us
    ppermute x3, starting transfers between devices, shards(): lax.ppermute(near[b], 'ctx', route(0, b, True))  2.29 us
  transfers between devices with their start and end apart: 19, of which 6 were waited for; matrix products, arithmetic and copies ran while one was open for 0% of the time, Pallas kernels for 16%

commit v1 on v0

--- a/solution.py
+++ b/solution.py
@@ -150,36 +150,29 @@
     lanes = lax.broadcasted_iota(jnp.int32, (live_count, stats.shape[2]), 1)
     if partial:
         stats[...] = jnp.zeros_like(stats)
-    batch = 2 if sources % 2 == 0 else 1
-
-    def one_head(h, carry):
-        columns = pl.ds(pl.multiple_of(h * depth, depth), depth)
-        keys = [units_ref[pl.ds(b * count, count), columns] for b in range(members)]
-        values = [ref[pl.ds(count, count), columns] for ref in pairs]
-        for first in range(0, sources, batch):
-            chosen = range(first, first + batch)
-            parts = [asks[s][:, columns] for s in chosen]
-            queries = jnp.concatenate(parts, axis=0) if batch > 1 else parts[0]
-            scores = [dot_nt(queries, k) for k in keys]
-            biggest = functools.reduce(jnp.maximum, scores)
-            biggest = jnp.max(biggest, axis=-1, keepdims=True)
-            weights = [jnp.exp2((s - biggest) * power) for s in scores]
-            totals = jnp.sum(functools.reduce(jnp.add, weights), axis=-1, keepdims=True)
-            summed = functools.reduce(jnp.add, [dot_f32(w.astype(jnp.bfloat16), v) for w, v in zip(weights, values)])
-            attended = (summed / totals).astype(jnp.bfloat16)
-            logged = biggest * factor + jnp.log(totals)
-            for n, s in enumerate(chosen):
-                rows = slice(n * live_count, (n + 1) * live_count)
-                outs[s][pl.ds(pl.multiple_of(h * live_count, live_count), live_count), :] = attended[rows]
-                if partial:
-                    rest = logged[rows]
-                    for piece in range(3):
-                        rounded = rest.astype(jnp.bfloat16).astype(jnp.float32)
-                        stats[s] = jnp.where(lanes == piece * own_heads + h, rounded, stats[s])
-                        rest = rest - rounded
-        return carry
-
-    lax.fori_loop(0, own_heads, one_head, 0)
+    ones = jnp.ones((count, depth), jnp.bfloat16)
+    for h in range(own_heads):
+        columns = slice(h * depth, (h + 1) * depth)
+        for s in range(sources):
+            queries = asks[s][:, columns]
+            scores = [dot_nt(queries, units_ref[pl.ds(b * count, count), columns]) for b in range(members)]
+            biggest = jnp.max(functools.reduce(jnp.maximum, scores), axis=-1, keepdims=True)
+            weights = [jnp.exp2((score - biggest) * power).astype(jnp.bfloat16) for score in scores]
+            summed = functools.reduce(
+                jnp.add,
+                [
+                    dot_f32(w, jnp.concatenate([ref[pl.ds(count, count), columns], ones], axis=1))
+                    for w, ref in zip(weights, pairs)
+                ],
+            )
+            totals = summed[:, depth : depth + 1]
+            outs[s][pl.ds(h * live_count, live_count), :] = (summed[:, :depth] / totals).astype(jnp.bfloat16)
+            if partial:
+                rest = biggest * factor + jnp.log(totals)
+                for piece in range(3):
+                    rounded = rest.astype(jnp.bfloat16).astype(jnp.float32)
+                    stats[s] = jnp.where(lanes == piece * own_heads + h, rounded, stats[s])
+                    rest = rest - rounded
     if partial:
         for s in range(sources):
             turned = jnp.transpose(stats[s])[:stat_rows]
@@ -268,6 +261,12 @@
     given_ref[...] = jnp.where(first_side, branch[half:], branch[:half])
 
 
+def store_kernel(block_ref, out_hbm, sem):
+    copy = pltpu.make_async_copy(block_ref, out_hbm, sem)
+    copy.start()
+    copy.wait()
+
+
 def guide_kernel(kept_ref, partner_ref, out_ref):
     first_side = lax.axis_index("cfg") == 0
     cond = jnp.where(first_side, kept_ref[...], partner_ref[...])
@@ -437,6 +436,14 @@
         [shaped((share, features), bf16), shaped((half, share), f32), shaped((half, share), f32)],
     )
     partner = lax.ppermute(given, "cfg", [(0, 1), (1, 0)])
+    (block_out,) = call(
+        store_kernel,
+        (block_out,),
+        [shaped((share, features), bf16)],
+        out_specs=[HBM],
+        scratch=[pltpu.SemaphoreType.DMA(())],
+        limit=4,
+    )
     (velocity,) = call(guide_kernel, (kept, partner), [shaped((half, share), f32)], limit=4)
     return (block_out[None], velocity.T)
 

time: 79.5 us -> 77.4 us (0.974)
  Pallas kernels: 22.6 us -> 21.3 us
  waiting for transfers between devices: 28.8 us -> 27.9 us
    pallas_call x11 -> x12, Pallas kernels: 22.6 us -> 21.3 us  [call(): pl.pallas_call(kernel, out_shape=outs, in_specs=in_specs or [VMEM] * len(...]
    ppermute x1, waiting for transfers between devices: 2.24 us -> 1.36 us  [shards(): partner = lax.ppermute(given, 'cfg', [(0, 1), (1, 0)])]
where the time goes in v1:
time: 77.4 us; the launch traced here: 77.2 us
  waiting for transfers between devices  27.9 us (36%)
  starting transfers between devices  27.3 us (35%)
  Pallas kernels  21.3 us (28%)
    pallas_call x12, Pallas kernels, call(): pl.pallas_call(kernel, out_shape=outs, in_specs=in_specs or [VMEM] * len(...  21.3 us
    ppermute x4, waiting for transfers between devices, shards(): lax.ppermute(asks[b], 'ctx', route(a, b, False))  16.2 us
    ppermute x4, waiting for transfers between devices, shards(): lax.ppermute(far[n - low], 'ctx', route(1 + n // members, n % members, Tr...  7.97 us
    ppermute x4, starting transfers between devices, shards(): lax.ppermute(far[n - low], 'ctx', route(1 + n // members, n % members, Tr...  7.2 us
    ppermute x3, starting transfers between devices, shards(): lax.ppermute(pairs[b], 'ctx', route(0, b, False))  6.03 us
    ppermute x4, starting transfers between devices, shards(): lax.ppermute(asks[b], 'ctx', route(a, b, False))  5.52 us
    ppermute x3, starting transfers between devices, shards(): lax.ppermute(asks[b], 'ctx', route(0, b, False))  4.67 us
    ppermute x3, starting transfers between devices, shards(): lax.ppermute(near[b], 'ctx', route(0, b, True))  2.29 us
  transfers between devices with their start and end apart: 19, of which 6 were waited for; matrix products, arithmetic and copies ran while one was open for 0% of the time, Pallas kernels for 16%

profile of v1, /device:TPU:0, one launch (start us, length us, event | category | flops | bytes accessed | tf_op | source)
XLA Modules:
  0.0 77.2 jit_solution(3724002637851754919)
XLA Ops:
  0.6 1.6 %shard_map.140 = (bf16[512,384]{1,0:T(8,128)(2,1)S(1)}, bf16[512,384]{1,0:T(8,128)(2,1)S(1)}, bf16[512,384]{1,0:T(8,128)(2,1)S(1)}, bf16[512,384]{1,0:T(8,128)(2,1)S(1)}) custom-call(bf16[256,1536]{1,0:T(8,128)(2,1)} %bitcast.12, bf16[256,1536]{1,0:T(8,128)(2,1)} %bitcast.13), custom_call_target="tpu_custom_call" | custom-call | tf_op jit(solution)/shard_map/pallas_call | solution.py:317
  2.2 3.0 %collective-permute-start = (bf16[512,384]{1,0:T(8,128)(2,1)S(1)}, bf16[512,384]{1,0:T(8,128)(2,1)S(1)}, u32[]{:S(2)}, u32[]{:S(2)}) collective-permute-start(bf16[512,384]{1,0:T(8,128)(2,1)S(1)} %get-tuple-element.38), channel_id=1, source_target_pairs={{0,2},{2,4},{4,6},{6,0},{8,10},{10,12},{12,14},{14,8},{1,3},{3,5},... | collective-permute-start | bytes 1179656 | tf_op jit(solution)/shard_map/ppermute | solution.py:338
  5.2 1.6 %collective-permute-start.1 = (bf16[512,384]{1,0:T(8,128)(2,1)S(1)}, bf16[512,384]{1,0:T(8,128)(2,1)S(1)}, u32[]{:S(2)}, u32[]{:S(2)}) collective-permute-start(bf16[512,384]{1,0:T(8,128)(2,1)S(1)} %get-tuple-element.39), channel_id=1, source_target_pairs={{0,4},{2,6},{4,0},{6,2},{8,12},{10,14},{12,8},{14,10},{1,5},{3,7},... | collective-permute-start | bytes 1179656 | tf_op jit(solution)/shard_map/ppermute | solution.py:338
  6.8 1.4 %collective-permute-start.2 = (bf16[512,384]{1,0:T(8,128)(2,1)S(1)}, bf16[512,384]{1,0:T(8,128)(2,1)S(1)}, u32[]{:S(2)}, u32[]{:S(2)}) collective-permute-start(bf16[512,384]{1,0:T(8,128)(2,1)S(1)} %get-tuple-element.40), channel_id=1, source_target_pairs={{0,6},{2,0},{4,2},{6,4},{8,14},{10,8},{12,10},{14,12},{1,7},{3,1},... | collective-permute-start | bytes 1179656 | tf_op jit(solution)/shard_map/ppermute | solution.py:338
  8.2 2.1 %shard_map.141 = (bf16[128,384]{1,0:T(8,128)(2,1)S(1)}, bf16[128,384]{1,0:T(8,128)(2,1)S(1)}, bf16[128,384]{1,0:T(8,128)(2,1)S(1)}, bf16[128,384]{1,0:T(8,128)(2,1)S(1)}) custom-call(s32[1,256]{1,0:T(1,128)} %refs_0_.1, f32[1,128]{1,0:T(1,128)} %bitcast.18, bf16[256,1536]{1,0:T(8,128)(2,1)} %bitcast.14, bf16[512,384]{1,0:T(8,128)(2,1)S(1)} %get-tuple-element.33.refs_0_.refs_1_), custom_call_target="tpu_custom_call" | custom-call | tf_op jit(solution)/shard_map/pallas_call | solution.py:317
  10.4 2.7 %collective-permute-start.4 = (bf16[128,384]{1,0:T(8,128)(2,1)S(1)}, bf16[128,384]{1,0:T(8,128)(2,1)S(1)}, u32[]{:S(2)}, u32[]{:S(2)}) collective-permute-start(bf16[128,384]{1,0:T(8,128)(2,1)S(1)} %get-tuple-element.42), channel_id=1, source_target_pairs={{0,10},{2,12},{4,14},{6,8},{8,2},{10,4},{12,6},{14,0},{1,11},{3,13... | collective-permute-start | bytes 294920 | tf_op jit(solution)/shard_map/ppermute | solution.py:353
  13.1 0.3 collective-permute-start.3
  13.4 16.2 %collective-permute-done.4.refs_7_ = bf16[128,384]{1,0:T(8,128)(2,1)S(1)} collective-permute-done((bf16[128,384]{1,0:T(8,128)(2,1)S(1)}, bf16[128,384]{1,0:T(8,128)(2,1)S(1)}, u32[]{:S(2)}, u32[]{:S(2)}) %collective-permute-start.4) | collective-permute-done | bytes 98336 | tf_op jit(solution)/shard_map/ppermute | solution.py:353
  29.6 2.5 %collective-permute-start.5 = (bf16[128,384]{1,0:T(8,128)(2,1)S(1)}, bf16[128,384]{1,0:T(8,128)(2,1)S(1)}, u32[]{:S(2)}, u32[]{:S(2)}) collective-permute-start(bf16[128,384]{1,0:T(8,128)(2,1)S(1)} %get-tuple-element.44), channel_id=1, source_target_pairs={{0,12},{2,14},{4,8},{6,10},{8,4},{10,6},{12,0},{14,2},{1,13},{3,15... | collective-permute-start | bytes 294920 | tf_op jit(solution)/shard_map/ppermute | solution.py:353
  32.1 0.0 collective-permute-done.3.refs_6_
  32.1 0.0 collective-permute-start.6
  32.1 0.0 collective-permute-done.refs_1_.refs_2_
  32.1 0.3 collective-permute-start.7
  32.4 0.0 collective-permute-done.1.refs_2_.refs_3_
  32.4 3.1 %collective-permute-start.8 = (bf16[128,384]{1,0:T(8,128)(2,1)S(1)}, bf16[128,384]{1,0:T(8,128)(2,1)S(1)}, u32[]{:S(2)}, u32[]{:S(2)}) collective-permute-start(bf16[128,384]{1,0:T(8,128)(2,1)S(1)} %get-tuple-element.44), channel_id=1, source_target_pairs={{0,4},{2,6},{4,0},{6,2},{8,12},{10,14},{12,8},{14,10},{1,5},{3,7},... | collective-permute-start | bytes 294920 | tf_op jit(solution)/shard_map/ppermute | solution.py:354
  35.5 0.0 collective-permute-done.2.refs_3_.refs_4_
  35.5 1.3 %collective-permute-start.9 = (bf16[128,384]{1,0:T(8,128)(2,1)S(1)}, bf16[128,384]{1,0:T(8,128)(2,1)S(1)}, u32[]{:S(2)}, u32[]{:S(2)}) collective-permute-start(bf16[128,384]{1,0:T(8,128)(2,1)S(1)} %get-tuple-element.45), channel_id=1, source_target_pairs={{0,6},{2,0},{4,2},{6,4},{8,14},{10,8},{12,10},{14,12},{1,7},{3,1},... | collective-permute-start | bytes 294920 | tf_op jit(solution)/shard_map/ppermute | solution.py:354
  36.8 4.3 %shard_map.142 = (s32[1,256]{1,0:T(1,128)S(1)}, f32[1,128]{1,0:T(1,128)S(1)}, bf16[1536,3072]{1,0:T(8,128)(2,1)S(1)}, bf16[128,3072]{1,0:T(8,128)(2,1)S(1)}, bf1...) custom-call(s32[1,256]{1,0:T(1,128)} %refs_0_.1, ...), custom_call_target="tpu_custom_call" | custom-call | bytes 22883328 | tf_op jit(solution)/shard_map/pallas_call | solution.py:317
  41.1 0.5 shard_map.143.refs_5_
  41.6 1.5 %shard_map.144 = (bf16[400,128]{1,0:T(8,128)(2,1)S(1)}, bf16[400,128]{1,0:T(8,128)(2,1)S(1)}) custom-call(s32[1,256]{1,0:T(1,128)S(1)} %get-tuple-element.35.refs_0_.mask_ref, bf16[512,384]{1,0:T(8,128)(2,1)S(1)} %get-tuple-element.33.refs_0_.refs_1_, bf16[512,384]{1,0:T(8,128)(2,1)S(1)} %collective-permute-done.refs_1_.refs_2_, ...), custom_call_target="tpu_custom_call" | custom-call | flops 402653184 | bytes 1048576 | tf_op jit(solution)/shard_map/pallas_call | solution.py:317
  43.1 0.0 collective-permute-done.5.refs_6_
  43.1 0.0 collective-permute-done.6.refs_7_
  43.2 1.5 %shard_map.145 = (bf16[400,128]{1,0:T(8,128)(2,1)S(1)}, bf16[400,128]{1,0:T(8,128)(2,1)S(1)}) custom-call(bf16[400,128]{1,0:T(8,128)(2,1)S(1)} %get-tuple-element.43.refs_0_, bf16[512,384]{1,0:T(8,128)(2,1)S(1)} %get-tuple-element.33.refs_0_.refs_1_, bf16[512,384]{1,0:T(8,128)(2,1)S(1)} %collective-permute-done.refs_1_.refs_2_, ...), custom_call_target="tpu_custom_call" | custom-call | flops 402653184 | bytes 1048576 | tf_op jit(solution)/shard_map/pallas_call | solution.py:317
  44.7 0.0 collective-permute-done.7.refs_7_
  44.7 0.0 collective-permute-done.8.refs_8_
  44.7 0.0 collective-permute-done.9.refs_9_
  44.7 2.7 %shard_map.146 = (bf16[400,128]{1,0:T(8,128)(2,1)S(1)}, bf16[400,128]{1,0:T(8,128)(2,1)S(1)}, bf16[400,128]{1,0:T(8,128)(2,1)S(1)}, bf16[400,128]{1,0:T(8,128)(2,1)S(1)}) custom-call(bf16[400,128]{1,0:T(8,128)(2,1)S(1)} %get-tuple-element.46.refs_0_, bf16[512,384]{1,0:T(8,128)(2,1)S(1)} %get-tuple-element.33.refs_0_.refs_1_, ...), custom_call_target="tpu_custom_call" | custom-call | flops 805306368 | bytes 1048576 | tf_op jit(solution)/shard_map/pallas_call | solution.py:317
  47.4 0.2 collective-permute-start.10
  47.6 2.0 %collective-permute-start.11 = (bf16[400,128]{1,0:T(8,128)(2,1)S(1)}, bf16[400,128]{1,0:T(8,128)(2,1)S(1)}, u32[]{:S(2)}, u32[]{:S(2)}) collective-permute-start(bf16[400,128]{1,0:T(8,128)(2,1)S(1)} %get-tuple-element.49), channel_id=1, source_target_pairs={{4,0},{6,2},{0,4},{2,6},{12,8},{14,10},{8,12},{10,14},{5,1},{7,3},... | collective-permute-start | bytes 307208 | tf_op jit(solution)/shard_map/ppermute | solution.py:414
  49.6 2.5 %collective-permute-start.15 = (bf16[400,128]{1,0:T(8,128)(2,1)S(1)}, bf16[400,128]{1,0:T(8,128)(2,1)S(1)}, u32[]{:S(2)}, u32[]{:S(2)}) collective-permute-start(bf16[400,128]{1,0:T(8,128)(2,1)S(1)} %get-tuple-element.46.refs_0_), channel_id=1, source_target_pairs={{12,0},{14,2},{8,4},{10,6},{4,8},{6,10},{0,12},{2,14},{13,1},{15,3... | collective-permute-start | bytes 307208 | tf_op jit(solution)/shard_map/ppermute | solution.py:410
  52.1 0.1 collective-permute-start.12
  52.1 2.7 %collective-permute-start.16 = (bf16[400,128]{1,0:T(8,128)(2,1)S(1)}, bf16[400,128]{1,0:T(8,128)(2,1)S(1)}, u32[]{:S(2)}, u32[]{:S(2)}) collective-permute-start(bf16[400,128]{1,0:T(8,128)(2,1)S(1)} %get-tuple-element.52), channel_id=1, source_target_pairs={{14,0},{8,2},{10,4},{12,6},{6,8},{0,10},{2,12},{4,14},{15,1},{9,3}... | collective-permute-start | bytes 307208 | tf_op jit(solution)/shard_map/ppermute | solution.py:410
  54.9 2.0 %collective-permute-start.14 = (bf16[400,128]{1,0:T(8,128)(2,1)S(1)}, bf16[400,128]{1,0:T(8,128)(2,1)S(1)}, u32[]{:S(2)}, u32[]{:S(2)}) collective-permute-start(bf16[400,128]{1,0:T(8,128)(2,1)S(1)} %get-tuple-element.51), channel_id=1, source_target_pairs={{10,0},{12,2},{14,4},{8,6},{2,8},{4,10},{6,12},{0,14},{11,1},{13,3... | collective-permute-start | bytes 307208 | tf_op jit(solution)/shard_map/ppermute | solution.py:410
  56.9 0.0 collective-permute-done.11.refs_2_
  56.9 1.5 %collective-permute-done.12.refs_3_ = bf16[400,128]{1,0:T(8,128)(2,1)S(1)} collective-permute-done((bf16[400,128]{1,0:T(8,128)(2,1)S(1)}, bf16[400,128]{1,0:T(8,128)(2,1)S(1)}, u32[]{:S(2)}, u32[]{:S(2)}) %collective-permute-start.12) | collective-permute-done | bytes 102432 | tf_op jit(solution)/shard_map/ppermute | solution.py:414
  58.3 2.1 %collective-permute-done.16.refs_7_ = bf16[400,128]{1,0:T(8,128)(2,1)S(1)} collective-permute-done((bf16[400,128]{1,0:T(8,128)(2,1)S(1)}, bf16[400,128]{1,0:T(8,128)(2,1)S(1)}, u32[]{:S(2)}, u32[]{:S(2)}) %collective-permute-start.16) | collective-permute-done | bytes 102432 | tf_op jit(solution)/shard_map/ppermute | solution.py:410
  60.4 0.0 collective-permute-done.15.refs_6_
  60.4 5.8 %collective-permute-done.14.refs_5_ = bf16[400,128]{1,0:T(8,128)(2,1)S(1)} collective-permute-done((bf16[400,128]{1,0:T(8,128)(2,1)S(1)}, bf16[400,128]{1,0:T(8,128)(2,1)S(1)}, u32[]{:S(2)}, u32[]{:S(2)}) %collective-permute-start.14) | collective-permute-done | bytes 102432 | tf_op jit(solution)/shard_map/ppermute | solution.py:410
  66.3 0.0 collective-permute-done.13.refs_4_
  66.3 2.7 %shard_map.147 = (bf16[128,3072]{1,0:T(8,128)(2,1)S(1)}, bf16[128,1536]{1,0:T(8,128)(2,1)S(1)}) custom-call(bf16[2,128,128]{2,1,0:T(8,128)(2,1)S(1)} %get-tuple-element.36.places_ref, bf16[1536,3072]{1,0:T(8,128)(2,1)S(1)} %get-tuple-element.37.weight_ref, bf16[400,128]{1,0:T(8,128)(2,1)S(1)} %get-tuple-element.47.refs_0_, ...), custom_call_target="tpu_custom_call" | custom-call | tf_op jit(solution)/shard_map/pallas_call | solution.py:317
  69.0 0.1 collective-permute-start.17
  69.1 1.4 %shard_map.148.own_ref = f32[128,3072]{1,0:T(8,128)S(1)} custom-call(bf16[128,1536]{1,0:T(8,128)(2,1)S(1)} %get-tuple-element.53.rows_ref, bf16[1536,3072]{1,0:T(8,128)(2,1)S(1)} %get-tuple-element.37.weight_ref), custom_call_target="tpu_custom_call" | custom-call | flops 1207959552 | bytes 1048576 | tf_op jit(solution)/shard_map/pallas_call | solution.py:317
  70.5 0.9 %collective-permute-done.17.refs_0_ = bf16[128,3072]{1,0:T(8,128)(2,1)S(1)} collective-permute-done((bf16[128,3072]{1,0:T(8,128)(2,1)S(1)}, bf16[128,3072]{1,0:T(8,128)(2,1)S(1)}, u32[]{:S(2)}, u32[]{:S(2)}) %collective-permute-start.17) | collective-permute-done | bytes 786464 | tf_op jit(solution)/shard_map/ppermute | solution.py:423
  71.4 1.4 %shard_map.149 = (bf16[128,3072]{1,0:T(8,128)(2,1)S(1)}, f32[32,128]{1,0:T(8,128)S(1)}, f32[32,128]{1,0:T(8,128)S(1)}) custom-call(s32[1,256]{1,0:T(1,128)S(1)} %get-tuple-element.35.refs_0_.mask_ref, f32[128,3072]{1,0:T(8,128)S(1)} %shard_map.148.own_ref, bf16[128,3072]{1,0:T(8,128)(2,1)S(1)} %collective-permute-done.17.refs_0_, ...), custom_call_target="tpu_custom_call" | custom-call | tf_op jit(solution)/shard_map/pallas_call | solution.py:317
  72.8 1.5 %collective-permute-start.18 = (f32[32,128]{1,0:T(8,128)S(1)}, f32[32,128]{1,0:T(8,128)S(1)}, u32[]{:S(2)}, u32[]{:S(2)}) collective-permute-start(f32[32,128]{1,0:T(8,128)S(1)} %get-tuple-element.63), channel_id=1, source_target_pairs={{0,16},{16,0},{1,17},{17,1},{2,18},{18,2},{3,19},{19,3},{4,20},{20... | collective-permute-start | bytes 49160 | tf_op jit(solution)/shard_map/ppermute | solution.py:438
  74.4 0.9 %shard_map.150 = bf16[128,3072]{1,0:T(8,128)(2,1)} custom-call(bf16[128,3072]{1,0:T(8,128)(2,1)S(1)} %get-tuple-element.61.block_ref), custom_call_target="tpu_custom_call" | custom-call | tf_op jit(solution)/shard_map/pallas_call | solution.py:317
  75.3 1.4 %collective-permute-done.18.partner_ref = f32[32,128]{1,0:T(8,128)S(1)} collective-permute-done((f32[32,128]{1,0:T(8,128)S(1)}, f32[32,128]{1,0:T(8,128)S(1)}, u32[]{:S(2)}, u32[]{:S(2)}) %collective-permute-start.18) | collective-permute-done | bytes 16416 | tf_op jit(solution)/shard_map/ppermute | solution.py:438
  76.6 0.6 shard_map.151
  (2 shorter events, 0.0 us)
Async XLA Ops:
  2.2 29.9 %collective-permute-start = (bf16[512,384]{1,0:T(8,128)(2,1)S(1)}, bf16[512,384]{1,0:T(8,128)(2,1)S(1)}, u32[]{:S(2)}, u32[]{:S(2)}) collective-permute-start(bf16[512,384]{1,0:T(8,128)(2,1)S(1)} %get-tuple-element.38), channel_id=1, source_target_pairs={{0,2},{2,4},{4,6},{6,0},{8,10},{10,12},{12,14},{14,8},{1,3},{3,5},... | collective-permute-start | bytes 1179656 | tf_op jit(solution)/shard_map/ppermute | solution.py:338
  5.2 27.2 %collective-permute-start.1 = (bf16[512,384]{1,0:T(8,128)(2,1)S(1)}, bf16[512,384]{1,0:T(8,128)(2,1)S(1)}, u32[]{:S(2)}, u32[]{:S(2)}) collective-permute-start(bf16[512,384]{1,0:T(8,128)(2,1)S(1)} %get-tuple-element.39), channel_id=1, source_target_pairs={{0,4},{2,6},{4,0},{6,2},{8,12},{10,14},{12,8},{14,10},{1,5},{3,7},... | collective-permute-start | bytes 1179656 | tf_op jit(solution)/shard_map/ppermute | solution.py:338
  6.8 28.7 %collective-permute-start.2 = (bf16[512,384]{1,0:T(8,128)(2,1)S(1)}, bf16[512,384]{1,0:T(8,128)(2,1)S(1)}, u32[]{:S(2)}, u32[]{:S(2)}) collective-permute-start(bf16[512,384]{1,0:T(8,128)(2,1)S(1)} %get-tuple-element.40), channel_id=1, source_target_pairs={{0,6},{2,0},{4,2},{6,4},{8,14},{10,8},{12,10},{14,12},{1,7},{3,1},... | collective-permute-start | bytes 1179656 | tf_op jit(solution)/shard_map/ppermute | solution.py:338
  10.4 19.3 %collective-permute-start.4 = (bf16[128,384]{1,0:T(8,128)(2,1)S(1)}, bf16[128,384]{1,0:T(8,128)(2,1)S(1)}, u32[]{:S(2)}, u32[]{:S(2)}) collective-permute-start(bf16[128,384]{1,0:T(8,128)(2,1)S(1)} %get-tuple-element.42), channel_id=1, source_target_pairs={{0,10},{2,12},{4,14},{6,8},{8,2},{10,4},{12,6},{14,0},{1,11},{3,13... | collective-permute-start | bytes 294920 | tf_op jit(solution)/shard_map/ppermute | solution.py:353
  13.1 19.0 %collective-permute-start.3 = (bf16[128,384]{1,0:T(8,128)(2,1)S(1)}, bf16[128,384]{1,0:T(8,128)(2,1)S(1)}, u32[]{:S(2)}, u32[]{:S(2)}) collective-permute-start(bf16[128,384]{1,0:T(8,128)(2,1)S(1)} %get-tuple-element.34.refs_9_.refs_6_), channel_id=1, source_target_pairs={{0,8},{2,10},{4,12},{6,14},{8,0},{10,2},{12,4},{14,6},{1,9},{3,11}... | collective-permute-start | bytes 294920 | tf_op jit(solution)/shard_map/ppermute | solution.py:353
  29.6 13.5 %collective-permute-start.5 = (bf16[128,384]{1,0:T(8,128)(2,1)S(1)}, bf16[128,384]{1,0:T(8,128)(2,1)S(1)}, u32[]{:S(2)}, u32[]{:S(2)}) collective-permute-start(bf16[128,384]{1,0:T(8,128)(2,1)S(1)} %get-tuple-element.44), channel_id=1, source_target_pairs={{0,12},{2,14},{4,8},{6,10},{8,4},{10,6},{12,0},{14,2},{1,13},{3,15... | collective-permute-start | bytes 294920 | tf_op jit(solution)/shard_map/ppermute | solution.py:353
  32.1 11.0 %collective-permute-start.6 = (bf16[128,384]{1,0:T(8,128)(2,1)S(1)}, bf16[128,384]{1,0:T(8,128)(2,1)S(1)}, u32[]{:S(2)}, u32[]{:S(2)}) collective-permute-start(bf16[128,384]{1,0:T(8,128)(2,1)S(1)} %get-tuple-element.45), channel_id=1, source_target_pairs={{0,14},{2,8},{4,10},{6,12},{8,6},{10,0},{12,2},{14,4},{1,15},{3,9}... | collective-permute-start | bytes 294920 | tf_op jit(solution)/shard_map/ppermute | solution.py:353
  32.1 12.6 %collective-permute-start.7 = (bf16[128,384]{1,0:T(8,128)(2,1)S(1)}, bf16[128,384]{1,0:T(8,128)(2,1)S(1)}, u32[]{:S(2)}, u32[]{:S(2)}) collective-permute-start(bf16[128,384]{1,0:T(8,128)(2,1)S(1)} %get-tuple-element.42), channel_id=1, source_target_pairs={{0,2},{2,4},{4,6},{6,0},{8,10},{10,12},{12,14},{14,8},{1,3},{3,5},... | collective-permute-start | bytes 294920 | tf_op jit(solution)/shard_map/ppermute | solution.py:354
  32.4 12.3 %collective-permute-start.8 = (bf16[128,384]{1,0:T(8,128)(2,1)S(1)}, bf16[128,384]{1,0:T(8,128)(2,1)S(1)}, u32[]{:S(2)}, u32[]{:S(2)}) collective-permute-start(bf16[128,384]{1,0:T(8,128)(2,1)S(1)} %get-tuple-element.44), channel_id=1, source_target_pairs={{0,4},{2,6},{4,0},{6,2},{8,12},{10,14},{12,8},{14,10},{1,5},{3,7},... | collective-permute-start | bytes 294920 | tf_op jit(solution)/shard_map/ppermute | solution.py:354
  35.5 9.2 %collective-permute-start.9 = (bf16[128,384]{1,0:T(8,128)(2,1)S(1)}, bf16[128,384]{1,0:T(8,128)(2,1)S(1)}, u32[]{:S(2)}, u32[]{:S(2)}) collective-permute-start(bf16[128,384]{1,0:T(8,128)(2,1)S(1)} %get-tuple-element.45), channel_id=1, source_target_pairs={{0,6},{2,0},{4,2},{6,4},{8,14},{10,8},{12,10},{14,12},{1,7},{3,1},... | collective-permute-start | bytes 294920 | tf_op jit(solution)/shard_map/ppermute | solution.py:354
  47.4 7.5 %collective-permute-start.10 = (bf16[400,128]{1,0:T(8,128)(2,1)S(1)}, bf16[400,128]{1,0:T(8,128)(2,1)S(1)}, u32[]{:S(2)}, u32[]{:S(2)}) collective-permute-start(bf16[400,128]{1,0:T(8,128)(2,1)S(1)} %get-tuple-element.48), channel_id=1, source_target_pairs={{2,0},{4,2},{6,4},{0,6},{10,8},{12,10},{14,12},{8,14},{3,1},{5,3},... | collective-permute-start | bytes 307208 | tf_op jit(solution)/shard_map/ppermute | solution.py:414
  47.6 9.2 %collective-permute-start.11 = (bf16[400,128]{1,0:T(8,128)(2,1)S(1)}, bf16[400,128]{1,0:T(8,128)(2,1)S(1)}, u32[]{:S(2)}, u32[]{:S(2)}) collective-permute-start(bf16[400,128]{1,0:T(8,128)(2,1)S(1)} %get-tuple-element.49), channel_id=1, source_target_pairs={{4,0},{6,2},{0,4},{2,6},{12,8},{14,10},{8,12},{10,14},{5,1},{7,3},... | collective-permute-start | bytes 307208 | tf_op jit(solution)/shard_map/ppermute | solution.py:414
  49.6 10.8 %collective-permute-start.15 = (bf16[400,128]{1,0:T(8,128)(2,1)S(1)}, bf16[400,128]{1,0:T(8,128)(2,1)S(1)}, u32[]{:S(2)}, u32[]{:S(2)}) collective-permute-start(bf16[400,128]{1,0:T(8,128)(2,1)S(1)} %get-tuple-element.46.refs_0_), channel_id=1, source_target_pairs={{12,0},{14,2},{8,4},{10,6},{4,8},{6,10},{0,12},{2,14},{13,1},{15,3... | collective-permute-start | bytes 307208 | tf_op jit(solution)/shard_map/ppermute | solution.py:410
  52.1 6.3 %collective-permute-start.12 = (bf16[400,128]{1,0:T(8,128)(2,1)S(1)}, bf16[400,128]{1,0:T(8,128)(2,1)S(1)}, u32[]{:S(2)}, u32[]{:S(2)}) collective-permute-start(bf16[400,128]{1,0:T(8,128)(2,1)S(1)} %get-tuple-element.50), channel_id=1, source_target_pairs={{6,0},{0,2},{2,4},{4,6},{14,8},{8,10},{10,12},{12,14},{7,1},{1,3},... | collective-permute-start | bytes 307208 | tf_op jit(solution)/shard_map/ppermute | solution.py:414
  52.1 8.3 %collective-permute-start.16 = (bf16[400,128]{1,0:T(8,128)(2,1)S(1)}, bf16[400,128]{1,0:T(8,128)(2,1)S(1)}, u32[]{:S(2)}, u32[]{:S(2)}) collective-permute-start(bf16[400,128]{1,0:T(8,128)(2,1)S(1)} %get-tuple-element.52), channel_id=1, source_target_pairs={{14,0},{8,2},{10,4},{12,6},{6,8},{0,10},{2,12},{4,14},{15,1},{9,3}... | collective-permute-start | bytes 307208 | tf_op jit(solution)/shard_map/ppermute | solution.py:410
  54.9 11.4 %collective-permute-start.14 = (bf16[400,128]{1,0:T(8,128)(2,1)S(1)}, bf16[400,128]{1,0:T(8,128)(2,1)S(1)}, u32[]{:S(2)}, u32[]{:S(2)}) collective-permute-start(bf16[400,128]{1,0:T(8,128)(2,1)S(1)} %get-tuple-element.51), channel_id=1, source_target_pairs={{10,0},{12,2},{14,4},{8,6},{2,8},{4,10},{6,12},{0,14},{11,1},{13,3... | collective-permute-start | bytes 307208 | tf_op jit(solution)/shard_map/ppermute | solution.py:410
  56.9 9.4 %collective-permute-start.13 = (bf16[400,128]{1,0:T(8,128)(2,1)S(1)}, bf16[400,128]{1,0:T(8,128)(2,1)S(1)}, u32[]{:S(2)}, u32[]{:S(2)}) collective-permute-start(bf16[400,128]{1,0:T(8,128)(2,1)S(1)} %get-tuple-element.43.refs_0_), channel_id=1, source_target_pairs={{8,0},{10,2},{12,4},{14,6},{0,8},{2,10},{4,12},{6,14},{9,1},{11,3}... | collective-permute-start | bytes 307208 | tf_op jit(solution)/shard_map/ppermute | solution.py:410
  69.0 2.4 %collective-permute-start.17 = (bf16[128,3072]{1,0:T(8,128)(2,1)S(1)}, bf16[128,3072]{1,0:T(8,128)(2,1)S(1)}, u32[]{:S(2)}, u32[]{:S(2)}) collective-permute-start(bf16[128,3072]{1,0:T(8,128)(2,1)S(1)} %get-tuple-element.54), channel_id=1, source_target_pairs={{0,1},{1,0},{2,3},{3,2},{4,5},{5,4},{6,7},{7,6},{8,9},{9,8},{10,11... | collective-permute-start | bytes 2359304 | tf_op jit(solution)/shard_map/ppermute | solution.py:423
  72.8 3.8 %collective-permute-start.18 = (f32[32,128]{1,0:T(8,128)S(1)}, f32[32,128]{1,0:T(8,128)S(1)}, u32[]{:S(2)}, u32[]{:S(2)}) collective-permute-start(f32[32,128]{1,0:T(8,128)S(1)} %get-tuple-element.63), channel_id=1, source_target_pairs={{0,16},{16,0},{1,17},{17,1},{2,18},{18,2},{3,19},{19,3},{4,20},{20... | collective-permute-start | bytes 49160 | tf_op jit(solution)/shard_map/ppermute | solution.py:438

commit v2 on v1

--- a/solution.py
+++ b/solution.py
@@ -184,40 +184,34 @@
     sources = members * groups
     parcels = refs[:sources]
     sends = refs[sources : sources + parts - 1]
-    own_ref, attended_ref = refs[sources + parts - 1 :]
+    own_ref, spread_ref = refs[sources + parts - 1 :]
+    share = own_ref.shape[0]
     width = own_heads * depth
     position = ring_place(members)
+    places = jnp.concatenate([places_ref[s] for s in range(parts)], axis=0)
     for b in range(members):
-        logged = []
+        held = [parcels[a * members + b] for a in range(groups)]
         if groups > 1:
-            for a in range(groups):
-                stat = parcels[a * members + b][pl.ds(own_heads * live_count, stat_rows), :].astype(jnp.float32)
-                full = jnp.concatenate([stat, jnp.zeros((depth - stat_rows, live_count), jnp.float32)], axis=0)
-                turned = jnp.transpose(full)
-                pieces = [turned[:, n : n + 1] for n in range(3 * own_heads)]
-                logged.append(
-                    [pieces[h] + pieces[own_heads + h] + pieces[2 * own_heads + h] for h in range(own_heads)]
-                )
+            stats = [ref[pl.ds(own_heads * live_count, stat_rows), :].astype(jnp.float32) for ref in held]
         for h in range(own_heads):
-            rows = pl.ds(h * live_count, live_count)
-            held = [parcels[a * members + b][rows, :] for a in range(groups)]
+            values = [ref[pl.ds(h * live_count, live_count), :] for ref in held]
             if groups > 1:
-                biggest = functools.reduce(jnp.maximum, [l[h] for l in logged])
-                shares = [jnp.exp(l[h] - biggest) for l in logged]
+                logged = [
+                    t[h : h + 1] + t[own_heads + h : own_heads + h + 1] + t[2 * own_heads + h : 2 * own_heads + h + 1]
+                    for t in stats
+                ]
+                biggest = functools.reduce(jnp.maximum, logged)
+                shares = [jnp.exp(l - biggest) for l in logged]
                 total = functools.reduce(jnp.add, shares)
-                mixed = functools.reduce(jnp.add, [w * o.astype(jnp.float32) for w, o in zip(shares, held)])
-                value = (mixed / total).astype(jnp.bfloat16)
+                spots = [places * (w / total).astype(jnp.bfloat16) for w in shares]
+                placed = dot_f32(jnp.concatenate(spots, axis=1), jnp.concatenate(values, axis=0))
             else:
-                value = held[0]
+                placed = dot_f32(places, values[0])
             base = lax.rem(position + b, members) * width + h * depth
-            attended_ref[:, pl.ds(pl.multiple_of(base, depth), depth)] = value
-    attended = attended_ref[...]
-    for s in list(range(1, parts)) + [0]:
-        placed = dot_f32(places_ref[s], attended).astype(jnp.bfloat16)
-        if s == 0:
-            own_ref[...] = placed
-        else:
-            project(placed, weight_ref, sends[s - 1])
+            spread_ref[:, pl.ds(pl.multiple_of(base, depth), depth)] = placed.astype(jnp.bfloat16)
+    own_ref[...] = spread_ref[pl.ds(0, share), :]
+    for s in range(1, parts):
+        project(spread_ref[pl.ds(s * share, share), :], weight_ref, sends[s - 1])
 
 
 def project(rows, weight_ref, out_ref):
@@ -417,7 +411,7 @@
         functools.partial(merge_kernel, (members, groups, own_heads, depth, live_count, stat_rows, parts)),
         (places, weight, *parcels),
         [shaped((share, features), bf16)] * (parts - 1) + [shaped((share, width), bf16)],
-        scratch=[pltpu.VMEM((live_count, width), bf16)],
+        scratch=[pltpu.VMEM((count, width), bf16)],
     )
     arrived = [
         lax.ppermute(merged[s - 1], "tp", [(i, (i + s) % parts) for i in range(parts)]) for s in range(1, parts)

time: 77.4 us -> 76.6 us (0.990)
  Pallas kernels: 21.3 us -> 20.5 us
    pallas_call x12, Pallas kernels: 21.3 us -> 20.5 us  [call(): pl.pallas_call(kernel, out_shape=outs, in_specs=in_specs or [VMEM] * len(...]
where the time goes in v2:
time: 76.6 us; the launch traced here: 76.5 us
  waiting for transfers between devices  27.9 us (36%)
  starting transfers between devices  27.3 us (36%)
  Pallas kernels  20.5 us (27%)
    pallas_call x12, Pallas kernels, call(): pl.pallas_call(kernel, out_shape=outs, in_specs=in_specs or [VMEM] * len(...  20.5 us
    ppermute x4, waiting for transfers between devices, shards(): lax.ppermute(asks[b], 'ctx', route(a, b, False))  16.2 us
    ppermute x4, waiting for transfers between devices, shards(): lax.ppermute(far[n - low], 'ctx', route(1 + n // members, n % members, Tr...  7.97 us
    ppermute x4, starting transfers between devices, shards(): lax.ppermute(far[n - low], 'ctx', route(1 + n // members, n % members, Tr...  7.2 us
    ppermute x3, starting transfers between devices, shards(): lax.ppermute(pairs[b], 'ctx', route(0, b, False))  6.03 us
    ppermute x4, starting transfers between devices, shards(): lax.ppermute(asks[b], 'ctx', route(a, b, False))  5.52 us
    ppermute x3, starting transfers between devices, shards(): lax.ppermute(asks[b], 'ctx', route(0, b, False))  4.67 us
    ppermute x3, starting transfers between devices, shards(): lax.ppermute(near[b], 'ctx', route(0, b, True))  2.29 us
  transfers between devices with their start and end apart: 19, of which 6 were waited for; matrix products, arithmetic and copies ran while one was open for 0% of the time, Pallas kernels for 16%

profile of v2, /device:TPU:0, one launch (start us, length us, event | category | flops | bytes accessed | tf_op | source)
XLA Modules:
  0.0 76.5 jit_solution(5296224066434893191)
XLA Ops:
  0.6 1.6 %shard_map.140 = (bf16[512,384]{1,0:T(8,128)(2,1)S(1)}, bf16[512,384]{1,0:T(8,128)(2,1)S(1)}, bf16[512,384]{1,0:T(8,128)(2,1)S(1)}, bf16[512,384]{1,0:T(8,128)(2,1)S(1)}) custom-call(bf16[256,1536]{1,0:T(8,128)(2,1)} %bitcast.12, bf16[256,1536]{1,0:T(8,128)(2,1)} %bitcast.13), custom_call_target="tpu_custom_call" | custom-call | tf_op jit(solution)/shard_map/pallas_call | solution.py:311
  2.2 3.0 %collective-permute-start = (bf16[512,384]{1,0:T(8,128)(2,1)S(1)}, bf16[512,384]{1,0:T(8,128)(2,1)S(1)}, u32[]{:S(2)}, u32[]{:S(2)}) collective-permute-start(bf16[512,384]{1,0:T(8,128)(2,1)S(1)} %get-tuple-element.38), channel_id=1, source_target_pairs={{0,2},{2,4},{4,6},{6,0},{8,10},{10,12},{12,14},{14,8},{1,3},{3,5},... | collective-permute-start | bytes 1179656 | tf_op jit(solution)/shard_map/ppermute | solution.py:332
  5.2 1.6 %collective-permute-start.1 = (bf16[512,384]{1,0:T(8,128)(2,1)S(1)}, bf16[512,384]{1,0:T(8,128)(2,1)S(1)}, u32[]{:S(2)}, u32[]{:S(2)}) collective-permute-start(bf16[512,384]{1,0:T(8,128)(2,1)S(1)} %get-tuple-element.39), channel_id=1, source_target_pairs={{0,4},{2,6},{4,0},{6,2},{8,12},{10,14},{12,8},{14,10},{1,5},{3,7},... | collective-permute-start | bytes 1179656 | tf_op jit(solution)/shard_map/ppermute | solution.py:332
  6.8 1.4 %collective-permute-start.2 = (bf16[512,384]{1,0:T(8,128)(2,1)S(1)}, bf16[512,384]{1,0:T(8,128)(2,1)S(1)}, u32[]{:S(2)}, u32[]{:S(2)}) collective-permute-start(bf16[512,384]{1,0:T(8,128)(2,1)S(1)} %get-tuple-element.40), channel_id=1, source_target_pairs={{0,6},{2,0},{4,2},{6,4},{8,14},{10,8},{12,10},{14,12},{1,7},{3,1},... | collective-permute-start | bytes 1179656 | tf_op jit(solution)/shard_map/ppermute | solution.py:332
  8.2 2.1 %shard_map.141 = (bf16[128,384]{1,0:T(8,128)(2,1)S(1)}, bf16[128,384]{1,0:T(8,128)(2,1)S(1)}, bf16[128,384]{1,0:T(8,128)(2,1)S(1)}, bf16[128,384]{1,0:T(8,128)(2,1)S(1)}) custom-call(s32[1,256]{1,0:T(1,128)} %refs_0_.1, f32[1,128]{1,0:T(1,128)} %bitcast.18, bf16[256,1536]{1,0:T(8,128)(2,1)} %bitcast.14, bf16[512,384]{1,0:T(8,128)(2,1)S(1)} %get-tuple-element.33.refs_0_.refs_1_), custom_call_target="tpu_custom_call" | custom-call | tf_op jit(solution)/shard_map/pallas_call | solution.py:311
  10.4 2.7 %collective-permute-start.4 = (bf16[128,384]{1,0:T(8,128)(2,1)S(1)}, bf16[128,384]{1,0:T(8,128)(2,1)S(1)}, u32[]{:S(2)}, u32[]{:S(2)}) collective-permute-start(bf16[128,384]{1,0:T(8,128)(2,1)S(1)} %get-tuple-element.42), channel_id=1, source_target_pairs={{0,10},{2,12},{4,14},{6,8},{8,2},{10,4},{12,6},{14,0},{1,11},{3,13... | collective-permute-start | bytes 294920 | tf_op jit(solution)/shard_map/ppermute | solution.py:347
  13.1 0.3 collective-permute-start.3
  13.4 16.2 %collective-permute-done.4.refs_7_ = bf16[128,384]{1,0:T(8,128)(2,1)S(1)} collective-permute-done((bf16[128,384]{1,0:T(8,128)(2,1)S(1)}, bf16[128,384]{1,0:T(8,128)(2,1)S(1)}, u32[]{:S(2)}, u32[]{:S(2)}) %collective-permute-start.4) | collective-permute-done | bytes 98336 | tf_op jit(solution)/shard_map/ppermute | solution.py:347
  29.6 2.5 %collective-permute-start.5 = (bf16[128,384]{1,0:T(8,128)(2,1)S(1)}, bf16[128,384]{1,0:T(8,128)(2,1)S(1)}, u32[]{:S(2)}, u32[]{:S(2)}) collective-permute-start(bf16[128,384]{1,0:T(8,128)(2,1)S(1)} %get-tuple-element.44), channel_id=1, source_target_pairs={{0,12},{2,14},{4,8},{6,10},{8,4},{10,6},{12,0},{14,2},{1,13},{3,15... | collective-permute-start | bytes 294920 | tf_op jit(solution)/shard_map/ppermute | solution.py:347
  32.1 0.0 collective-permute-done.3.refs_6_
  32.1 0.0 collective-permute-start.6
  32.1 0.0 collective-permute-done.refs_1_.refs_2_
  32.1 0.3 collective-permute-start.7
  32.4 0.0 collective-permute-done.1.refs_2_.refs_3_
  32.4 3.1 %collective-permute-start.8 = (bf16[128,384]{1,0:T(8,128)(2,1)S(1)}, bf16[128,384]{1,0:T(8,128)(2,1)S(1)}, u32[]{:S(2)}, u32[]{:S(2)}) collective-permute-start(bf16[128,384]{1,0:T(8,128)(2,1)S(1)} %get-tuple-element.44), channel_id=1, source_target_pairs={{0,4},{2,6},{4,0},{6,2},{8,12},{10,14},{12,8},{14,10},{1,5},{3,7},... | collective-permute-start | bytes 294920 | tf_op jit(solution)/shard_map/ppermute | solution.py:348
  35.5 0.0 collective-permute-done.2.refs_3_.refs_4_
  35.5 1.3 %collective-permute-start.9 = (bf16[128,384]{1,0:T(8,128)(2,1)S(1)}, bf16[128,384]{1,0:T(8,128)(2,1)S(1)}, u32[]{:S(2)}, u32[]{:S(2)}) collective-permute-start(bf16[128,384]{1,0:T(8,128)(2,1)S(1)} %get-tuple-element.45), channel_id=1, source_target_pairs={{0,6},{2,0},{4,2},{6,4},{8,14},{10,8},{12,10},{14,12},{1,7},{3,1},... | collective-permute-start | bytes 294920 | tf_op jit(solution)/shard_map/ppermute | solution.py:348
  36.8 4.3 %shard_map.142 = (s32[1,256]{1,0:T(1,128)S(1)}, f32[1,128]{1,0:T(1,128)S(1)}, bf16[1536,3072]{1,0:T(8,128)(2,1)S(1)}, bf16[128,3072]{1,0:T(8,128)(2,1)S(1)}, bf1...) custom-call(s32[1,256]{1,0:T(1,128)} %refs_0_.1, ...), custom_call_target="tpu_custom_call" | custom-call | bytes 22883328 | tf_op jit(solution)/shard_map/pallas_call | solution.py:311
  41.1 0.5 shard_map.143.refs_5_
  41.6 1.5 %shard_map.144 = (bf16[400,128]{1,0:T(8,128)(2,1)S(1)}, bf16[400,128]{1,0:T(8,128)(2,1)S(1)}) custom-call(s32[1,256]{1,0:T(1,128)S(1)} %get-tuple-element.35.refs_0_.mask_ref, bf16[512,384]{1,0:T(8,128)(2,1)S(1)} %get-tuple-element.33.refs_0_.refs_1_, bf16[512,384]{1,0:T(8,128)(2,1)S(1)} %collective-permute-done.refs_1_.refs_2_, ...), custom_call_target="tpu_custom_call" | custom-call | flops 402653184 | bytes 1048576 | tf_op jit(solution)/shard_map/pallas_call | solution.py:311
  43.1 0.0 collective-permute-done.5.refs_6_
  43.1 0.0 collective-permute-done.6.refs_7_
  43.2 1.5 %shard_map.145 = (bf16[400,128]{1,0:T(8,128)(2,1)S(1)}, bf16[400,128]{1,0:T(8,128)(2,1)S(1)}) custom-call(bf16[400,128]{1,0:T(8,128)(2,1)S(1)} %get-tuple-element.43.refs_0_, bf16[512,384]{1,0:T(8,128)(2,1)S(1)} %get-tuple-element.33.refs_0_.refs_1_, bf16[512,384]{1,0:T(8,128)(2,1)S(1)} %collective-permute-done.refs_1_.refs_2_, ...), custom_call_target="tpu_custom_call" | custom-call | flops 402653184 | bytes 1048576 | tf_op jit(solution)/shard_map/pallas_call | solution.py:311
  44.7 0.0 collective-permute-done.7.refs_7_
  44.7 0.0 collective-permute-done.8.refs_8_
  44.7 0.0 collective-permute-done.9.refs_9_
  44.7 2.7 %shard_map.146 = (bf16[400,128]{1,0:T(8,128)(2,1)S(1)}, bf16[400,128]{1,0:T(8,128)(2,1)S(1)}, bf16[400,128]{1,0:T(8,128)(2,1)S(1)}, bf16[400,128]{1,0:T(8,128)(2,1)S(1)}) custom-call(bf16[400,128]{1,0:T(8,128)(2,1)S(1)} %get-tuple-element.46.refs_0_, bf16[512,384]{1,0:T(8,128)(2,1)S(1)} %get-tuple-element.33.refs_0_.refs_1_, ...), custom_call_target="tpu_custom_call" | custom-call | flops 805306368 | bytes 1048576 | tf_op jit(solution)/shard_map/pallas_call | solution.py:311
  47.4 0.2 collective-permute-start.10
  47.6 2.0 %collective-permute-start.11 = (bf16[400,128]{1,0:T(8,128)(2,1)S(1)}, bf16[400,128]{1,0:T(8,128)(2,1)S(1)}, u32[]{:S(2)}, u32[]{:S(2)}) collective-permute-start(bf16[400,128]{1,0:T(8,128)(2,1)S(1)} %get-tuple-element.49), channel_id=1, source_target_pairs={{4,0},{6,2},{0,4},{2,6},{12,8},{14,10},{8,12},{10,14},{5,1},{7,3},... | collective-permute-start | bytes 307208 | tf_op jit(solution)/shard_map/ppermute | solution.py:408
  49.6 2.5 %collective-permute-start.15 = (bf16[400,128]{1,0:T(8,128)(2,1)S(1)}, bf16[400,128]{1,0:T(8,128)(2,1)S(1)}, u32[]{:S(2)}, u32[]{:S(2)}) collective-permute-start(bf16[400,128]{1,0:T(8,128)(2,1)S(1)} %get-tuple-element.46.refs_0_), channel_id=1, source_target_pairs={{12,0},{14,2},{8,4},{10,6},{4,8},{6,10},{0,12},{2,14},{13,1},{15,3... | collective-permute-start | bytes 307208 | tf_op jit(solution)/shard_map/ppermute | solution.py:404
  52.1 0.1 collective-permute-start.12
  52.1 2.7 %collective-permute-start.16 = (bf16[400,128]{1,0:T(8,128)(2,1)S(1)}, bf16[400,128]{1,0:T(8,128)(2,1)S(1)}, u32[]{:S(2)}, u32[]{:S(2)}) collective-permute-start(bf16[400,128]{1,0:T(8,128)(2,1)S(1)} %get-tuple-element.52), channel_id=1, source_target_pairs={{14,0},{8,2},{10,4},{12,6},{6,8},{0,10},{2,12},{4,14},{15,1},{9,3}... | collective-permute-start | bytes 307208 | tf_op jit(solution)/shard_map/ppermute | solution.py:404
  54.9 2.0 %collective-permute-start.14 = (bf16[400,128]{1,0:T(8,128)(2,1)S(1)}, bf16[400,128]{1,0:T(8,128)(2,1)S(1)}, u32[]{:S(2)}, u32[]{:S(2)}) collective-permute-start(bf16[400,128]{1,0:T(8,128)(2,1)S(1)} %get-tuple-element.51), channel_id=1, source_target_pairs={{10,0},{12,2},{14,4},{8,6},{2,8},{4,10},{6,12},{0,14},{11,1},{13,3... | collective-permute-start | bytes 307208 | tf_op jit(solution)/shard_map/ppermute | solution.py:404
  56.9 0.0 collective-permute-done.11.refs_2_
  56.9 1.5 %collective-permute-done.12.refs_3_ = bf16[400,128]{1,0:T(8,128)(2,1)S(1)} collective-permute-done((bf16[400,128]{1,0:T(8,128)(2,1)S(1)}, bf16[400,128]{1,0:T(8,128)(2,1)S(1)}, u32[]{:S(2)}, u32[]{:S(2)}) %collective-permute-start.12) | collective-permute-done | bytes 102432 | tf_op jit(solution)/shard_map/ppermute | solution.py:408
  58.3 2.1 %collective-permute-done.16.refs_7_ = bf16[400,128]{1,0:T(8,128)(2,1)S(1)} collective-permute-done((bf16[400,128]{1,0:T(8,128)(2,1)S(1)}, bf16[400,128]{1,0:T(8,128)(2,1)S(1)}, u32[]{:S(2)}, u32[]{:S(2)}) %collective-permute-start.16) | collective-permute-done | bytes 102432 | tf_op jit(solution)/shard_map/ppermute | solution.py:404
  60.4 0.0 collective-permute-done.15.refs_6_
  60.4 5.8 %collective-permute-done.14.refs_5_ = bf16[400,128]{1,0:T(8,128)(2,1)S(1)} collective-permute-done((bf16[400,128]{1,0:T(8,128)(2,1)S(1)}, bf16[400,128]{1,0:T(8,128)(2,1)S(1)}, u32[]{:S(2)}, u32[]{:S(2)}) %collective-permute-start.14) | collective-permute-done | bytes 102432 | tf_op jit(solution)/shard_map/ppermute | solution.py:404
  66.3 0.0 collective-permute-done.13.refs_4_
  66.3 1.9 %shard_map.147 = (bf16[128,3072]{1,0:T(8,128)(2,1)S(1)}, bf16[128,1536]{1,0:T(8,128)(2,1)S(1)}) custom-call(bf16[2,128,128]{2,1,0:T(8,128)(2,1)S(1)} %get-tuple-element.36.places_ref, bf16[1536,3072]{1,0:T(8,128)(2,1)S(1)} %get-tuple-element.37.weight_ref, bf16[400,128]{1,0:T(8,128)(2,1)S(1)} %get-tuple-element.47.refs_0_, ...), custom_call_target="tpu_custom_call" | custom-call | tf_op jit(solution)/shard_map/pallas_call | solution.py:311
  68.3 0.1 collective-permute-start.17
  68.3 1.4 %shard_map.148.own_ref = f32[128,3072]{1,0:T(8,128)S(1)} custom-call(bf16[128,1536]{1,0:T(8,128)(2,1)S(1)} %get-tuple-element.53.rows_ref, bf16[1536,3072]{1,0:T(8,128)(2,1)S(1)} %get-tuple-element.37.weight_ref), custom_call_target="tpu_custom_call" | custom-call | flops 1207959552 | bytes 1048576 | tf_op jit(solution)/shard_map/pallas_call | solution.py:311
  69.7 0.9 %collective-permute-done.17.refs_0_ = bf16[128,3072]{1,0:T(8,128)(2,1)S(1)} collective-permute-done((bf16[128,3072]{1,0:T(8,128)(2,1)S(1)}, bf16[128,3072]{1,0:T(8,128)(2,1)S(1)}, u32[]{:S(2)}, u32[]{:S(2)}) %collective-permute-start.17) | collective-permute-done | bytes 786464 | tf_op jit(solution)/shard_map/ppermute | solution.py:417
  70.6 1.4 %shard_map.149 = (bf16[128,3072]{1,0:T(8,128)(2,1)S(1)}, f32[32,128]{1,0:T(8,128)S(1)}, f32[32,128]{1,0:T(8,128)S(1)}) custom-call(s32[1,256]{1,0:T(1,128)S(1)} %get-tuple-element.35.refs_0_.mask_ref, f32[128,3072]{1,0:T(8,128)S(1)} %shard_map.148.own_ref, bf16[128,3072]{1,0:T(8,128)(2,1)S(1)} %collective-permute-done.17.refs_0_, ...), custom_call_target="tpu_custom_call" | custom-call | tf_op jit(solution)/shard_map/pallas_call | solution.py:311
  72.0 1.5 %collective-permute-start.18 = (f32[32,128]{1,0:T(8,128)S(1)}, f32[32,128]{1,0:T(8,128)S(1)}, u32[]{:S(2)}, u32[]{:S(2)}) collective-permute-start(f32[32,128]{1,0:T(8,128)S(1)} %get-tuple-element.63), channel_id=1, source_target_pairs={{0,16},{16,0},{1,17},{17,1},{2,18},{18,2},{3,19},{19,3},{4,20},{20... | collective-permute-start | bytes 49160 | tf_op jit(solution)/shard_map/ppermute | solution.py:432
  73.6 0.9 %shard_map.150 = bf16[128,3072]{1,0:T(8,128)(2,1)} custom-call(bf16[128,3072]{1,0:T(8,128)(2,1)S(1)} %get-tuple-element.61.block_ref), custom_call_target="tpu_custom_call" | custom-call | tf_op jit(solution)/shard_map/pallas_call | solution.py:311
  74.5 1.4 %collective-permute-done.18.partner_ref = f32[32,128]{1,0:T(8,128)S(1)} collective-permute-done((f32[32,128]{1,0:T(8,128)S(1)}, f32[32,128]{1,0:T(8,128)S(1)}, u32[]{:S(2)}, u32[]{:S(2)}) %collective-permute-start.18) | collective-permute-done | bytes 16416 | tf_op jit(solution)/shard_map/ppermute | solution.py:432
  75.8 0.6 shard_map.151
  (2 shorter events, 0.0 us)
Async XLA Ops:
  2.2 29.9 %collective-permute-start = (bf16[512,384]{1,0:T(8,128)(2,1)S(1)}, bf16[512,384]{1,0:T(8,128)(2,1)S(1)}, u32[]{:S(2)}, u32[]{:S(2)}) collective-permute-start(bf16[512,384]{1,0:T(8,128)(2,1)S(1)} %get-tuple-element.38), channel_id=1, source_target_pairs={{0,2},{2,4},{4,6},{6,0},{8,10},{10,12},{12,14},{14,8},{1,3},{3,5},... | collective-permute-start | bytes 1179656 | tf_op jit(solution)/shard_map/ppermute | solution.py:332
  5.2 27.2 %collective-permute-start.1 = (bf16[512,384]{1,0:T(8,128)(2,1)S(1)}, bf16[512,384]{1,0:T(8,128)(2,1)S(1)}, u32[]{:S(2)}, u32[]{:S(2)}) collective-permute-start(bf16[512,384]{1,0:T(8,128)(2,1)S(1)} %get-tuple-element.39), channel_id=1, source_target_pairs={{0,4},{2,6},{4,0},{6,2},{8,12},{10,14},{12,8},{14,10},{1,5},{3,7},... | collective-permute-start | bytes 1179656 | tf_op jit(solution)/shard_map/ppermute | solution.py:332
  6.8 28.7 %collective-permute-start.2 = (bf16[512,384]{1,0:T(8,128)(2,1)S(1)}, bf16[512,384]{1,0:T(8,128)(2,1)S(1)}, u32[]{:S(2)}, u32[]{:S(2)}) collective-permute-start(bf16[512,384]{1,0:T(8,128)(2,1)S(1)} %get-tuple-element.40), channel_id=1, source_target_pairs={{0,6},{2,0},{4,2},{6,4},{8,14},{10,8},{12,10},{14,12},{1,7},{3,1},... | collective-permute-start | bytes 1179656 | tf_op jit(solution)/shard_map/ppermute | solution.py:332
  10.4 19.3 %collective-permute-start.4 = (bf16[128,384]{1,0:T(8,128)(2,1)S(1)}, bf16[128,384]{1,0:T(8,128)(2,1)S(1)}, u32[]{:S(2)}, u32[]{:S(2)}) collective-permute-start(bf16[128,384]{1,0:T(8,128)(2,1)S(1)} %get-tuple-element.42), channel_id=1, source_target_pairs={{0,10},{2,12},{4,14},{6,8},{8,2},{10,4},{12,6},{14,0},{1,11},{3,13... | collective-permute-start | bytes 294920 | tf_op jit(solution)/shard_map/ppermute | solution.py:347
  13.1 19.0 %collective-permute-start.3 = (bf16[128,384]{1,0:T(8,128)(2,1)S(1)}, bf16[128,384]{1,0:T(8,128)(2,1)S(1)}, u32[]{:S(2)}, u32[]{:S(2)}) collective-permute-start(bf16[128,384]{1,0:T(8,128)(2,1)S(1)} %get-tuple-element.34.refs_9_.refs_6_), channel_id=1, source_target_pairs={{0,8},{2,10},{4,12},{6,14},{8,0},{10,2},{12,4},{14,6},{1,9},{3,11}... | collective-permute-start | bytes 294920 | tf_op jit(solution)/shard_map/ppermute | solution.py:347
  29.6 13.5 %collective-permute-start.5 = (bf16[128,384]{1,0:T(8,128)(2,1)S(1)}, bf16[128,384]{1,0:T(8,128)(2,1)S(1)}, u32[]{:S(2)}, u32[]{:S(2)}) collective-permute-start(bf16[128,384]{1,0:T(8,128)(2,1)S(1)} %get-tuple-element.44), channel_id=1, source_target_pairs={{0,12},{2,14},{4,8},{6,10},{8,4},{10,6},{12,0},{14,2},{1,13},{3,15... | collective-permute-start | bytes 294920 | tf_op jit(solution)/shard_map/ppermute | solution.py:347
  32.1 11.0 %collective-permute-start.6 = (bf16[128,384]{1,0:T(8,128)(2,1)S(1)}, bf16[128,384]{1,0:T(8,128)(2,1)S(1)}, u32[]{:S(2)}, u32[]{:S(2)}) collective-permute-start(bf16[128,384]{1,0:T(8,128)(2,1)S(1)} %get-tuple-element.45), channel_id=1, source_target_pairs={{0,14},{2,8},{4,10},{6,12},{8,6},{10,0},{12,2},{14,4},{1,15},{3,9}... | collective-permute-start | bytes 294920 | tf_op jit(solution)/shard_map/ppermute | solution.py:347
  32.1 12.6 %collective-permute-start.7 = (bf16[128,384]{1,0:T(8,128)(2,1)S(1)}, bf16[128,384]{1,0:T(8,128)(2,1)S(1)}, u32[]{:S(2)}, u32[]{:S(2)}) collective-permute-start(bf16[128,384]{1,0:T(8,128)(2,1)S(1)} %get-tuple-element.42), channel_id=1, source_target_pairs={{0,2},{2,4},{4,6},{6,0},{8,10},{10,12},{12,14},{14,8},{1,3},{3,5},... | collective-permute-start | bytes 294920 | tf_op jit(solution)/shard_map/ppermute | solution.py:348
  32.4 12.3 %collective-permute-start.8 = (bf16[128,384]{1,0:T(8,128)(2,1)S(1)}, bf16[128,384]{1,0:T(8,128)(2,1)S(1)}, u32[]{:S(2)}, u32[]{:S(2)}) collective-permute-start(bf16[128,384]{1,0:T(8,128)(2,1)S(1)} %get-tuple-element.44), channel_id=1, source_target_pairs={{0,4},{2,6},{4,0},{6,2},{8,12},{10,14},{12,8},{14,10},{1,5},{3,7},... | collective-permute-start | bytes 294920 | tf_op jit(solution)/shard_map/ppermute | solution.py:348
  35.5 9.2 %collective-permute-start.9 = (bf16[128,384]{1,0:T(8,128)(2,1)S(1)}, bf16[128,384]{1,0:T(8,128)(2,1)S(1)}, u32[]{:S(2)}, u32[]{:S(2)}) collective-permute-start(bf16[128,384]{1,0:T(8,128)(2,1)S(1)} %get-tuple-element.45), channel_id=1, source_target_pairs={{0,6},{2,0},{4,2},{6,4},{8,14},{10,8},{12,10},{14,12},{1,7},{3,1},... | collective-permute-start | bytes 294920 | tf_op jit(solution)/shard_map/ppermute | solution.py:348
  47.4 7.5 %collective-permute-start.10 = (bf16[400,128]{1,0:T(8,128)(2,1)S(1)}, bf16[400,128]{1,0:T(8,128)(2,1)S(1)}, u32[]{:S(2)}, u32[]{:S(2)}) collective-permute-start(bf16[400,128]{1,0:T(8,128)(2,1)S(1)} %get-tuple-element.48), channel_id=1, source_target_pairs={{2,0},{4,2},{6,4},{0,6},{10,8},{12,10},{14,12},{8,14},{3,1},{5,3},... | collective-permute-start | bytes 307208 | tf_op jit(solution)/shard_map/ppermute | solution.py:408
  47.6 9.2 %collective-permute-start.11 = (bf16[400,128]{1,0:T(8,128)(2,1)S(1)}, bf16[400,128]{1,0:T(8,128)(2,1)S(1)}, u32[]{:S(2)}, u32[]{:S(2)}) collective-permute-start(bf16[400,128]{1,0:T(8,128)(2,1)S(1)} %get-tuple-element.49), channel_id=1, source_target_pairs={{4,0},{6,2},{0,4},{2,6},{12,8},{14,10},{8,12},{10,14},{5,1},{7,3},... | collective-permute-start | bytes 307208 | tf_op jit(solution)/shard_map/ppermute | solution.py:408
  49.6 10.8 %collective-permute-start.15 = (bf16[400,128]{1,0:T(8,128)(2,1)S(1)}, bf16[400,128]{1,0:T(8,128)(2,1)S(1)}, u32[]{:S(2)}, u32[]{:S(2)}) collective-permute-start(bf16[400,128]{1,0:T(8,128)(2,1)S(1)} %get-tuple-element.46.refs_0_), channel_id=1, source_target_pairs={{12,0},{14,2},{8,4},{10,6},{4,8},{6,10},{0,12},{2,14},{13,1},{15,3... | collective-permute-start | bytes 307208 | tf_op jit(solution)/shard_map/ppermute | solution.py:404
  52.1 6.3 %collective-permute-start.12 = (bf16[400,128]{1,0:T(8,128)(2,1)S(1)}, bf16[400,128]{1,0:T(8,128)(2,1)S(1)}, u32[]{:S(2)}, u32[]{:S(2)}) collective-permute-start(bf16[400,128]{1,0:T(8,128)(2,1)S(1)} %get-tuple-element.50), channel_id=1, source_target_pairs={{6,0},{0,2},{2,4},{4,6},{14,8},{8,10},{10,12},{12,14},{7,1},{1,3},... | collective-permute-start | bytes 307208 | tf_op jit(solution)/shard_map/ppermute | solution.py:408
  52.1 8.3 %collective-permute-start.16 = (bf16[400,128]{1,0:T(8,128)(2,1)S(1)}, bf16[400,128]{1,0:T(8,128)(2,1)S(1)}, u32[]{:S(2)}, u32[]{:S(2)}) collective-permute-start(bf16[400,128]{1,0:T(8,128)(2,1)S(1)} %get-tuple-element.52), channel_id=1, source_target_pairs={{14,0},{8,2},{10,4},{12,6},{6,8},{0,10},{2,12},{4,14},{15,1},{9,3}... | collective-permute-start | bytes 307208 | tf_op jit(solution)/shard_map/ppermute | solution.py:404
  54.9 11.4 %collective-permute-start.14 = (bf16[400,128]{1,0:T(8,128)(2,1)S(1)}, bf16[400,128]{1,0:T(8,128)(2,1)S(1)}, u32[]{:S(2)}, u32[]{:S(2)}) collective-permute-start(bf16[400,128]{1,0:T(8,128)(2,1)S(1)} %get-tuple-element.51), channel_id=1, source_target_pairs={{10,0},{12,2},{14,4},{8,6},{2,8},{4,10},{6,12},{0,14},{11,1},{13,3... | collective-permute-start | bytes 307208 | tf_op jit(solution)/shard_map/ppermute | solution.py:404
  56.9 9.4 %collective-permute-start.13 = (bf16[400,128]{1,0:T(8,128)(2,1)S(1)}, bf16[400,128]{1,0:T(8,128)(2,1)S(1)}, u32[]{:S(2)}, u32[]{:S(2)}) collective-permute-start(bf16[400,128]{1,0:T(8,128)(2,1)S(1)} %get-tuple-element.43.refs_0_), channel_id=1, source_target_pairs={{8,0},{10,2},{12,4},{14,6},{0,8},{2,10},{4,12},{6,14},{9,1},{11,3}... | collective-permute-start | bytes 307208 | tf_op jit(solution)/shard_map/ppermute | solution.py:404
  68.3 2.4 %collective-permute-start.17 = (bf16[128,3072]{1,0:T(8,128)(2,1)S(1)}, bf16[128,3072]{1,0:T(8,128)(2,1)S(1)}, u32[]{:S(2)}, u32[]{:S(2)}) collective-permute-start(bf16[128,3072]{1,0:T(8,128)(2,1)S(1)} %get-tuple-element.54), channel_id=1, source_target_pairs={{0,1},{1,0},{2,3},{3,2},{4,5},{5,4},{6,7},{7,6},{8,9},{9,8},{10,11... | collective-permute-start | bytes 2359304 | tf_op jit(solution)/shard_map/ppermute | solution.py:417
  72.0 3.8 %collective-permute-start.18 = (f32[32,128]{1,0:T(8,128)S(1)}, f32[32,128]{1,0:T(8,128)S(1)}, u32[]{:S(2)}, u32[]{:S(2)}) collective-permute-start(f32[32,128]{1,0:T(8,128)S(1)} %get-tuple-element.63), channel_id=1, source_target_pairs={{0,16},{16,0},{1,17},{17,1},{2,18},{18,2},{3,19},{19,3},{4,20},{20... | collective-permute-start | bytes 49160 | tf_op jit(solution)/shard_map/ppermute | solution.py:432

commit v3 on v2

--- a/solution.py
+++ b/solution.py
@@ -57,6 +57,10 @@
     return jnp.where(hit, 1.0, 0.0).astype(jnp.bfloat16)
 
 
+def hop(place, step, size):
+    return place ^ step if size & (size - 1) == 0 else (place + step) % size
+
+
 def ring_place(members):
     return lax.rem(lax.axis_index("ctx"), members)
 
@@ -74,7 +78,7 @@
     position = ring_place(members)
     copies = []
     for b in [b for b in range(1, members)] + [0]:
-        columns = pl.ds(pl.multiple_of(lax.rem(position + b, members) * width, depth), width)
+        columns = pl.ds(pl.multiple_of(hop(position, b, members) * width, depth), width)
         for n, source in enumerate((k_hbm, v_hbm)):
             target = outs[b].at[pl.ds(n * count, count), :]
             copies.append(pltpu.make_async_copy(source.at[:, columns], target, sems.at[n, b]))
@@ -99,7 +103,7 @@
     order = [b for b in range(1, members)] + [0]
     loads = {}
     for b in order:
-        columns = pl.ds(pl.multiple_of(lax.rem(position + b, members) * width, depth), width)
+        columns = pl.ds(pl.multiple_of(hop(position, b, members) * width, depth), width)
         loads[b] = pltpu.make_async_copy(q_hbm.at[:, columns], q_ref.at[b], q_sems.at[b])
         loads[b].start()
     for copy in small:
@@ -114,14 +118,11 @@
             asks[b][:, columns] = unit_rows(picked[:, columns], gain)
 
 
-def unit_kernel(depth, gain_ref, *refs):
-    pairs, out_ref = refs[:-1], refs[-1]
-    count = out_ref.shape[0] // len(pairs)
-    gain = gain_ref[...]
-    for b, ref in enumerate(pairs):
-        for first in range(0, out_ref.shape[1], depth):
-            columns = slice(first, first + depth)
-            out_ref[pl.ds(b * count, count), columns] = unit_rows(ref[pl.ds(0, count), columns], gain)
+def unit_kernel(depth, gain_ref, pair_ref, out_ref):
+    count = out_ref.shape[0]
+    for first in range(0, out_ref.shape[1], depth):
+        columns = slice(first, first + depth)
+        out_ref[:, columns] = unit_rows(pair_ref[pl.ds(0, count), columns], gain_ref[...])
 
 
 def fetch_kernel(dims, *refs):
@@ -142,9 +143,9 @@
 
 def attend_kernel(dims, *refs):
     members, partial, own_heads, depth, live_count, count, stat_rows, sources = dims
-    pairs, units_ref = refs[1 : members + 1], refs[members + 1]
-    asks = refs[members + 2 : members + 2 + sources]
-    outs, stats = refs[members + 2 + sources : -1], refs[-1]
+    pairs, units = refs[1 : members + 1], refs[members + 1 : 2 * members + 1]
+    asks = refs[2 * members + 1 : 2 * members + 1 + sources]
+    outs, stats = refs[2 * members + 1 + sources : -1], refs[-1]
     factor = depth ** (-0.5)
     power = factor * math.log2(math.e)
     lanes = lax.broadcasted_iota(jnp.int32, (live_count, stats.shape[2]), 1)
@@ -155,7 +156,7 @@
         columns = slice(h * depth, (h + 1) * depth)
         for s in range(sources):
             queries = asks[s][:, columns]
-            scores = [dot_nt(queries, units_ref[pl.ds(b * count, count), columns]) for b in range(members)]
+            scores = [dot_nt(queries, unit[:, columns]) for unit in units]
             biggest = jnp.max(functools.reduce(jnp.maximum, scores), axis=-1, keepdims=True)
             weights = [jnp.exp2((score - biggest) * power).astype(jnp.bfloat16) for score in scores]
             summed = functools.reduce(
@@ -207,7 +208,7 @@
                 placed = dot_f32(jnp.concatenate(spots, axis=1), jnp.concatenate(values, axis=0))
             else:
                 placed = dot_f32(places, values[0])
-            base = lax.rem(position + b, members) * width + h * depth
+            base = hop(position, b, members) * width + h * depth
             spread_ref[:, pl.ds(pl.multiple_of(base, depth), depth)] = placed.astype(jnp.bfloat16)
     own_ref[...] = spread_ref[pl.ds(0, share), :]
     for s in range(1, parts):
@@ -303,7 +304,7 @@
         pairs = []
         for g in range(groups):
             for p in range(members):
-                other = ((g + a) % groups) * members + (p + b) % members
+                other = hop(g, a, groups) * members + hop(p, b, members)
                 pairs.append((other, g * members + p) if back else (g * members + p, other))
         return pairs
 
@@ -329,7 +330,10 @@
         scratch=[pltpu.SemaphoreType.DMA((2, members))],
         limit=8,
     )
-    pairs = [pairs[0]] + [lax.ppermute(pairs[b], "ctx", route(0, b, False)) for b in range(1, members)]
+    pairs = list(pairs)
+    pair_order = sorted(range(1, members), key=lambda b: (b < members // 2, b))
+    for b in pair_order:
+        pairs[b] = lax.ppermute(pairs[b], "ctx", route(0, b, False))
     asks = call(
         functools.partial(ask_kernel, (members, own_heads, depth, live_count)),
         (*map(in_hbm, (replay_mask, query_gain[None], query_proj[0])), pairs[0]),
@@ -344,7 +348,12 @@
         ],
         limit=16,
     )
-    far_asks = [lax.ppermute(asks[b], "ctx", route(a, b, False)) for a in range(1, groups) for b in range(members)]
+    pieces = 2
+    far_routes = sorted(((a, b) for a in range(1, groups) for b in range(members)), key=lambda r: (r[1] % 2, r))
+    cuts = [piece * len(far_routes) // pieces for piece in range(pieces + 1)]
+    far_asks = []
+    for a, b in far_routes:
+        far_asks.append(lax.ppermute(asks[b], "ctx", route(a, b, False)))
     near_asks = [asks[0]] + [lax.ppermute(asks[b], "ctx", route(0, b, False)) for b in range(1, members)]
 
     wanted = (
@@ -372,12 +381,15 @@
     parcel_rows = own_heads * live_count + (stat_rows if partial else 0)
     parcel_shape = shaped((parcel_rows, depth), bf16)
 
-    (units,) = call(
-        functools.partial(unit_kernel, depth),
-        (key_gain_here, *pairs),
-        [shaped((members * count, own_width), bf16)],
-        cost=pl.CostEstimate(flops=0, transcendentals=0, bytes_accessed=1 << 20),
-    )
+    units = [
+        call(
+            functools.partial(unit_kernel, depth),
+            (key_gain_here, pair),
+            [shaped((count, own_width), bf16)],
+            cost=pl.CostEstimate(flops=0, transcendentals=0, bytes_accessed=1 << 18),
+        )[0]
+        for pair in pairs
+    ]
 
     def attend(after, asks):
         scores = len(asks) * live_count * members * count * own_heads
@@ -386,26 +398,27 @@
                 attend_kernel,
                 (members, partial, own_heads, depth, live_count, count, stat_rows, len(asks)),
             ),
-            (after, *pairs, units, *asks),
+            (after, *pairs, *units, *asks),
             [parcel_shape] * len(asks),
             scratch=[pltpu.VMEM((len(asks), live_count, live_count), f32)],
             cost=pl.CostEstimate(flops=4 * scores * depth, transcendentals=scores, bytes_accessed=1 << 20),
         )
 
-    after, distant = mask, []
-    pieces = 2
+    after = mask
+    parcels = {}
     for piece in range(pieces):
-        low, high = (piece * len(far_asks) // pieces, (piece + 1) * len(far_asks) // pieces)
+        low, high = cuts[piece], cuts[piece + 1]
         if low == high:
             continue
         far = attend(after, far_asks[low:high])
         after = far[0]
-        distant += [
-            lax.ppermute(far[n - low], "ctx", route(1 + n // members, n % members, True))
-            for n in range(low, high)
-        ]
+        for n in range(low, high):
+            parcels[far_routes[n]] = lax.ppermute(far[n - low], "ctx", route(*far_routes[n], True))
     near = attend(after, near_asks)
-    parcels = [near[0]] + [lax.ppermute(near[b], "ctx", route(0, b, True)) for b in range(1, members)] + distant
+    parcels[0, 0] = near[0]
+    for b in range(1, members):
+        parcels[0, b] = lax.ppermute(near[b], "ctx", route(0, b, True))
+    parcels = [parcels[a, b] for a in range(groups) for b in range(members)]
 
     merged = call(
         functools.partial(merge_kernel, (members, groups, own_heads, depth, live_count, stat_rows, parts)),

time: 76.6 us -> 76.5 us (level)
  starting transfers between devices: 27.3 us -> 26.1 us
  waiting for transfers between devices: 27.9 us -> 28.7 us
    ppermute x14, starting transfers between devices: 21 us -> 19.8 us  [the longest x3 5.32 us: shards(): parcels[0, b] = lax.ppermute(near[b], 'ctx', route(0, b, True))]
    ppermute x14, waiting for transfers between devices: 25.7 us -> 26.5 us  [the longest x4 16.8 us: shards(): far_asks.append(lax.ppermute(asks[b], 'ctx', route(a, b, False)))]
    pallas_call x12 -> x15, Pallas kernels: 20.5 us -> 20.8 us  [call(): pl.pallas_call(kernel, out_shape=outs, in_specs=in_specs or [VMEM] * len(...]
  transfers between devices with their start and end apart: 19 -> 19, of which waited for: 6 -> 7; matrix products, arithmetic and copies ran while one was open for 0% -> 0% of each run, Pallas kernels for 16% -> 16%
where the time goes in v3:
time: 76.5 us; the launch traced here: 76.4 us
  waiting for transfers between devices  28.7 us (38%)
  starting transfers between devices  26.1 us (34%)
  Pallas kernels  20.8 us (27%)
    pallas_call x15, Pallas kernels, call(): pl.pallas_call(kernel, out_shape=outs, in_specs=in_specs or [VMEM] * len(...  20.8 us
    ppermute x4, waiting for transfers between devices, shards(): far_asks.append(lax.ppermute(asks[b], 'ctx', route(a, b, False)))  16.8 us
    ppermute x4, waiting for transfers between devices, shards(): lax.ppermute(far[n - low], 'ctx', route(*far_routes[n], True))  9.06 us
    ppermute x3, starting transfers between devices, shards(): parcels[0, b] = lax.ppermute(near[b], 'ctx', route(0, b, True))  5.32 us
    ppermute x4, starting transfers between devices, shards(): far_asks.append(lax.ppermute(asks[b], 'ctx', route(a, b, False)))  5.29 us
    ppermute x3, starting transfers between devices, shards(): lax.ppermute(asks[b], 'ctx', route(0, b, False))  4.69 us
    ppermute x3, starting transfers between devices, shards(): pairs[b] = lax.ppermute(pairs[b], 'ctx', route(0, b, False))  4.64 us
    ppermute x4, starting transfers between devices, shards(): lax.ppermute(far[n - low], 'ctx', route(*far_routes[n], True))  4.52 us
  transfers between devices with their start and end apart: 19, of which 7 were waited for; matrix products, arithmetic and copies ran while one was open for 0% of the time, Pallas kernels for 16%

profile of v3, /device:TPU:0, one launch (start us, length us, event | category | flops | bytes accessed | tf_op | source)
XLA Modules:
  0.0 76.4 jit_solution(16729163385555794153)
XLA Ops:
  0.6 1.6 %shard_map.140 = (bf16[512,384]{1,0:T(8,128)(2,1)S(1)}, bf16[512,384]{1,0:T(8,128)(2,1)S(1)}, bf16[512,384]{1,0:T(8,128)(2,1)S(1)}, bf16[512,384]{1,0:T(8,128)(2,1)S(1)}) custom-call(bf16[256,1536]{1,0:T(8,128)(2,1)} %bitcast.12, bf16[256,1536]{1,0:T(8,128)(2,1)} %bitcast.13), custom_call_target="tpu_custom_call" | custom-call | tf_op jit(solution)/shard_map/pallas_call | solution.py:312
  2.2 3.1 %collective-permute-start = (bf16[512,384]{1,0:T(8,128)(2,1)S(1)}, bf16[512,384]{1,0:T(8,128)(2,1)S(1)}, u32[]{:S(2)}, u32[]{:S(2)}) collective-permute-start(bf16[512,384]{1,0:T(8,128)(2,1)S(1)} %get-tuple-element.38), channel_id=1, source_target_pairs={{0,2},{2,0},{4,6},{6,4},{8,10},{10,8},{12,14},{14,12},{1,3},{3,1},... | collective-permute-start | bytes 1179656 | tf_op jit(solution)/shard_map/ppermute | solution.py:336
  5.3 1.6 %collective-permute-start.1 = (bf16[512,384]{1,0:T(8,128)(2,1)S(1)}, bf16[512,384]{1,0:T(8,128)(2,1)S(1)}, u32[]{:S(2)}, u32[]{:S(2)}) collective-permute-start(bf16[512,384]{1,0:T(8,128)(2,1)S(1)} %get-tuple-element.39), channel_id=1, source_target_pairs={{0,4},{2,6},{4,0},{6,2},{8,12},{10,14},{12,8},{14,10},{1,5},{3,7},... | collective-permute-start | bytes 1179656 | tf_op jit(solution)/shard_map/ppermute | solution.py:336
  6.8 0.0 collective-permute-start.2
  6.8 2.1 %shard_map.141 = (bf16[128,384]{1,0:T(8,128)(2,1)S(1)}, bf16[128,384]{1,0:T(8,128)(2,1)S(1)}, bf16[128,384]{1,0:T(8,128)(2,1)S(1)}, bf16[128,384]{1,0:T(8,128)(2,1)S(1)}) custom-call(s32[1,256]{1,0:T(1,128)} %refs_0_.1, f32[1,128]{1,0:T(1,128)} %bitcast.18, bf16[256,1536]{1,0:T(8,128)(2,1)} %bitcast.14, ...), custom_call_target="tpu_custom_call" | custom-call | tf_op jit(solution)/shard_map/pallas_call | solution.py:312
  9.0 4.1 %collective-permute-start.4 = (bf16[128,384]{1,0:T(8,128)(2,1)S(1)}, bf16[128,384]{1,0:T(8,128)(2,1)S(1)}, u32[]{:S(2)}, u32[]{:S(2)}) collective-permute-start(bf16[128,384]{1,0:T(8,128)(2,1)S(1)} %get-tuple-element.42), channel_id=1, source_target_pairs={{0,12},{2,14},{4,8},{6,10},{8,4},{10,6},{12,0},{14,2},{1,13},{3,15... | collective-permute-start | bytes 294920 | tf_op jit(solution)/shard_map/ppermute | solution.py:356
  13.0 0.0 collective-permute-start.3
  13.0 16.7 %collective-permute-done.4.refs_10_ = bf16[128,384]{1,0:T(8,128)(2,1)S(1)} collective-permute-done((bf16[128,384]{1,0:T(8,128)(2,1)S(1)}, bf16[128,384]{1,0:T(8,128)(2,1)S(1)}, u32[]{:S(2)}, u32[]{:S(2)}) %collective-permute-start.4) | collective-permute-done | bytes 98336 | tf_op jit(solution)/shard_map/ppermute | solution.py:356
  29.8 0.0 collective-permute-start.5
  29.8 0.0 collective-permute-done.3.refs_9_
  29.8 1.2 %collective-permute-start.6 = (bf16[128,384]{1,0:T(8,128)(2,1)S(1)}, bf16[128,384]{1,0:T(8,128)(2,1)S(1)}, u32[]{:S(2)}, u32[]{:S(2)}) collective-permute-start(bf16[128,384]{1,0:T(8,128)(2,1)S(1)} %get-tuple-element.45), channel_id=1, source_target_pairs={{0,14},{2,12},{4,10},{6,8},{8,6},{10,4},{12,2},{14,0},{1,15},{3,13... | collective-permute-start | bytes 294920 | tf_op jit(solution)/shard_map/ppermute | solution.py:356
  31.0 0.0 collective-permute-done.pair_ref.refs_2_
  31.0 3.2 %collective-permute-start.8 = (bf16[128,384]{1,0:T(8,128)(2,1)S(1)}, bf16[128,384]{1,0:T(8,128)(2,1)S(1)}, u32[]{:S(2)}, u32[]{:S(2)}) collective-permute-start(bf16[128,384]{1,0:T(8,128)(2,1)S(1)} %get-tuple-element.42), channel_id=1, source_target_pairs={{0,4},{2,6},{4,0},{6,2},{8,12},{10,14},{12,8},{14,10},{1,5},{3,7},... | collective-permute-start | bytes 294920 | tf_op jit(solution)/shard_map/ppermute | solution.py:357
  34.2 0.0 collective-permute-done.1.pair_ref.refs_3_
  34.2 0.5 collective-permute-start.7
  34.7 0.0 collective-permute-done.2.pair_ref.refs_4_
  34.7 1.0 %collective-permute-start.9 = (bf16[128,384]{1,0:T(8,128)(2,1)S(1)}, bf16[128,384]{1,0:T(8,128)(2,1)S(1)}, u32[]{:S(2)}, u32[]{:S(2)}) collective-permute-start(bf16[128,384]{1,0:T(8,128)(2,1)S(1)} %get-tuple-element.45), channel_id=1, source_target_pairs={{0,6},{2,4},{4,2},{6,0},{8,14},{10,12},{12,10},{14,8},{1,7},{3,5},... | collective-permute-start | bytes 294920 | tf_op jit(solution)/shard_map/ppermute | solution.py:357
  35.7 4.3 %shard_map.142 = (s32[1,256]{1,0:T(1,128)S(1)}, f32[1,128]{1,0:T(1,128)S(1)}, bf16[1536,3072]{1,0:T(8,128)(2,1)S(1)}, bf16[128,3072]{1,0:T(8,128)(2,1)S(1)}, bf1...) custom-call(s32[1,256]{1,0:T(1,128)} %refs_0_.1, ...), custom_call_target="tpu_custom_call" | custom-call | bytes 22883328 | tf_op jit(solution)/shard_map/pallas_call | solution.py:312
  40.0 0.2 shard_map.143.refs_5_
  40.2 0.2 shard_map.146.refs_8_
  40.4 0.2 shard_map.145.refs_7_
  40.6 0.2 shard_map.144.refs_6_
  40.8 1.6 %shard_map.147 = (bf16[400,128]{1,0:T(8,128)(2,1)S(1)}, bf16[400,128]{1,0:T(8,128)(2,1)S(1)}) custom-call(s32[1,256]{1,0:T(1,128)S(1)} %get-tuple-element.35.refs_0_.mask_ref, bf16[512,384]{1,0:T(8,128)(2,1)S(1)} %get-tuple-element.33.refs_0_.pair_ref.refs_1_, bf16[512,384]{1,0:T(8,128)(2,1)S(1)} %collective-permute-done.pair_ref.refs_2_, ...), custom_call_target="tpu_custom_call" | custom-call | flops 402653184 | bytes 1048576 | tf_op jit(solution)/shard_map/pallas_call | solution.py:312
  42.4 0.0 collective-permute-done.5.refs_9_
  42.4 0.0 collective-permute-done.6.refs_10_
  42.4 1.6 %shard_map.148 = (bf16[400,128]{1,0:T(8,128)(2,1)S(1)}, bf16[400,128]{1,0:T(8,128)(2,1)S(1)}) custom-call(bf16[400,128]{1,0:T(8,128)(2,1)S(1)} %get-tuple-element.43.refs_0_, bf16[512,384]{1,0:T(8,128)(2,1)S(1)} %get-tuple-element.33.refs_0_.pair_ref.refs_1_, bf16[512,384]{1,0:T(8,128)(2,1)S(1)} %collective-permute-done.pair_ref.refs_2_, ...), custom_call_target="tpu_custom_call" | custom-call | flops 402653184 | bytes 1048576 | tf_op jit(solution)/shard_map/pallas_call | solution.py:312
  43.9 2.7 %shard_map.149 = (bf16[400,128]{1,0:T(8,128)(2,1)S(1)}, bf16[400,128]{1,0:T(8,128)(2,1)S(1)}, bf16[400,128]{1,0:T(8,128)(2,1)S(1)}, bf16[400,128]{1,0:T(8,128)(2,1)S(1)}) custom-call(bf16[400,128]{1,0:T(8,128)(2,1)S(1)} %get-tuple-element.46.refs_0_, bf16[512,384]{1,0:T(8,128)(2,1)S(1)} %get-tuple-element.33.refs_0_.pair_ref.refs_1_, ...), custom_call_target="tpu_custom_call" | custom-call | flops 805306368 | bytes 1048576 | tf_op jit(solution)/shard_map/pallas_call | solution.py:312
  46.6 0.7 collective-permute-start.10
  47.3 1.8 %collective-permute-start.11 = (bf16[400,128]{1,0:T(8,128)(2,1)S(1)}, bf16[400,128]{1,0:T(8,128)(2,1)S(1)}, u32[]{:S(2)}, u32[]{:S(2)}) collective-permute-start(bf16[400,128]{1,0:T(8,128)(2,1)S(1)} %get-tuple-element.49), channel_id=1, source_target_pairs={{4,0},{6,2},{0,4},{2,6},{12,8},{14,10},{8,12},{10,14},{5,1},{7,3},... | collective-permute-start | bytes 307208 | tf_op jit(solution)/shard_map/ppermute | solution.py:420
  49.1 0.9 %collective-permute-start.14 = (bf16[400,128]{1,0:T(8,128)(2,1)S(1)}, bf16[400,128]{1,0:T(8,128)(2,1)S(1)}, u32[]{:S(2)}, u32[]{:S(2)}) collective-permute-start(bf16[400,128]{1,0:T(8,128)(2,1)S(1)} %get-tuple-element.46.refs_0_), channel_id=1, source_target_pairs={{10,0},{8,2},{14,4},{12,6},{2,8},{0,10},{6,12},{4,14},{11,1},{9,3}... | collective-permute-start | bytes 307208 | tf_op jit(solution)/shard_map/ppermute | solution.py:416
  50.0 2.8 %collective-permute-start.12 = (bf16[400,128]{1,0:T(8,128)(2,1)S(1)}, bf16[400,128]{1,0:T(8,128)(2,1)S(1)}, u32[]{:S(2)}, u32[]{:S(2)}) collective-permute-start(bf16[400,128]{1,0:T(8,128)(2,1)S(1)} %get-tuple-element.50), channel_id=1, source_target_pairs={{6,0},{4,2},{2,4},{0,6},{14,8},{12,10},{10,12},{8,14},{7,1},{5,3},... | collective-permute-start | bytes 307208 | tf_op jit(solution)/shard_map/ppermute | solution.py:420
  52.8 2.5 %collective-permute-start.16 = (bf16[400,128]{1,0:T(8,128)(2,1)S(1)}, bf16[400,128]{1,0:T(8,128)(2,1)S(1)}, u32[]{:S(2)}, u32[]{:S(2)}) collective-permute-start(bf16[400,128]{1,0:T(8,128)(2,1)S(1)} %get-tuple-element.52), channel_id=1, source_target_pairs={{14,0},{12,2},{10,4},{8,6},{6,8},{4,10},{2,12},{0,14},{15,1},{13,3... | collective-permute-start | bytes 307208 | tf_op jit(solution)/shard_map/ppermute | solution.py:416
  55.4 1.1 %collective-permute-start.15 = (bf16[400,128]{1,0:T(8,128)(2,1)S(1)}, bf16[400,128]{1,0:T(8,128)(2,1)S(1)}, u32[]{:S(2)}, u32[]{:S(2)}) collective-permute-start(bf16[400,128]{1,0:T(8,128)(2,1)S(1)} %get-tuple-element.51), channel_id=1, source_target_pairs={{12,0},{14,2},{8,4},{10,6},{4,8},{6,10},{0,12},{2,14},{13,1},{15,3... | collective-permute-start | bytes 307208 | tf_op jit(solution)/shard_map/ppermute | solution.py:416
  56.5 0.0 collective-permute-done.11.refs_2_
  56.5 0.0 collective-permute-start.13
  56.5 0.6 collective-permute-done.12.refs_3_
  57.1 3.3 %collective-permute-done.16.refs_7_ = bf16[400,128]{1,0:T(8,128)(2,1)S(1)} collective-permute-done((bf16[400,128]{1,0:T(8,128)(2,1)S(1)}, bf16[400,128]{1,0:T(8,128)(2,1)S(1)}, u32[]{:S(2)}, u32[]{:S(2)}) %collective-permute-start.16) | collective-permute-done | bytes 102432 | tf_op jit(solution)/shard_map/ppermute | solution.py:416
  60.4 2.8 %collective-permute-done.14.refs_5_ = bf16[400,128]{1,0:T(8,128)(2,1)S(1)} collective-permute-done((bf16[400,128]{1,0:T(8,128)(2,1)S(1)}, bf16[400,128]{1,0:T(8,128)(2,1)S(1)}, u32[]{:S(2)}, u32[]{:S(2)}) %collective-permute-start.14) | collective-permute-done | bytes 102432 | tf_op jit(solution)/shard_map/ppermute | solution.py:416
  63.2 2.9 %collective-permute-done.13.refs_4_ = bf16[400,128]{1,0:T(8,128)(2,1)S(1)} collective-permute-done((bf16[400,128]{1,0:T(8,128)(2,1)S(1)}, bf16[400,128]{1,0:T(8,128)(2,1)S(1)}, u32[]{:S(2)}, u32[]{:S(2)}) %collective-permute-start.13) | collective-permute-done | bytes 102432 | tf_op jit(solution)/shard_map/ppermute | solution.py:416
  66.2 2.0 %shard_map.150 = (bf16[128,3072]{1,0:T(8,128)(2,1)S(1)}, bf16[128,1536]{1,0:T(8,128)(2,1)S(1)}) custom-call(bf16[2,128,128]{2,1,0:T(8,128)(2,1)S(1)} %get-tuple-element.36.places_ref, bf16[1536,3072]{1,0:T(8,128)(2,1)S(1)} %get-tuple-element.37.weight_ref, bf16[400,128]{1,0:T(8,128)(2,1)S(1)} %get-tuple-element.47.refs_0_, ...), custom_call_target="tpu_custom_call" | custom-call | tf_op jit(solution)/shard_map/pallas_call | solution.py:312
  68.2 0.1 collective-permute-start.17
  68.2 1.4 %shard_map.151.own_ref = f32[128,3072]{1,0:T(8,128)S(1)} custom-call(bf16[128,1536]{1,0:T(8,128)(2,1)S(1)} %get-tuple-element.53.rows_ref, bf16[1536,3072]{1,0:T(8,128)(2,1)S(1)} %get-tuple-element.37.weight_ref), custom_call_target="tpu_custom_call" | custom-call | flops 1207959552 | bytes 1048576 | tf_op jit(solution)/shard_map/pallas_call | solution.py:312
  69.6 0.9 %collective-permute-done.17.refs_0_ = bf16[128,3072]{1,0:T(8,128)(2,1)S(1)} collective-permute-done((bf16[128,3072]{1,0:T(8,128)(2,1)S(1)}, bf16[128,3072]{1,0:T(8,128)(2,1)S(1)}, u32[]{:S(2)}, u32[]{:S(2)}) %collective-permute-start.17) | collective-permute-done | bytes 786464 | tf_op jit(solution)/shard_map/ppermute | solution.py:430
  70.5 1.4 %shard_map.152 = (bf16[128,3072]{1,0:T(8,128)(2,1)S(1)}, f32[32,128]{1,0:T(8,128)S(1)}, f32[32,128]{1,0:T(8,128)S(1)}) custom-call(s32[1,256]{1,0:T(1,128)S(1)} %get-tuple-element.35.refs_0_.mask_ref, f32[128,3072]{1,0:T(8,128)S(1)} %shard_map.151.own_ref, bf16[128,3072]{1,0:T(8,128)(2,1)S(1)} %collective-permute-done.17.refs_0_, ...), custom_call_target="tpu_custom_call" | custom-call | tf_op jit(solution)/shard_map/pallas_call | solution.py:312
  71.9 1.6 %collective-permute-start.18 = (f32[32,128]{1,0:T(8,128)S(1)}, f32[32,128]{1,0:T(8,128)S(1)}, u32[]{:S(2)}, u32[]{:S(2)}) collective-permute-start(f32[32,128]{1,0:T(8,128)S(1)} %get-tuple-element.63), channel_id=1, source_target_pairs={{0,16},{16,0},{1,17},{17,1},{2,18},{18,2},{3,19},{19,3},{4,20},{20... | collective-permute-start | bytes 49160 | tf_op jit(solution)/shard_map/ppermute | solution.py:445
  73.5 0.9 %shard_map.153 = bf16[128,3072]{1,0:T(8,128)(2,1)} custom-call(bf16[128,3072]{1,0:T(8,128)(2,1)S(1)} %get-tuple-element.61.block_ref), custom_call_target="tpu_custom_call" | custom-call | tf_op jit(solution)/shard_map/pallas_call | solution.py:312
  74.4 1.4 %collective-permute-done.18.partner_ref = f32[32,128]{1,0:T(8,128)S(1)} collective-permute-done((f32[32,128]{1,0:T(8,128)S(1)}, f32[32,128]{1,0:T(8,128)S(1)}, u32[]{:S(2)}, u32[]{:S(2)}) %collective-permute-start.18) | collective-permute-done | bytes 16416 | tf_op jit(solution)/shard_map/ppermute | solution.py:445
  75.7 0.6 shard_map.154
  (5 shorter events, 0.0 us)
Async XLA Ops:
  2.2 28.8 %collective-permute-start = (bf16[512,384]{1,0:T(8,128)(2,1)S(1)}, bf16[512,384]{1,0:T(8,128)(2,1)S(1)}, u32[]{:S(2)}, u32[]{:S(2)}) collective-permute-start(bf16[512,384]{1,0:T(8,128)(2,1)S(1)} %get-tuple-element.38), channel_id=1, source_target_pairs={{0,2},{2,0},{4,6},{6,4},{8,10},{10,8},{12,14},{14,12},{1,3},{3,1},... | collective-permute-start | bytes 1179656 | tf_op jit(solution)/shard_map/ppermute | solution.py:336
  5.3 28.9 %collective-permute-start.1 = (bf16[512,384]{1,0:T(8,128)(2,1)S(1)}, bf16[512,384]{1,0:T(8,128)(2,1)S(1)}, u32[]{:S(2)}, u32[]{:S(2)}) collective-permute-start(bf16[512,384]{1,0:T(8,128)(2,1)S(1)} %get-tuple-element.39), channel_id=1, source_target_pairs={{0,4},{2,6},{4,0},{6,2},{8,12},{10,14},{12,8},{14,10},{1,5},{3,7},... | collective-permute-start | bytes 1179656 | tf_op jit(solution)/shard_map/ppermute | solution.py:336
  6.8 27.9 %collective-permute-start.2 = (bf16[512,384]{1,0:T(8,128)(2,1)S(1)}, bf16[512,384]{1,0:T(8,128)(2,1)S(1)}, u32[]{:S(2)}, u32[]{:S(2)}) collective-permute-start(bf16[512,384]{1,0:T(8,128)(2,1)S(1)} %get-tuple-element.40), channel_id=1, source_target_pairs={{0,6},{2,4},{4,2},{6,0},{8,14},{10,12},{12,10},{14,8},{1,7},{3,5},... | collective-permute-start | bytes 1179656 | tf_op jit(solution)/shard_map/ppermute | solution.py:336
  9.0 20.8 %collective-permute-start.4 = (bf16[128,384]{1,0:T(8,128)(2,1)S(1)}, bf16[128,384]{1,0:T(8,128)(2,1)S(1)}, u32[]{:S(2)}, u32[]{:S(2)}) collective-permute-start(bf16[128,384]{1,0:T(8,128)(2,1)S(1)} %get-tuple-element.42), channel_id=1, source_target_pairs={{0,12},{2,14},{4,8},{6,10},{8,4},{10,6},{12,0},{14,2},{1,13},{3,15... | collective-permute-start | bytes 294920 | tf_op jit(solution)/shard_map/ppermute | solution.py:356
  13.0 16.8 %collective-permute-start.3 = (bf16[128,384]{1,0:T(8,128)(2,1)S(1)}, bf16[128,384]{1,0:T(8,128)(2,1)S(1)}, u32[]{:S(2)}, u32[]{:S(2)}) collective-permute-start(bf16[128,384]{1,0:T(8,128)(2,1)S(1)} %get-tuple-element.34.refs_9_), channel_id=1, source_target_pairs={{0,8},{2,10},{4,12},{6,14},{8,0},{10,2},{12,4},{14,6},{1,9},{3,11}... | collective-permute-start | bytes 294920 | tf_op jit(solution)/shard_map/ppermute | solution.py:356
  29.8 12.6 %collective-permute-start.5 = (bf16[128,384]{1,0:T(8,128)(2,1)S(1)}, bf16[128,384]{1,0:T(8,128)(2,1)S(1)}, u32[]{:S(2)}, u32[]{:S(2)}) collective-permute-start(bf16[128,384]{1,0:T(8,128)(2,1)S(1)} %get-tuple-element.44), channel_id=1, source_target_pairs={{0,10},{2,8},{4,14},{6,12},{8,2},{10,0},{12,6},{14,4},{1,11},{3,9}... | collective-permute-start | bytes 294920 | tf_op jit(solution)/shard_map/ppermute | solution.py:356
  29.8 12.6 %collective-permute-start.6 = (bf16[128,384]{1,0:T(8,128)(2,1)S(1)}, bf16[128,384]{1,0:T(8,128)(2,1)S(1)}, u32[]{:S(2)}, u32[]{:S(2)}) collective-permute-start(bf16[128,384]{1,0:T(8,128)(2,1)S(1)} %get-tuple-element.45), channel_id=1, source_target_pairs={{0,14},{2,12},{4,10},{6,8},{8,6},{10,4},{12,2},{14,0},{1,15},{3,13... | collective-permute-start | bytes 294920 | tf_op jit(solution)/shard_map/ppermute | solution.py:356
  31.0 12.9 %collective-permute-start.8 = (bf16[128,384]{1,0:T(8,128)(2,1)S(1)}, bf16[128,384]{1,0:T(8,128)(2,1)S(1)}, u32[]{:S(2)}, u32[]{:S(2)}) collective-permute-start(bf16[128,384]{1,0:T(8,128)(2,1)S(1)} %get-tuple-element.42), channel_id=1, source_target_pairs={{0,4},{2,6},{4,0},{6,2},{8,12},{10,14},{12,8},{14,10},{1,5},{3,7},... | collective-permute-start | bytes 294920 | tf_op jit(solution)/shard_map/ppermute | solution.py:357
  34.2 9.7 %collective-permute-start.7 = (bf16[128,384]{1,0:T(8,128)(2,1)S(1)}, bf16[128,384]{1,0:T(8,128)(2,1)S(1)}, u32[]{:S(2)}, u32[]{:S(2)}) collective-permute-start(bf16[128,384]{1,0:T(8,128)(2,1)S(1)} %get-tuple-element.44), channel_id=1, source_target_pairs={{0,2},{2,0},{4,6},{6,4},{8,10},{10,8},{12,14},{14,12},{1,3},{3,1},... | collective-permute-start | bytes 294920 | tf_op jit(solution)/shard_map/ppermute | solution.py:357
  34.7 9.2 %collective-permute-start.9 = (bf16[128,384]{1,0:T(8,128)(2,1)S(1)}, bf16[128,384]{1,0:T(8,128)(2,1)S(1)}, u32[]{:S(2)}, u32[]{:S(2)}) collective-permute-start(bf16[128,384]{1,0:T(8,128)(2,1)S(1)} %get-tuple-element.45), channel_id=1, source_target_pairs={{0,6},{2,4},{4,2},{6,0},{8,14},{10,12},{12,10},{14,8},{1,7},{3,5},... | collective-permute-start | bytes 294920 | tf_op jit(solution)/shard_map/ppermute | solution.py:357
  46.6 8.7 %collective-permute-start.10 = (bf16[400,128]{1,0:T(8,128)(2,1)S(1)}, bf16[400,128]{1,0:T(8,128)(2,1)S(1)}, u32[]{:S(2)}, u32[]{:S(2)}) collective-permute-start(bf16[400,128]{1,0:T(8,128)(2,1)S(1)} %get-tuple-element.48), channel_id=1, source_target_pairs={{2,0},{0,2},{6,4},{4,6},{10,8},{8,10},{14,12},{12,14},{3,1},{1,3},... | collective-permute-start | bytes 307208 | tf_op jit(solution)/shard_map/ppermute | solution.py:420
  47.3 9.1 %collective-permute-start.11 = (bf16[400,128]{1,0:T(8,128)(2,1)S(1)}, bf16[400,128]{1,0:T(8,128)(2,1)S(1)}, u32[]{:S(2)}, u32[]{:S(2)}) collective-permute-start(bf16[400,128]{1,0:T(8,128)(2,1)S(1)} %get-tuple-element.49), channel_id=1, source_target_pairs={{4,0},{6,2},{0,4},{2,6},{12,8},{14,10},{8,12},{10,14},{5,1},{7,3},... | collective-permute-start | bytes 307208 | tf_op jit(solution)/shard_map/ppermute | solution.py:420
  49.1 14.1 %collective-permute-start.14 = (bf16[400,128]{1,0:T(8,128)(2,1)S(1)}, bf16[400,128]{1,0:T(8,128)(2,1)S(1)}, u32[]{:S(2)}, u32[]{:S(2)}) collective-permute-start(bf16[400,128]{1,0:T(8,128)(2,1)S(1)} %get-tuple-element.46.refs_0_), channel_id=1, source_target_pairs={{10,0},{8,2},{14,4},{12,6},{2,8},{0,10},{6,12},{4,14},{11,1},{9,3}... | collective-permute-start | bytes 307208 | tf_op jit(solution)/shard_map/ppermute | solution.py:416
  50.0 7.1 %collective-permute-start.12 = (bf16[400,128]{1,0:T(8,128)(2,1)S(1)}, bf16[400,128]{1,0:T(8,128)(2,1)S(1)}, u32[]{:S(2)}, u32[]{:S(2)}) collective-permute-start(bf16[400,128]{1,0:T(8,128)(2,1)S(1)} %get-tuple-element.50), channel_id=1, source_target_pairs={{6,0},{4,2},{2,4},{0,6},{14,8},{12,10},{10,12},{8,14},{7,1},{5,3},... | collective-permute-start | bytes 307208 | tf_op jit(solution)/shard_map/ppermute | solution.py:420
  52.8 7.6 %collective-permute-start.16 = (bf16[400,128]{1,0:T(8,128)(2,1)S(1)}, bf16[400,128]{1,0:T(8,128)(2,1)S(1)}, u32[]{:S(2)}, u32[]{:S(2)}) collective-permute-start(bf16[400,128]{1,0:T(8,128)(2,1)S(1)} %get-tuple-element.52), channel_id=1, source_target_pairs={{14,0},{12,2},{10,4},{8,6},{6,8},{4,10},{2,12},{0,14},{15,1},{13,3... | collective-permute-start | bytes 307208 | tf_op jit(solution)/shard_map/ppermute | solution.py:416
  55.4 7.9 %collective-permute-start.15 = (bf16[400,128]{1,0:T(8,128)(2,1)S(1)}, bf16[400,128]{1,0:T(8,128)(2,1)S(1)}, u32[]{:S(2)}, u32[]{:S(2)}) collective-permute-start(bf16[400,128]{1,0:T(8,128)(2,1)S(1)} %get-tuple-element.51), channel_id=1, source_target_pairs={{12,0},{14,2},{8,4},{10,6},{4,8},{6,10},{0,12},{2,14},{13,1},{15,3... | collective-permute-start | bytes 307208 | tf_op jit(solution)/shard_map/ppermute | solution.py:416
  56.5 9.7 %collective-permute-start.13 = (bf16[400,128]{1,0:T(8,128)(2,1)S(1)}, bf16[400,128]{1,0:T(8,128)(2,1)S(1)}, u32[]{:S(2)}, u32[]{:S(2)}) collective-permute-start(bf16[400,128]{1,0:T(8,128)(2,1)S(1)} %get-tuple-element.43.refs_0_), channel_id=1, source_target_pairs={{8,0},{10,2},{12,4},{14,6},{0,8},{2,10},{4,12},{6,14},{9,1},{11,3}... | collective-permute-start | bytes 307208 | tf_op jit(solution)/shard_map/ppermute | solution.py:416
  68.2 2.4 %collective-permute-start.17 = (bf16[128,3072]{1,0:T(8,128)(2,1)S(1)}, bf16[128,3072]{1,0:T(8,128)(2,1)S(1)}, u32[]{:S(2)}, u32[]{:S(2)}) collective-permute-start(bf16[128,3072]{1,0:T(8,128)(2,1)S(1)} %get-tuple-element.54), channel_id=1, source_target_pairs={{0,1},{1,0},{2,3},{3,2},{4,5},{5,4},{6,7},{7,6},{8,9},{9,8},{10,11... | collective-permute-start | bytes 2359304 | tf_op jit(solution)/shard_map/ppermute | solution.py:430
  71.9 3.8 %collective-permute-start.18 = (f32[32,128]{1,0:T(8,128)S(1)}, f32[32,128]{1,0:T(8,128)S(1)}, u32[]{:S(2)}, u32[]{:S(2)}) collective-permute-start(f32[32,128]{1,0:T(8,128)S(1)} %get-tuple-element.63), channel_id=1, source_target_pairs={{0,16},{16,0},{1,17},{17,1},{2,18},{18,2},{3,19},{19,3},{4,20},{20... | collective-permute-start | bytes 49160 | tf_op jit(solution)/shard_map/ppermute | solution.py:445

commit v4 on v3

--- a/solution.py
+++ b/solution.py
@@ -348,9 +348,7 @@
         ],
         limit=16,
     )
-    pieces = 2
-    far_routes = sorted(((a, b) for a in range(1, groups) for b in range(members)), key=lambda r: (r[1] % 2, r))
-    cuts = [piece * len(far_routes) // pieces for piece in range(pieces + 1)]
+    far_routes = [(a, b) for a in range(1, groups) for b in range(members)]
     far_asks = []
     for a, b in far_routes:
         far_asks.append(lax.ppermute(asks[b], "ctx", route(a, b, False)))
@@ -404,20 +402,17 @@
             cost=pl.CostEstimate(flops=4 * scores * depth, transcendentals=scores, bytes_accessed=1 << 20),
         )
 
-    after = mask
-    parcels = {}
-    for piece in range(pieces):
-        low, high = cuts[piece], cuts[piece + 1]
-        if low == high:
-            continue
-        far = attend(after, far_asks[low:high])
-        after = far[0]
-        for n in range(low, high):
-            parcels[far_routes[n]] = lax.ppermute(far[n - low], "ctx", route(*far_routes[n], True))
-    near = attend(after, near_asks)
-    parcels[0, 0] = near[0]
-    for b in range(1, members):
-        parcels[0, b] = lax.ppermute(near[b], "ctx", route(0, b, True))
+    after, parcels = mask, {}
+    for n, ask in enumerate(far_asks):
+        (far,) = attend(after, [ask])
+        after = far
+        parcels[far_routes[n]] = lax.ppermute(far, "ctx", route(*far_routes[n], True))
+    if members > 1:
+        near = attend(after, near_asks[1:])
+        after = near[0]
+        for b in range(1, members):
+            parcels[0, b] = lax.ppermute(near[b - 1], "ctx", route(0, b, True))
+    (parcels[0, 0],) = attend(after, near_asks[:1])
     parcels = [parcels[a, b] for a in range(groups) for b in range(members)]
 
     merged = call(

time: 76.5 us -> 76.5 us (level)
  waiting for transfers between devices: 28.7 us -> 22.7 us
  starting transfers between devices: 26.1 us -> 30.5 us
  Pallas kernels: 20.8 us -> 22.3 us
    ppermute x4, starting transfers between devices: 5.29 us -> 8.86 us  [shards(): far_asks.append(lax.ppermute(asks[b], 'ctx', route(a, b, False)))]
    ppermute x4, waiting for transfers between devices: 16.8 us -> 13.2 us  [shards(): far_asks.append(lax.ppermute(asks[b], 'ctx', route(a, b, False)))]
    ppermute x7, waiting for transfers between devices: 9.71 us -> 7.3 us  [the longest x4 7.15 us: shards(): lax.ppermute(far, 'ctx', route(*far_routes[n], True))]
    ppermute x7, starting transfers between devices: 9.84 us -> 11.5 us  [the longest x4 6.89 us: shards(): lax.ppermute(far, 'ctx', route(*far_routes[n], True))]
    pallas_call x15 -> x18, Pallas kernels: 20.8 us -> 22.3 us  [call(): pl.pallas_call(kernel, out_shape=outs, in_specs=in_specs or [VMEM] * len(...]
    ppermute x3, starting transfers between devices: 4.69 us -> 3.84 us  [shards(): lax.ppermute(asks[b], 'ctx', route(0, b, False))]
  transfers between devices with their start and end apart: 19 -> 19, of which waited for: 7 -> 6; matrix products, arithmetic and copies ran while one was open for 0% -> 0% of each run, Pallas kernels for 16% -> 19%
where the time goes in v4:
time: 76.5 us; the launch traced here: 76.3 us
  starting transfers between devices  30.5 us (40%)
  waiting for transfers between devices  22.7 us (30%)
  Pallas kernels  22.3 us (29%)
    pallas_call x18, Pallas kernels, call(): pl.pallas_call(kernel, out_shape=outs, in_specs=in_specs or [VMEM] * len(...  22.3 us
    ppermute x4, waiting for transfers between devices, shards(): far_asks.append(lax.ppermute(asks[b], 'ctx', route(a, b, False)))  13.2 us
    ppermute x4, starting transfers between devices, shards(): far_asks.append(lax.ppermute(asks[b], 'ctx', route(a, b, False)))  8.86 us
    ppermute x4, waiting for transfers between devices, shards(): lax.ppermute(far, 'ctx', route(*far_routes[n], True))  7.15 us
    ppermute x4, starting transfers between devices, shards(): lax.ppermute(far, 'ctx', route(*far_routes[n], True))  6.89 us
    ppermute x3, starting transfers between devices, shards(): pairs[b] = lax.ppermute(pairs[b], 'ctx', route(0, b, False))  4.64 us
    ppermute x3, starting transfers between devices, shards(): parcels[0, b] = lax.ppermute(near[b - 1], 'ctx', route(0, b, True))  4.64 us
    ppermute x3, starting transfers between devices, shards(): lax.ppermute(asks[b], 'ctx', route(0, b, False))  3.84 us
  transfers between devices with their start and end apart: 19, of which 6 were waited for; matrix products, arithmetic and copies ran while one was open for 0% of the time, Pallas kernels for 19%

profile of v4, /device:TPU:0, one launch (start us, length us, event | category | flops | bytes accessed | tf_op | source)
XLA Modules:
  0.0 76.3 jit_solution(12305250854117464803)
XLA Ops:
  0.6 1.6 %shard_map.140 = (bf16[512,384]{1,0:T(8,128)(2,1)S(1)}, bf16[512,384]{1,0:T(8,128)(2,1)S(1)}, bf16[512,384]{1,0:T(8,128)(2,1)S(1)}, bf16[512,384]{1,0:T(8,128)(2,1)S(1)}) custom-call(bf16[256,1536]{1,0:T(8,128)(2,1)} %bitcast.12, bf16[256,1536]{1,0:T(8,128)(2,1)} %bitcast.13), custom_call_target="tpu_custom_call" | custom-call | tf_op jit(solution)/shard_map/pallas_call | solution.py:312
  2.2 3.1 %collective-permute-start = (bf16[512,384]{1,0:T(8,128)(2,1)S(1)}, bf16[512,384]{1,0:T(8,128)(2,1)S(1)}, u32[]{:S(2)}, u32[]{:S(2)}) collective-permute-start(bf16[512,384]{1,0:T(8,128)(2,1)S(1)} %get-tuple-element.33), channel_id=1, source_target_pairs={{0,2},{2,0},{4,6},{6,4},{8,10},{10,8},{12,14},{14,12},{1,3},{3,1},... | collective-permute-start | bytes 1179656 | tf_op jit(solution)/shard_map/ppermute | solution.py:336
  5.3 1.6 %collective-permute-start.1 = (bf16[512,384]{1,0:T(8,128)(2,1)S(1)}, bf16[512,384]{1,0:T(8,128)(2,1)S(1)}, u32[]{:S(2)}, u32[]{:S(2)}) collective-permute-start(bf16[512,384]{1,0:T(8,128)(2,1)S(1)} %get-tuple-element.34), channel_id=1, source_target_pairs={{0,4},{2,6},{4,0},{6,2},{8,12},{10,14},{12,8},{14,10},{1,5},{3,7},... | collective-permute-start | bytes 1179656 | tf_op jit(solution)/shard_map/ppermute | solution.py:336
  6.8 0.0 collective-permute-start.2
  6.8 2.1 %shard_map.141 = (bf16[128,384]{1,0:T(8,128)(2,1)S(1)}, bf16[128,384]{1,0:T(8,128)(2,1)S(1)}, bf16[128,384]{1,0:T(8,128)(2,1)S(1)}, bf16[128,384]{1,0:T(8,128)(2,1)S(1)}) custom-call(s32[1,256]{1,0:T(1,128)} %refs_0_.1, f32[1,128]{1,0:T(1,128)} %bitcast.18, bf16[256,1536]{1,0:T(8,128)(2,1)} %bitcast.14, ...), custom_call_target="tpu_custom_call" | custom-call | tf_op jit(solution)/shard_map/pallas_call | solution.py:312
  9.0 4.0 %collective-permute-start.4 = (bf16[128,384]{1,0:T(8,128)(2,1)S(1)}, bf16[128,384]{1,0:T(8,128)(2,1)S(1)}, u32[]{:S(2)}, u32[]{:S(2)}) collective-permute-start(bf16[128,384]{1,0:T(8,128)(2,1)S(1)} %get-tuple-element.37), channel_id=1, source_target_pairs={{0,10},{2,8},{4,14},{6,12},{8,2},{10,0},{12,6},{14,4},{1,11},{3,9}... | collective-permute-start | bytes 294920 | tf_op jit(solution)/shard_map/ppermute | solution.py:354
  13.0 0.3 collective-permute-start.3
  13.3 13.2 %collective-permute-done.4.refs_9_ = bf16[128,384]{1,0:T(8,128)(2,1)S(1)} collective-permute-done((bf16[128,384]{1,0:T(8,128)(2,1)S(1)}, bf16[128,384]{1,0:T(8,128)(2,1)S(1)}, u32[]{:S(2)}, u32[]{:S(2)}) %collective-permute-start.4) | collective-permute-done | bytes 98336 | tf_op jit(solution)/shard_map/ppermute | solution.py:354
  26.5 2.8 %collective-permute-start.5 = (bf16[128,384]{1,0:T(8,128)(2,1)S(1)}, bf16[128,384]{1,0:T(8,128)(2,1)S(1)}, u32[]{:S(2)}, u32[]{:S(2)}) collective-permute-start(bf16[128,384]{1,0:T(8,128)(2,1)S(1)} %get-tuple-element.38), channel_id=1, source_target_pairs={{0,12},{2,14},{4,8},{6,10},{8,4},{10,6},{12,0},{14,2},{1,13},{3,15... | collective-permute-start | bytes 294920 | tf_op jit(solution)/shard_map/ppermute | solution.py:354
  29.3 1.7 %collective-permute-start.6 = (bf16[128,384]{1,0:T(8,128)(2,1)S(1)}, bf16[128,384]{1,0:T(8,128)(2,1)S(1)}, u32[]{:S(2)}, u32[]{:S(2)}) collective-permute-start(bf16[128,384]{1,0:T(8,128)(2,1)S(1)} %get-tuple-element.39), channel_id=1, source_target_pairs={{0,14},{2,12},{4,10},{6,8},{8,6},{10,4},{12,2},{14,0},{1,15},{3,13... | collective-permute-start | bytes 294920 | tf_op jit(solution)/shard_map/ppermute | solution.py:354
  31.0 0.0 collective-permute-done.pair_ref.refs_2_
  31.0 1.9 %collective-permute-start.7 = (bf16[128,384]{1,0:T(8,128)(2,1)S(1)}, bf16[128,384]{1,0:T(8,128)(2,1)S(1)}, u32[]{:S(2)}, u32[]{:S(2)}) collective-permute-start(bf16[128,384]{1,0:T(8,128)(2,1)S(1)} %get-tuple-element.37), channel_id=1, source_target_pairs={{0,2},{2,0},{4,6},{6,4},{8,10},{10,8},{12,14},{14,12},{1,3},{3,1},... | collective-permute-start | bytes 294920 | tf_op jit(solution)/shard_map/ppermute | solution.py:355
  33.0 0.9 %collective-permute-start.8 = (bf16[128,384]{1,0:T(8,128)(2,1)S(1)}, bf16[128,384]{1,0:T(8,128)(2,1)S(1)}, u32[]{:S(2)}, u32[]{:S(2)}) collective-permute-start(bf16[128,384]{1,0:T(8,128)(2,1)S(1)} %get-tuple-element.38), channel_id=1, source_target_pairs={{0,4},{2,6},{4,0},{6,2},{8,12},{10,14},{12,8},{14,10},{1,5},{3,7},... | collective-permute-start | bytes 294920 | tf_op jit(solution)/shard_map/ppermute | solution.py:355
  33.9 0.0 collective-permute-done.2.pair_ref.refs_4_
  33.9 1.0 %collective-permute-start.9 = (bf16[128,384]{1,0:T(8,128)(2,1)S(1)}, bf16[128,384]{1,0:T(8,128)(2,1)S(1)}, u32[]{:S(2)}, u32[]{:S(2)}) collective-permute-start(bf16[128,384]{1,0:T(8,128)(2,1)S(1)} %get-tuple-element.39), channel_id=1, source_target_pairs={{0,6},{2,4},{4,2},{6,0},{8,14},{10,12},{12,10},{14,8},{1,7},{3,5},... | collective-permute-start | bytes 294920 | tf_op jit(solution)/shard_map/ppermute | solution.py:355
  34.9 4.3 %shard_map.142 = (s32[1,256]{1,0:T(1,128)S(1)}, f32[1,128]{1,0:T(1,128)S(1)}, bf16[1536,3072]{1,0:T(8,128)(2,1)S(1)}, bf16[128,3072]{1,0:T(8,128)(2,1)S(1)}, bf1...) custom-call(s32[1,256]{1,0:T(1,128)} %refs_0_.1, ...), custom_call_target="tpu_custom_call" | custom-call | bytes 22883328 | tf_op jit(solution)/shard_map/pallas_call | solution.py:312
  39.2 0.2 shard_map.143.refs_5_
  39.4 0.2 shard_map.146.refs_8_
  39.6 0.2 shard_map.145.refs_7_
  39.8 0.2 shard_map.144.refs_6_
  40.0 1.0 %shard_map.147.refs_0_ = bf16[400,128]{1,0:T(8,128)(2,1)S(1)} custom-call(s32[1,256]{1,0:T(1,128)S(1)} %get-tuple-element.30.refs_0_.mask_ref, bf16[512,384]{1,0:T(8,128)(2,1)S(1)} %get-tuple-element.28.refs_0_.pair_ref.refs_1_, bf16[512,384]{1,0:T(8,128)(2,1)S(1)} %collective-permute-done.pair_ref.refs_2_, ...), custom_call_target="tpu_custom_call" | custom-call | flops 201326592 | bytes 1048576 | tf_op jit(solution)/shard_map/pallas_call | solution.py:312
  41.0 1.0 %shard_map.148.refs_0_ = bf16[400,128]{1,0:T(8,128)(2,1)S(1)} custom-call(bf16[400,128]{1,0:T(8,128)(2,1)S(1)} %shard_map.147.refs_0_, bf16[512,384]{1,0:T(8,128)(2,1)S(1)} %get-tuple-element.28.refs_0_.pair_ref.refs_1_, bf16[512,384]{1,0:T(8,128)(2,1)S(1)} %collective-permute-done.pair_ref.refs_2_, ...), custom_call_target="tpu_custom_call" | custom-call | flops 201326592 | bytes 1048576 | tf_op jit(solution)/shard_map/pallas_call | solution.py:312
  42.0 1.0 %shard_map.149.refs_0_ = bf16[400,128]{1,0:T(8,128)(2,1)S(1)} custom-call(bf16[400,128]{1,0:T(8,128)(2,1)S(1)} %shard_map.148.refs_0_, bf16[512,384]{1,0:T(8,128)(2,1)S(1)} %get-tuple-element.28.refs_0_.pair_ref.refs_1_, bf16[512,384]{1,0:T(8,128)(2,1)S(1)} %collective-permute-done.pair_ref.refs_2_, ...), custom_call_target="tpu_custom_call" | custom-call | flops 201326592 | bytes 1048576 | tf_op jit(solution)/shard_map/pallas_call | solution.py:312
  43.1 0.0 collective-permute-done.6.refs_9_
  43.1 1.0 %shard_map.150.refs_0_ = bf16[400,128]{1,0:T(8,128)(2,1)S(1)} custom-call(bf16[400,128]{1,0:T(8,128)(2,1)S(1)} %shard_map.149.refs_0_, bf16[512,384]{1,0:T(8,128)(2,1)S(1)} %get-tuple-element.28.refs_0_.pair_ref.refs_1_, bf16[512,384]{1,0:T(8,128)(2,1)S(1)} %collective-permute-done.pair_ref.refs_2_, ...), custom_call_target="tpu_custom_call" | custom-call | flops 201326592 | bytes 1048576 | tf_op jit(solution)/shard_map/pallas_call | solution.py:312
  44.1 0.0 collective-permute-done.9.refs_11_
  44.2 2.1 %shard_map.151 = (bf16[400,128]{1,0:T(8,128)(2,1)S(1)}, bf16[400,128]{1,0:T(8,128)(2,1)S(1)}, bf16[400,128]{1,0:T(8,128)(2,1)S(1)}) custom-call(bf16[400,128]{1,0:T(8,128)(2,1)S(1)} %shard_map.150.refs_0_, bf16[512,384]{1,0:T(8,128)(2,1)S(1)} %get-tuple-element.28.refs_0_.pair_ref.refs_1_, bf16[512,384]{1,0:T(8,128)(2,1)S(1)} %collective-permute-done.pair_ref.refs_2_, ...), custom_call_target="tpu_custom_call" | custom-call | flops 603979776 | bytes 1048576 | tf_op jit(solution)/shard_map/pallas_call | solution.py:312
  46.3 2.0 %collective-permute-start.11 = (bf16[400,128]{1,0:T(8,128)(2,1)S(1)}, bf16[400,128]{1,0:T(8,128)(2,1)S(1)}, u32[]{:S(2)}, u32[]{:S(2)}) collective-permute-start(bf16[400,128]{1,0:T(8,128)(2,1)S(1)} %get-tuple-element.41), channel_id=1, source_target_pairs={{4,0},{6,2},{0,4},{2,6},{12,8},{14,10},{8,12},{10,14},{5,1},{7,3},... | collective-permute-start | bytes 307208 | tf_op jit(solution)/shard_map/ppermute | solution.py:414
  48.3 1.1 %collective-permute-start.12 = (bf16[400,128]{1,0:T(8,128)(2,1)S(1)}, bf16[400,128]{1,0:T(8,128)(2,1)S(1)}, u32[]{:S(2)}, u32[]{:S(2)}) collective-permute-start(bf16[400,128]{1,0:T(8,128)(2,1)S(1)} %get-tuple-element.42), channel_id=1, source_target_pairs={{6,0},{4,2},{2,4},{0,6},{14,8},{12,10},{10,12},{8,14},{7,1},{5,3},... | collective-permute-start | bytes 307208 | tf_op jit(solution)/shard_map/ppermute | solution.py:414
  49.3 2.0 %collective-permute-start.16 = (bf16[400,128]{1,0:T(8,128)(2,1)S(1)}, bf16[400,128]{1,0:T(8,128)(2,1)S(1)}, u32[]{:S(2)}, u32[]{:S(2)}) collective-permute-start(bf16[400,128]{1,0:T(8,128)(2,1)S(1)} %shard_map.150.refs_0_), channel_id=1, source_target_pairs={{14,0},{12,2},{10,4},{8,6},{6,8},{4,10},{2,12},{0,14},{15,1},{13,3... | collective-permute-start | bytes 307208 | tf_op jit(solution)/shard_map/ppermute | solution.py:409
  51.3 1.7 %collective-permute-start.15 = (bf16[400,128]{1,0:T(8,128)(2,1)S(1)}, bf16[400,128]{1,0:T(8,128)(2,1)S(1)}, u32[]{:S(2)}, u32[]{:S(2)}) collective-permute-start(bf16[400,128]{1,0:T(8,128)(2,1)S(1)} %shard_map.149.refs_0_), channel_id=1, source_target_pairs={{12,0},{14,2},{8,4},{10,6},{4,8},{6,10},{0,12},{2,14},{13,1},{15,3... | collective-permute-start | bytes 307208 | tf_op jit(solution)/shard_map/ppermute | solution.py:409
  53.1 1.6 %collective-permute-start.10 = (bf16[400,128]{1,0:T(8,128)(2,1)S(1)}, bf16[400,128]{1,0:T(8,128)(2,1)S(1)}, u32[]{:S(2)}, u32[]{:S(2)}) collective-permute-start(bf16[400,128]{1,0:T(8,128)(2,1)S(1)} %get-tuple-element.40.refs_0_), channel_id=1, source_target_pairs={{2,0},{0,2},{6,4},{4,6},{10,8},{8,10},{14,12},{12,14},{3,1},{1,3},... | collective-permute-start | bytes 307208 | tf_op jit(solution)/shard_map/ppermute | solution.py:414
  54.6 1.0 %collective-permute-start.14 = (bf16[400,128]{1,0:T(8,128)(2,1)S(1)}, bf16[400,128]{1,0:T(8,128)(2,1)S(1)}, u32[]{:S(2)}, u32[]{:S(2)}) collective-permute-start(bf16[400,128]{1,0:T(8,128)(2,1)S(1)} %shard_map.148.refs_0_), channel_id=1, source_target_pairs={{10,0},{8,2},{14,4},{12,6},{2,8},{0,10},{6,12},{4,14},{11,1},{9,3}... | collective-permute-start | bytes 307208 | tf_op jit(solution)/shard_map/ppermute | solution.py:409
  55.6 0.0 collective-permute-done.12.refs_3_
  55.6 2.2 %collective-permute-start.13 = (bf16[400,128]{1,0:T(8,128)(2,1)S(1)}, bf16[400,128]{1,0:T(8,128)(2,1)S(1)}, u32[]{:S(2)}, u32[]{:S(2)}) collective-permute-start(bf16[400,128]{1,0:T(8,128)(2,1)S(1)} %shard_map.147.refs_0_), channel_id=1, source_target_pairs={{8,0},{10,2},{12,4},{14,6},{0,8},{2,10},{4,12},{6,14},{9,1},{11,3}... | collective-permute-start | bytes 307208 | tf_op jit(solution)/shard_map/ppermute | solution.py:409
  57.8 1.0 %shard_map.152.refs_0_ = bf16[400,128]{1,0:T(8,128)(2,1)S(1)} custom-call(bf16[400,128]{1,0:T(8,128)(2,1)S(1)} %get-tuple-element.40.refs_0_, bf16[512,384]{1,0:T(8,128)(2,1)S(1)} %get-tuple-element.28.refs_0_.pair_ref.refs_1_, bf16[512,384]{1,0:T(8,128)(2,1)S(1)} %collective-permute-done.pair_ref.refs_2_, ...), custom_call_target="tpu_custom_call" | custom-call | flops 201326592 | bytes 1048576 | tf_op jit(solution)/shard_map/pallas_call | solution.py:312
  58.8 0.1 collective-permute-done.10.refs_1_
  59.0 6.8 %collective-permute-done.14.refs_5_ = bf16[400,128]{1,0:T(8,128)(2,1)S(1)} collective-permute-done((bf16[400,128]{1,0:T(8,128)(2,1)S(1)}, bf16[400,128]{1,0:T(8,128)(2,1)S(1)}, u32[]{:S(2)}, u32[]{:S(2)}) %collective-permute-start.14) | collective-permute-done | bytes 102432 | tf_op jit(solution)/shard_map/ppermute | solution.py:409
  65.8 0.3 collective-permute-done.13.refs_4_
  66.1 2.0 %shard_map.153 = (bf16[128,3072]{1,0:T(8,128)(2,1)S(1)}, bf16[128,1536]{1,0:T(8,128)(2,1)S(1)}) custom-call(bf16[2,128,128]{2,1,0:T(8,128)(2,1)S(1)} %get-tuple-element.31.places_ref, bf16[1536,3072]{1,0:T(8,128)(2,1)S(1)} %get-tuple-element.32.weight_ref, bf16[400,128]{1,0:T(8,128)(2,1)S(1)} %shard_map.152.refs_0_, ...), custom_call_target="tpu_custom_call" | custom-call | tf_op jit(solution)/shard_map/pallas_call | solution.py:312
  68.1 0.1 collective-permute-start.17
  68.2 1.4 %shard_map.154.own_ref = f32[128,3072]{1,0:T(8,128)S(1)} custom-call(bf16[128,1536]{1,0:T(8,128)(2,1)S(1)} %get-tuple-element.43.rows_ref, bf16[1536,3072]{1,0:T(8,128)(2,1)S(1)} %get-tuple-element.32.weight_ref), custom_call_target="tpu_custom_call" | custom-call | flops 1207959552 | bytes 1048576 | tf_op jit(solution)/shard_map/pallas_call | solution.py:312
  69.6 0.9 %collective-permute-done.17.refs_0_ = bf16[128,3072]{1,0:T(8,128)(2,1)S(1)} collective-permute-done((bf16[128,3072]{1,0:T(8,128)(2,1)S(1)}, bf16[128,3072]{1,0:T(8,128)(2,1)S(1)}, u32[]{:S(2)}, u32[]{:S(2)}) %collective-permute-start.17) | collective-permute-done | bytes 786464 | tf_op jit(solution)/shard_map/ppermute | solution.py:425
  70.5 1.4 %shard_map.155 = (bf16[128,3072]{1,0:T(8,128)(2,1)S(1)}, f32[32,128]{1,0:T(8,128)S(1)}, f32[32,128]{1,0:T(8,128)S(1)}) custom-call(s32[1,256]{1,0:T(1,128)S(1)} %get-tuple-element.30.refs_0_.mask_ref, f32[128,3072]{1,0:T(8,128)S(1)} %shard_map.154.own_ref, bf16[128,3072]{1,0:T(8,128)(2,1)S(1)} %collective-permute-done.17.refs_0_, ...), custom_call_target="tpu_custom_call" | custom-call | tf_op jit(solution)/shard_map/pallas_call | solution.py:312
  71.9 1.6 %collective-permute-start.18 = (f32[32,128]{1,0:T(8,128)S(1)}, f32[32,128]{1,0:T(8,128)S(1)}, u32[]{:S(2)}, u32[]{:S(2)}) collective-permute-start(f32[32,128]{1,0:T(8,128)S(1)} %get-tuple-element.53), channel_id=1, source_target_pairs={{0,16},{16,0},{1,17},{17,1},{2,18},{18,2},{3,19},{19,3},{4,20},{20... | collective-permute-start | bytes 49160 | tf_op jit(solution)/shard_map/ppermute | solution.py:440
  73.5 0.9 %shard_map.156 = bf16[128,3072]{1,0:T(8,128)(2,1)} custom-call(bf16[128,3072]{1,0:T(8,128)(2,1)S(1)} %get-tuple-element.51.block_ref), custom_call_target="tpu_custom_call" | custom-call | tf_op jit(solution)/shard_map/pallas_call | solution.py:312
  74.3 1.3 %collective-permute-done.18.partner_ref = f32[32,128]{1,0:T(8,128)S(1)} collective-permute-done((f32[32,128]{1,0:T(8,128)S(1)}, f32[32,128]{1,0:T(8,128)S(1)}, u32[]{:S(2)}, u32[]{:S(2)}) %collective-permute-start.18) | collective-permute-done | bytes 16416 | tf_op jit(solution)/shard_map/ppermute | solution.py:440
  75.7 0.6 shard_map.157
  (8 shorter events, 0.0 us)
Async XLA Ops:
  2.2 28.8 %collective-permute-start = (bf16[512,384]{1,0:T(8,128)(2,1)S(1)}, bf16[512,384]{1,0:T(8,128)(2,1)S(1)}, u32[]{:S(2)}, u32[]{:S(2)}) collective-permute-start(bf16[512,384]{1,0:T(8,128)(2,1)S(1)} %get-tuple-element.33), channel_id=1, source_target_pairs={{0,2},{2,0},{4,6},{6,4},{8,10},{10,8},{12,14},{14,12},{1,3},{3,1},... | collective-permute-start | bytes 1179656 | tf_op jit(solution)/shard_map/ppermute | solution.py:336
  5.3 27.7 %collective-permute-start.1 = (bf16[512,384]{1,0:T(8,128)(2,1)S(1)}, bf16[512,384]{1,0:T(8,128)(2,1)S(1)}, u32[]{:S(2)}, u32[]{:S(2)}) collective-permute-start(bf16[512,384]{1,0:T(8,128)(2,1)S(1)} %get-tuple-element.34), channel_id=1, source_target_pairs={{0,4},{2,6},{4,0},{6,2},{8,12},{10,14},{12,8},{14,10},{1,5},{3,7},... | collective-permute-start | bytes 1179656 | tf_op jit(solution)/shard_map/ppermute | solution.py:336
  6.8 27.1 %collective-permute-start.2 = (bf16[512,384]{1,0:T(8,128)(2,1)S(1)}, bf16[512,384]{1,0:T(8,128)(2,1)S(1)}, u32[]{:S(2)}, u32[]{:S(2)}) collective-permute-start(bf16[512,384]{1,0:T(8,128)(2,1)S(1)} %get-tuple-element.35), channel_id=1, source_target_pairs={{0,6},{2,4},{4,2},{6,0},{8,14},{10,12},{12,10},{14,8},{1,7},{3,5},... | collective-permute-start | bytes 1179656 | tf_op jit(solution)/shard_map/ppermute | solution.py:336
  9.0 17.5 %collective-permute-start.4 = (bf16[128,384]{1,0:T(8,128)(2,1)S(1)}, bf16[128,384]{1,0:T(8,128)(2,1)S(1)}, u32[]{:S(2)}, u32[]{:S(2)}) collective-permute-start(bf16[128,384]{1,0:T(8,128)(2,1)S(1)} %get-tuple-element.37), channel_id=1, source_target_pairs={{0,10},{2,8},{4,14},{6,12},{8,2},{10,0},{12,6},{14,4},{1,11},{3,9}... | collective-permute-start | bytes 294920 | tf_op jit(solution)/shard_map/ppermute | solution.py:354
  13.0 16.4 %collective-permute-start.3 = (bf16[128,384]{1,0:T(8,128)(2,1)S(1)}, bf16[128,384]{1,0:T(8,128)(2,1)S(1)}, u32[]{:S(2)}, u32[]{:S(2)}) collective-permute-start(bf16[128,384]{1,0:T(8,128)(2,1)S(1)} %get-tuple-element.29.refs_9_), channel_id=1, source_target_pairs={{0,8},{2,10},{4,12},{6,14},{8,0},{10,2},{12,4},{14,6},{1,9},{3,11}... | collective-permute-start | bytes 294920 | tf_op jit(solution)/shard_map/ppermute | solution.py:354
  26.5 15.5 %collective-permute-start.5 = (bf16[128,384]{1,0:T(8,128)(2,1)S(1)}, bf16[128,384]{1,0:T(8,128)(2,1)S(1)}, u32[]{:S(2)}, u32[]{:S(2)}) collective-permute-start(bf16[128,384]{1,0:T(8,128)(2,1)S(1)} %get-tuple-element.38), channel_id=1, source_target_pairs={{0,12},{2,14},{4,8},{6,10},{8,4},{10,6},{12,0},{14,2},{1,13},{3,15... | collective-permute-start | bytes 294920 | tf_op jit(solution)/shard_map/ppermute | solution.py:354
  29.3 13.7 %collective-permute-start.6 = (bf16[128,384]{1,0:T(8,128)(2,1)S(1)}, bf16[128,384]{1,0:T(8,128)(2,1)S(1)}, u32[]{:S(2)}, u32[]{:S(2)}) collective-permute-start(bf16[128,384]{1,0:T(8,128)(2,1)S(1)} %get-tuple-element.39), channel_id=1, source_target_pairs={{0,14},{2,12},{4,10},{6,8},{8,6},{10,4},{12,2},{14,0},{1,15},{3,13... | collective-permute-start | bytes 294920 | tf_op jit(solution)/shard_map/ppermute | solution.py:354
  31.0 13.1 %collective-permute-start.7 = (bf16[128,384]{1,0:T(8,128)(2,1)S(1)}, bf16[128,384]{1,0:T(8,128)(2,1)S(1)}, u32[]{:S(2)}, u32[]{:S(2)}) collective-permute-start(bf16[128,384]{1,0:T(8,128)(2,1)S(1)} %get-tuple-element.37), channel_id=1, source_target_pairs={{0,2},{2,0},{4,6},{6,4},{8,10},{10,8},{12,14},{14,12},{1,3},{3,1},... | collective-permute-start | bytes 294920 | tf_op jit(solution)/shard_map/ppermute | solution.py:355
  33.0 11.2 %collective-permute-start.8 = (bf16[128,384]{1,0:T(8,128)(2,1)S(1)}, bf16[128,384]{1,0:T(8,128)(2,1)S(1)}, u32[]{:S(2)}, u32[]{:S(2)}) collective-permute-start(bf16[128,384]{1,0:T(8,128)(2,1)S(1)} %get-tuple-element.38), channel_id=1, source_target_pairs={{0,4},{2,6},{4,0},{6,2},{8,12},{10,14},{12,8},{14,10},{1,5},{3,7},... | collective-permute-start | bytes 294920 | tf_op jit(solution)/shard_map/ppermute | solution.py:355
  33.9 10.3 %collective-permute-start.9 = (bf16[128,384]{1,0:T(8,128)(2,1)S(1)}, bf16[128,384]{1,0:T(8,128)(2,1)S(1)}, u32[]{:S(2)}, u32[]{:S(2)}) collective-permute-start(bf16[128,384]{1,0:T(8,128)(2,1)S(1)} %get-tuple-element.39), channel_id=1, source_target_pairs={{0,6},{2,4},{4,2},{6,0},{8,14},{10,12},{12,10},{14,8},{1,7},{3,5},... | collective-permute-start | bytes 294920 | tf_op jit(solution)/shard_map/ppermute | solution.py:355
  46.3 8.4 %collective-permute-start.11 = (bf16[400,128]{1,0:T(8,128)(2,1)S(1)}, bf16[400,128]{1,0:T(8,128)(2,1)S(1)}, u32[]{:S(2)}, u32[]{:S(2)}) collective-permute-start(bf16[400,128]{1,0:T(8,128)(2,1)S(1)} %get-tuple-element.41), channel_id=1, source_target_pairs={{4,0},{6,2},{0,4},{2,6},{12,8},{14,10},{8,12},{10,14},{5,1},{7,3},... | collective-permute-start | bytes 307208 | tf_op jit(solution)/shard_map/ppermute | solution.py:414
  48.3 7.3 %collective-permute-start.12 = (bf16[400,128]{1,0:T(8,128)(2,1)S(1)}, bf16[400,128]{1,0:T(8,128)(2,1)S(1)}, u32[]{:S(2)}, u32[]{:S(2)}) collective-permute-start(bf16[400,128]{1,0:T(8,128)(2,1)S(1)} %get-tuple-element.42), channel_id=1, source_target_pairs={{6,0},{4,2},{2,4},{0,6},{14,8},{12,10},{10,12},{8,14},{7,1},{5,3},... | collective-permute-start | bytes 307208 | tf_op jit(solution)/shard_map/ppermute | solution.py:414
  49.3 9.6 %collective-permute-start.16 = (bf16[400,128]{1,0:T(8,128)(2,1)S(1)}, bf16[400,128]{1,0:T(8,128)(2,1)S(1)}, u32[]{:S(2)}, u32[]{:S(2)}) collective-permute-start(bf16[400,128]{1,0:T(8,128)(2,1)S(1)} %shard_map.150.refs_0_), channel_id=1, source_target_pairs={{14,0},{12,2},{10,4},{8,6},{6,8},{4,10},{2,12},{0,14},{15,1},{13,3... | collective-permute-start | bytes 307208 | tf_op jit(solution)/shard_map/ppermute | solution.py:409
  51.3 7.7 %collective-permute-start.15 = (bf16[400,128]{1,0:T(8,128)(2,1)S(1)}, bf16[400,128]{1,0:T(8,128)(2,1)S(1)}, u32[]{:S(2)}, u32[]{:S(2)}) collective-permute-start(bf16[400,128]{1,0:T(8,128)(2,1)S(1)} %shard_map.149.refs_0_), channel_id=1, source_target_pairs={{12,0},{14,2},{8,4},{10,6},{4,8},{6,10},{0,12},{2,14},{13,1},{15,3... | collective-permute-start | bytes 307208 | tf_op jit(solution)/shard_map/ppermute | solution.py:409
  53.1 5.9 %collective-permute-start.10 = (bf16[400,128]{1,0:T(8,128)(2,1)S(1)}, bf16[400,128]{1,0:T(8,128)(2,1)S(1)}, u32[]{:S(2)}, u32[]{:S(2)}) collective-permute-start(bf16[400,128]{1,0:T(8,128)(2,1)S(1)} %get-tuple-element.40.refs_0_), channel_id=1, source_target_pairs={{2,0},{0,2},{6,4},{4,6},{10,8},{8,10},{14,12},{12,14},{3,1},{1,3},... | collective-permute-start | bytes 307208 | tf_op jit(solution)/shard_map/ppermute | solution.py:414
  54.6 11.2 %collective-permute-start.14 = (bf16[400,128]{1,0:T(8,128)(2,1)S(1)}, bf16[400,128]{1,0:T(8,128)(2,1)S(1)}, u32[]{:S(2)}, u32[]{:S(2)}) collective-permute-start(bf16[400,128]{1,0:T(8,128)(2,1)S(1)} %shard_map.148.refs_0_), channel_id=1, source_target_pairs={{10,0},{8,2},{14,4},{12,6},{2,8},{0,10},{6,12},{4,14},{11,1},{9,3}... | collective-permute-start | bytes 307208 | tf_op jit(solution)/shard_map/ppermute | solution.py:409
  55.6 10.5 %collective-permute-start.13 = (bf16[400,128]{1,0:T(8,128)(2,1)S(1)}, bf16[400,128]{1,0:T(8,128)(2,1)S(1)}, u32[]{:S(2)}, u32[]{:S(2)}) collective-permute-start(bf16[400,128]{1,0:T(8,128)(2,1)S(1)} %shard_map.147.refs_0_), channel_id=1, source_target_pairs={{8,0},{10,2},{12,4},{14,6},{0,8},{2,10},{4,12},{6,14},{9,1},{11,3}... | collective-permute-start | bytes 307208 | tf_op jit(solution)/shard_map/ppermute | solution.py:409
  68.1 2.4 %collective-permute-start.17 = (bf16[128,3072]{1,0:T(8,128)(2,1)S(1)}, bf16[128,3072]{1,0:T(8,128)(2,1)S(1)}, u32[]{:S(2)}, u32[]{:S(2)}) collective-permute-start(bf16[128,3072]{1,0:T(8,128)(2,1)S(1)} %get-tuple-element.44), channel_id=1, source_target_pairs={{0,1},{1,0},{2,3},{3,2},{4,5},{5,4},{6,7},{7,6},{8,9},{9,8},{10,11... | collective-permute-start | bytes 2359304 | tf_op jit(solution)/shard_map/ppermute | solution.py:425
  71.9 3.8 %collective-permute-start.18 = (f32[32,128]{1,0:T(8,128)S(1)}, f32[32,128]{1,0:T(8,128)S(1)}, u32[]{:S(2)}, u32[]{:S(2)}) collective-permute-start(f32[32,128]{1,0:T(8,128)S(1)} %get-tuple-element.53), channel_id=1, source_target_pairs={{0,16},{16,0},{1,17},{17,1},{2,18},{18,2},{3,19},{19,3},{4,20},{20... | collective-permute-start | bytes 49160 | tf_op jit(solution)/shard_map/ppermute | solution.py:440

commit v5 on v4

--- a/solution.py
+++ b/solution.py
@@ -145,12 +145,12 @@
     members, partial, own_heads, depth, live_count, count, stat_rows, sources = dims
     pairs, units = refs[1 : members + 1], refs[members + 1 : 2 * members + 1]
     asks = refs[2 * members + 1 : 2 * members + 1 + sources]
-    outs, stats = refs[2 * members + 1 + sources : -1], refs[-1]
+    outs = refs[2 * members + 1 + sources :]
     factor = depth ** (-0.5)
     power = factor * math.log2(math.e)
-    lanes = lax.broadcasted_iota(jnp.int32, (live_count, stats.shape[2]), 1)
-    if partial:
-        stats[...] = jnp.zeros_like(stats)
+    lanes = lax.broadcasted_iota(jnp.int32, (live_count, depth), 1)
+    padded = -(-own_heads // 8) * 8
+    stats = [jnp.zeros((live_count, depth), jnp.float32)] * sources
     ones = jnp.ones((count, depth), jnp.bfloat16)
     for h in range(own_heads):
         columns = slice(h * depth, (h + 1) * depth)
@@ -166,18 +166,20 @@
                     for w, ref in zip(weights, pairs)
                 ],
             )
-            totals = summed[:, depth : depth + 1]
+            totals = summed[:, depth:]
             outs[s][pl.ds(h * live_count, live_count), :] = (summed[:, :depth] / totals).astype(jnp.bfloat16)
-            if partial:
-                rest = biggest * factor + jnp.log(totals)
-                for piece in range(3):
-                    rounded = rest.astype(jnp.bfloat16).astype(jnp.float32)
-                    stats[s] = jnp.where(lanes == piece * own_heads + h, rounded, stats[s])
-                    rest = rest - rounded
+            stats[s] = jnp.where(lanes == h, biggest, jnp.where(lanes == padded + h, totals, stats[s]))
     if partial:
+        blank = jnp.zeros((stat_rows - 3 * own_heads, live_count), jnp.float32)
         for s in range(sources):
-            turned = jnp.transpose(stats[s])[:stat_rows]
-            outs[s][pl.ds(own_heads * live_count, stat_rows), :] = turned.astype(jnp.bfloat16)
+            turned = jnp.transpose(stats[s])
+            rest = turned[:own_heads] * factor + jnp.log(turned[padded : padded + own_heads])
+            pieces = []
+            for _ in range(3):
+                pieces.append(rest.astype(jnp.bfloat16).astype(jnp.float32))
+                rest = rest - pieces[-1]
+            stat = jnp.concatenate([*pieces, blank], axis=0)
+            outs[s][pl.ds(own_heads * live_count, stat_rows), :] = stat.astype(jnp.bfloat16)
 
 
 def merge_kernel(dims, places_ref, weight_ref, *refs):
@@ -223,26 +225,27 @@
         out_ref[:, columns] = dot_f32(rows, weight_ref[:, columns]).astype(out_ref.dtype)
 
 
-def project_kernel(rows_ref, weight_ref, out_ref):
-    project(rows_ref[...], weight_ref, out_ref)
+def project_kernel(rows_ref, weight_ref, input_ref, gate_ref, out_ref):
+    features = weight_ref.shape[1]
+    tile = 512 if features % 512 == 0 else features
+    for first in range(0, features, tile):
+        columns = pl.ds(first, tile)
+        product = dot_f32(rows_ref[...], weight_ref[:, columns])
+        out_ref[:, columns] = input_ref[:, columns].astype(jnp.float32) + gate_ref[:, columns] * product
 
 
 def tail_kernel(parts, mask_ref, own_ref, *refs):
     arrived = refs[: parts - 1]
-    input_ref, cached_ref, gate_ref, shift_ref, scale_ref, patch_ref, block_ref, kept_ref, given_ref = refs[
-        parts - 1 :
-    ]
-    projected = own_ref[...]
-    for ref in arrived:
-        projected = projected + ref[...].astype(jnp.float32)
-    share = projected.shape[0]
+    cached_ref, gate_ref, shift_ref, scale_ref, patch_ref, block_ref, kept_ref, given_ref = refs[parts - 1 :]
+    others = functools.reduce(jnp.add, [ref[...].astype(jnp.float32) for ref in arrived])
+    mixed = own_ref[...] + gate_ref[...] * others
+    share = mixed.shape[0]
     count = mask_ref.shape[1]
     first = lax.axis_index("tp") * share
     rows = lax.broadcasted_iota(jnp.int32, (share, count), 0) + first
     cols = lax.broadcasted_iota(jnp.int32, (share, count), 1)
     replayed = jnp.where((cols == rows) & (jnp.broadcast_to(mask_ref[...], rows.shape) == 1), 1.0, 0.0)
     replayed = jnp.sum(replayed, axis=-1, keepdims=True) > 0.5
-    mixed = input_ref[...].astype(jnp.float32) + gate_ref[...] * projected
     block = jnp.where(replayed, cached_ref[...].astype(jnp.float32), mixed).astype(jnp.bfloat16)
     block_ref[...] = block
     lifted = block.astype(jnp.float32)
@@ -398,7 +401,6 @@
             ),
             (after, *pairs, *units, *asks),
             [parcel_shape] * len(asks),
-            scratch=[pltpu.VMEM((len(asks), live_count, live_count), f32)],
             cost=pl.CostEstimate(flops=4 * scores * depth, transcendentals=scores, bytes_accessed=1 << 20),
         )
 
@@ -426,7 +428,7 @@
     ]
     (own,) = call(
         project_kernel,
-        (merged[-1], weight),
+        (merged[-1], weight, inputs_here, gate),
         [shaped((share, features), f32)],
         cost=pl.CostEstimate(flops=2 * share * width * features, transcendentals=0, bytes_accessed=1 << 20),
     )
@@ -434,7 +436,7 @@
     half = channels // 2
     block_out, kept, given = call(
         functools.partial(tail_kernel, parts),
-        (mask, own, *arrived, inputs_here, cached_here, gate, shift, scale, patch),
+        (mask, own, *arrived, cached_here, gate, shift, scale, patch),
         [shaped((share, features), bf16), shaped((half, share), f32), shaped((half, share), f32)],
     )
     partner = lax.ppermute(given, "cfg", [(0, 1), (1, 0)])

time: 76.5 us -> 76 us (level)
  no operation moved by 1% of the time
where the time goes in v5:
time: 76 us; the launch traced here: 75.8 us
  starting transfers between devices  30.5 us (40%)
  waiting for transfers between devices  22.8 us (30%)
  Pallas kernels  21.7 us (29%)
  between operations  0.78 us (1%)
    pallas_call x18, Pallas kernels, call(): pl.pallas_call(kernel, out_shape=outs, in_specs=in_specs or [VMEM] * len(...  21.7 us
    ppermute x4, waiting for transfers between devices, shards(): far_asks.append(lax.ppermute(asks[b], 'ctx', route(a, b, False)))  13.2 us
    ppermute x4, starting transfers between devices, shards(): far_asks.append(lax.ppermute(asks[b], 'ctx', route(a, b, False)))  8.86 us
    ppermute x4, waiting for transfers between devices, shards(): lax.ppermute(far, 'ctx', route(*far_routes[n], True))  7.15 us
    ppermute x4, starting transfers between devices, shards(): lax.ppermute(far, 'ctx', route(*far_routes[n], True))  6.9 us
    ppermute x3, starting transfers between devices, shards(): parcels[0, b] = lax.ppermute(near[b - 1], 'ctx', route(0, b, True))  4.65 us
    ppermute x3, starting transfers between devices, shards(): pairs[b] = lax.ppermute(pairs[b], 'ctx', route(0, b, False))  4.64 us
    ppermute x3, starting transfers between devices, shards(): lax.ppermute(asks[b], 'ctx', route(0, b, False))  3.84 us
  transfers between devices with their start and end apart: 19, of which 6 were waited for; matrix products, arithmetic and copies ran while one was open for 0% of the time, Pallas kernels for 19%

profile of v5, /device:TPU:0, one launch (start us, length us, event | category | flops | bytes accessed | tf_op | source)
XLA Modules:
  0.0 75.8 jit_solution(4480870715029630534)
XLA Ops:
  0.6 1.6 %shard_map.140 = (bf16[512,384]{1,0:T(8,128)(2,1)S(1)}, bf16[512,384]{1,0:T(8,128)(2,1)S(1)}, bf16[512,384]{1,0:T(8,128)(2,1)S(1)}, bf16[512,384]{1,0:T(8,128)(2,1)S(1)}) custom-call(bf16[256,1536]{1,0:T(8,128)(2,1)} %bitcast.12, bf16[256,1536]{1,0:T(8,128)(2,1)} %bitcast.13), custom_call_target="tpu_custom_call" | custom-call | tf_op jit(solution)/shard_map/pallas_call | solution.py:315
  2.2 3.1 %collective-permute-start = (bf16[512,384]{1,0:T(8,128)(2,1)S(1)}, bf16[512,384]{1,0:T(8,128)(2,1)S(1)}, u32[]{:S(2)}, u32[]{:S(2)}) collective-permute-start(bf16[512,384]{1,0:T(8,128)(2,1)S(1)} %get-tuple-element.33), channel_id=1, source_target_pairs={{0,2},{2,0},{4,6},{6,4},{8,10},{10,8},{12,14},{14,12},{1,3},{3,1},... | collective-permute-start | bytes 1179656 | tf_op jit(solution)/shard_map/ppermute | solution.py:339
  5.3 1.6 %collective-permute-start.1 = (bf16[512,384]{1,0:T(8,128)(2,1)S(1)}, bf16[512,384]{1,0:T(8,128)(2,1)S(1)}, u32[]{:S(2)}, u32[]{:S(2)}) collective-permute-start(bf16[512,384]{1,0:T(8,128)(2,1)S(1)} %get-tuple-element.34), channel_id=1, source_target_pairs={{0,4},{2,6},{4,0},{6,2},{8,12},{10,14},{12,8},{14,10},{1,5},{3,7},... | collective-permute-start | bytes 1179656 | tf_op jit(solution)/shard_map/ppermute | solution.py:339
  6.8 0.0 collective-permute-start.2
  6.8 2.1 %shard_map.141 = (bf16[128,384]{1,0:T(8,128)(2,1)S(1)}, bf16[128,384]{1,0:T(8,128)(2,1)S(1)}, bf16[128,384]{1,0:T(8,128)(2,1)S(1)}, bf16[128,384]{1,0:T(8,128)(2,1)S(1)}) custom-call(s32[1,256]{1,0:T(1,128)} %refs_0_.1, f32[1,128]{1,0:T(1,128)} %bitcast.18, bf16[256,1536]{1,0:T(8,128)(2,1)} %bitcast.14, ...), custom_call_target="tpu_custom_call" | custom-call | tf_op jit(solution)/shard_map/pallas_call | solution.py:315
  9.0 4.0 %collective-permute-start.4 = (bf16[128,384]{1,0:T(8,128)(2,1)S(1)}, bf16[128,384]{1,0:T(8,128)(2,1)S(1)}, u32[]{:S(2)}, u32[]{:S(2)}) collective-permute-start(bf16[128,384]{1,0:T(8,128)(2,1)S(1)} %get-tuple-element.37), channel_id=1, source_target_pairs={{0,10},{2,8},{4,14},{6,12},{8,2},{10,0},{12,6},{14,4},{1,11},{3,9}... | collective-permute-start | bytes 294920 | tf_op jit(solution)/shard_map/ppermute | solution.py:357
  13.0 0.3 collective-permute-start.3
  13.3 13.2 %collective-permute-done.4.refs_9_ = bf16[128,384]{1,0:T(8,128)(2,1)S(1)} collective-permute-done((bf16[128,384]{1,0:T(8,128)(2,1)S(1)}, bf16[128,384]{1,0:T(8,128)(2,1)S(1)}, u32[]{:S(2)}, u32[]{:S(2)}) %collective-permute-start.4) | collective-permute-done | bytes 98336 | tf_op jit(solution)/shard_map/ppermute | solution.py:357
  26.5 2.8 %collective-permute-start.5 = (bf16[128,384]{1,0:T(8,128)(2,1)S(1)}, bf16[128,384]{1,0:T(8,128)(2,1)S(1)}, u32[]{:S(2)}, u32[]{:S(2)}) collective-permute-start(bf16[128,384]{1,0:T(8,128)(2,1)S(1)} %get-tuple-element.38), channel_id=1, source_target_pairs={{0,12},{2,14},{4,8},{6,10},{8,4},{10,6},{12,0},{14,2},{1,13},{3,15... | collective-permute-start | bytes 294920 | tf_op jit(solution)/shard_map/ppermute | solution.py:357
  29.3 1.7 %collective-permute-start.6 = (bf16[128,384]{1,0:T(8,128)(2,1)S(1)}, bf16[128,384]{1,0:T(8,128)(2,1)S(1)}, u32[]{:S(2)}, u32[]{:S(2)}) collective-permute-start(bf16[128,384]{1,0:T(8,128)(2,1)S(1)} %get-tuple-element.39), channel_id=1, source_target_pairs={{0,14},{2,12},{4,10},{6,8},{8,6},{10,4},{12,2},{14,0},{1,15},{3,13... | collective-permute-start | bytes 294920 | tf_op jit(solution)/shard_map/ppermute | solution.py:357
  31.0 0.0 collective-permute-done.pair_ref.refs_2_
  31.0 1.9 %collective-permute-start.7 = (bf16[128,384]{1,0:T(8,128)(2,1)S(1)}, bf16[128,384]{1,0:T(8,128)(2,1)S(1)}, u32[]{:S(2)}, u32[]{:S(2)}) collective-permute-start(bf16[128,384]{1,0:T(8,128)(2,1)S(1)} %get-tuple-element.37), channel_id=1, source_target_pairs={{0,2},{2,0},{4,6},{6,4},{8,10},{10,8},{12,14},{14,12},{1,3},{3,1},... | collective-permute-start | bytes 294920 | tf_op jit(solution)/shard_map/ppermute | solution.py:358
  33.0 0.9 %collective-permute-start.8 = (bf16[128,384]{1,0:T(8,128)(2,1)S(1)}, bf16[128,384]{1,0:T(8,128)(2,1)S(1)}, u32[]{:S(2)}, u32[]{:S(2)}) collective-permute-start(bf16[128,384]{1,0:T(8,128)(2,1)S(1)} %get-tuple-element.38), channel_id=1, source_target_pairs={{0,4},{2,6},{4,0},{6,2},{8,12},{10,14},{12,8},{14,10},{1,5},{3,7},... | collective-permute-start | bytes 294920 | tf_op jit(solution)/shard_map/ppermute | solution.py:358
  33.9 0.0 collective-permute-done.2.pair_ref.refs_4_
  33.9 1.0 %collective-permute-start.9 = (bf16[128,384]{1,0:T(8,128)(2,1)S(1)}, bf16[128,384]{1,0:T(8,128)(2,1)S(1)}, u32[]{:S(2)}, u32[]{:S(2)}) collective-permute-start(bf16[128,384]{1,0:T(8,128)(2,1)S(1)} %get-tuple-element.39), channel_id=1, source_target_pairs={{0,6},{2,4},{4,2},{6,0},{8,14},{10,12},{12,10},{14,8},{1,7},{3,5},... | collective-permute-start | bytes 294920 | tf_op jit(solution)/shard_map/ppermute | solution.py:358
  34.9 4.3 %shard_map.142 = (s32[1,256]{1,0:T(1,128)S(1)}, f32[1,128]{1,0:T(1,128)S(1)}, bf16[1536,3072]{1,0:T(8,128)(2,1)S(1)}, bf16[128,3072]{1,0:T(8,128)(2,1)S(1)}, bf1...) custom-call(s32[1,256]{1,0:T(1,128)} %refs_0_.1, ...), custom_call_target="tpu_custom_call" | custom-call | bytes 22883328 | tf_op jit(solution)/shard_map/pallas_call | solution.py:315
  39.2 0.2 shard_map.143.refs_5_
  39.4 0.2 shard_map.146.refs_8_
  39.6 0.2 shard_map.145.refs_7_
  39.8 0.2 shard_map.144.refs_6_
  40.0 1.0 %shard_map.147.refs_0_ = bf16[400,128]{1,0:T(8,128)(2,1)S(1)} custom-call(s32[1,256]{1,0:T(1,128)S(1)} %get-tuple-element.30.refs_0_.mask_ref, bf16[512,384]{1,0:T(8,128)(2,1)S(1)} %get-tuple-element.28.refs_0_.pair_ref.refs_1_, bf16[512,384]{1,0:T(8,128)(2,1)S(1)} %collective-permute-done.pair_ref.refs_2_, ...), custom_call_target="tpu_custom_call" | custom-call | flops 201326592 | bytes 1048576 | tf_op jit(solution)/shard_map/pallas_call | solution.py:315
  40.9 1.0 %shard_map.148.refs_0_ = bf16[400,128]{1,0:T(8,128)(2,1)S(1)} custom-call(bf16[400,128]{1,0:T(8,128)(2,1)S(1)} %shard_map.147.refs_0_, bf16[512,384]{1,0:T(8,128)(2,1)S(1)} %get-tuple-element.28.refs_0_.pair_ref.refs_1_, bf16[512,384]{1,0:T(8,128)(2,1)S(1)} %collective-permute-done.pair_ref.refs_2_, ...), custom_call_target="tpu_custom_call" | custom-call | flops 201326592 | bytes 1048576 | tf_op jit(solution)/shard_map/pallas_call | solution.py:315
  41.9 0.0 collective-permute-done.5.refs_9_
  41.9 1.0 %shard_map.149.refs_0_ = bf16[400,128]{1,0:T(8,128)(2,1)S(1)} custom-call(bf16[400,128]{1,0:T(8,128)(2,1)S(1)} %shard_map.148.refs_0_, bf16[512,384]{1,0:T(8,128)(2,1)S(1)} %get-tuple-element.28.refs_0_.pair_ref.refs_1_, bf16[512,384]{1,0:T(8,128)(2,1)S(1)} %collective-permute-done.pair_ref.refs_2_, ...), custom_call_target="tpu_custom_call" | custom-call | flops 201326592 | bytes 1048576 | tf_op jit(solution)/shard_map/pallas_call | solution.py:315
  42.9 0.0 collective-permute-done.6.refs_9_
  42.9 1.0 %shard_map.150.refs_0_ = bf16[400,128]{1,0:T(8,128)(2,1)S(1)} custom-call(bf16[400,128]{1,0:T(8,128)(2,1)S(1)} %shard_map.149.refs_0_, bf16[512,384]{1,0:T(8,128)(2,1)S(1)} %get-tuple-element.28.refs_0_.pair_ref.refs_1_, bf16[512,384]{1,0:T(8,128)(2,1)S(1)} %collective-permute-done.pair_ref.refs_2_, ...), custom_call_target="tpu_custom_call" | custom-call | flops 201326592 | bytes 1048576 | tf_op jit(solution)/shard_map/pallas_call | solution.py:315
  43.8 0.0 collective-permute-done.9.refs_11_
  43.9 2.0 %shard_map.151 = (bf16[400,128]{1,0:T(8,128)(2,1)S(1)}, bf16[400,128]{1,0:T(8,128)(2,1)S(1)}, bf16[400,128]{1,0:T(8,128)(2,1)S(1)}) custom-call(bf16[400,128]{1,0:T(8,128)(2,1)S(1)} %shard_map.150.refs_0_, bf16[512,384]{1,0:T(8,128)(2,1)S(1)} %get-tuple-element.28.refs_0_.pair_ref.refs_1_, bf16[512,384]{1,0:T(8,128)(2,1)S(1)} %collective-permute-done.pair_ref.refs_2_, ...), custom_call_target="tpu_custom_call" | custom-call | flops 603979776 | bytes 1048576 | tf_op jit(solution)/shard_map/pallas_call | solution.py:315
  45.8 2.0 %collective-permute-start.11 = (bf16[400,128]{1,0:T(8,128)(2,1)S(1)}, bf16[400,128]{1,0:T(8,128)(2,1)S(1)}, u32[]{:S(2)}, u32[]{:S(2)}) collective-permute-start(bf16[400,128]{1,0:T(8,128)(2,1)S(1)} %get-tuple-element.41), channel_id=1, source_target_pairs={{4,0},{6,2},{0,4},{2,6},{12,8},{14,10},{8,12},{10,14},{5,1},{7,3},... | collective-permute-start | bytes 307208 | tf_op jit(solution)/shard_map/ppermute | solution.py:416
  47.8 1.1 %collective-permute-start.12 = (bf16[400,128]{1,0:T(8,128)(2,1)S(1)}, bf16[400,128]{1,0:T(8,128)(2,1)S(1)}, u32[]{:S(2)}, u32[]{:S(2)}) collective-permute-start(bf16[400,128]{1,0:T(8,128)(2,1)S(1)} %get-tuple-element.42), channel_id=1, source_target_pairs={{6,0},{4,2},{2,4},{0,6},{14,8},{12,10},{10,12},{8,14},{7,1},{5,3},... | collective-permute-start | bytes 307208 | tf_op jit(solution)/shard_map/ppermute | solution.py:416
  48.9 2.0 %collective-permute-start.16 = (bf16[400,128]{1,0:T(8,128)(2,1)S(1)}, bf16[400,128]{1,0:T(8,128)(2,1)S(1)}, u32[]{:S(2)}, u32[]{:S(2)}) collective-permute-start(bf16[400,128]{1,0:T(8,128)(2,1)S(1)} %shard_map.150.refs_0_), channel_id=1, source_target_pairs={{14,0},{12,2},{10,4},{8,6},{6,8},{4,10},{2,12},{0,14},{15,1},{13,3... | collective-permute-start | bytes 307208 | tf_op jit(solution)/shard_map/ppermute | solution.py:411
  50.9 1.7 %collective-permute-start.15 = (bf16[400,128]{1,0:T(8,128)(2,1)S(1)}, bf16[400,128]{1,0:T(8,128)(2,1)S(1)}, u32[]{:S(2)}, u32[]{:S(2)}) collective-permute-start(bf16[400,128]{1,0:T(8,128)(2,1)S(1)} %shard_map.149.refs_0_), channel_id=1, source_target_pairs={{12,0},{14,2},{8,4},{10,6},{4,8},{6,10},{0,12},{2,14},{13,1},{15,3... | collective-permute-start | bytes 307208 | tf_op jit(solution)/shard_map/ppermute | solution.py:411
  52.6 1.6 %collective-permute-start.10 = (bf16[400,128]{1,0:T(8,128)(2,1)S(1)}, bf16[400,128]{1,0:T(8,128)(2,1)S(1)}, u32[]{:S(2)}, u32[]{:S(2)}) collective-permute-start(bf16[400,128]{1,0:T(8,128)(2,1)S(1)} %get-tuple-element.40.refs_0_), channel_id=1, source_target_pairs={{2,0},{0,2},{6,4},{4,6},{10,8},{8,10},{14,12},{12,14},{3,1},{1,3},... | collective-permute-start | bytes 307208 | tf_op jit(solution)/shard_map/ppermute | solution.py:416
  54.2 1.0 %collective-permute-start.14 = (bf16[400,128]{1,0:T(8,128)(2,1)S(1)}, bf16[400,128]{1,0:T(8,128)(2,1)S(1)}, u32[]{:S(2)}, u32[]{:S(2)}) collective-permute-start(bf16[400,128]{1,0:T(8,128)(2,1)S(1)} %shard_map.148.refs_0_), channel_id=1, source_target_pairs={{10,0},{8,2},{14,4},{12,6},{2,8},{0,10},{6,12},{4,14},{11,1},{9,3}... | collective-permute-start | bytes 307208 | tf_op jit(solution)/shard_map/ppermute | solution.py:411
  55.2 2.2 %collective-permute-start.13 = (bf16[400,128]{1,0:T(8,128)(2,1)S(1)}, bf16[400,128]{1,0:T(8,128)(2,1)S(1)}, u32[]{:S(2)}, u32[]{:S(2)}) collective-permute-start(bf16[400,128]{1,0:T(8,128)(2,1)S(1)} %shard_map.147.refs_0_), channel_id=1, source_target_pairs={{8,0},{10,2},{12,4},{14,6},{0,8},{2,10},{4,12},{6,14},{9,1},{11,3}... | collective-permute-start | bytes 307208 | tf_op jit(solution)/shard_map/ppermute | solution.py:411
  57.4 1.0 %shard_map.152.refs_0_ = bf16[400,128]{1,0:T(8,128)(2,1)S(1)} custom-call(bf16[400,128]{1,0:T(8,128)(2,1)S(1)} %get-tuple-element.40.refs_0_, bf16[512,384]{1,0:T(8,128)(2,1)S(1)} %get-tuple-element.28.refs_0_.pair_ref.refs_1_, bf16[512,384]{1,0:T(8,128)(2,1)S(1)} %collective-permute-done.pair_ref.refs_2_, ...), custom_call_target="tpu_custom_call" | custom-call | flops 201326592 | bytes 1048576 | tf_op jit(solution)/shard_map/pallas_call | solution.py:315
  58.3 0.2 collective-permute-done.10.refs_1_
  58.6 6.8 %collective-permute-done.14.refs_5_ = bf16[400,128]{1,0:T(8,128)(2,1)S(1)} collective-permute-done((bf16[400,128]{1,0:T(8,128)(2,1)S(1)}, bf16[400,128]{1,0:T(8,128)(2,1)S(1)}, u32[]{:S(2)}, u32[]{:S(2)}) %collective-permute-start.14) | collective-permute-done | bytes 102432 | tf_op jit(solution)/shard_map/ppermute | solution.py:411
  65.4 0.3 collective-permute-done.13.refs_4_
  65.7 2.0 %shard_map.153 = (bf16[128,3072]{1,0:T(8,128)(2,1)S(1)}, bf16[128,1536]{1,0:T(8,128)(2,1)S(1)}) custom-call(bf16[2,128,128]{2,1,0:T(8,128)(2,1)S(1)} %get-tuple-element.31.places_ref, bf16[1536,3072]{1,0:T(8,128)(2,1)S(1)} %get-tuple-element.32.weight_ref, bf16[400,128]{1,0:T(8,128)(2,1)S(1)} %shard_map.152.refs_0_, ...), custom_call_target="tpu_custom_call" | custom-call | tf_op jit(solution)/shard_map/pallas_call | solution.py:315
  67.7 0.1 collective-permute-start.17
  67.8 1.4 %shard_map.154.own_ref = f32[128,3072]{1,0:T(8,128)S(1)} custom-call(bf16[128,1536]{1,0:T(8,128)(2,1)S(1)} %get-tuple-element.43.rows_ref, bf16[1536,3072]{1,0:T(8,128)(2,1)S(1)} %get-tuple-element.32.weight_ref, bf16[128,3072]{1,0:T(8,128)(2,1)S(1)} %get-tuple-element.44.input_ref, f32[1,3072]{1,0:T(1,128)S(1)} %get-tuple-element.45.gate_ref.refs_2_), custom_call_target="tpu_custom_call" | custom-call | flops 1207959552 | bytes 1048576 | tf_op jit(solution)/shard_map/pallas_call | solution.py:315
  69.2 0.9 %collective-permute-done.17.refs_0_ = bf16[128,3072]{1,0:T(8,128)(2,1)S(1)} collective-permute-done((bf16[128,3072]{1,0:T(8,128)(2,1)S(1)}, bf16[128,3072]{1,0:T(8,128)(2,1)S(1)}, u32[]{:S(2)}, u32[]{:S(2)}) %collective-permute-start.17) | collective-permute-done | bytes 786464 | tf_op jit(solution)/shard_map/ppermute | solution.py:427
  70.1 1.3 %shard_map.155 = (bf16[128,3072]{1,0:T(8,128)(2,1)S(1)}, f32[32,128]{1,0:T(8,128)S(1)}, f32[32,128]{1,0:T(8,128)S(1)}) custom-call(s32[1,256]{1,0:T(1,128)S(1)} %get-tuple-element.30.refs_0_.mask_ref, f32[128,3072]{1,0:T(8,128)S(1)} %shard_map.154.own_ref, bf16[128,3072]{1,0:T(8,128)(2,1)S(1)} %collective-permute-done.17.refs_0_, ...), custom_call_target="tpu_custom_call" | custom-call | tf_op jit(solution)/shard_map/pallas_call | solution.py:315
  71.4 1.6 %collective-permute-start.18 = (f32[32,128]{1,0:T(8,128)S(1)}, f32[32,128]{1,0:T(8,128)S(1)}, u32[]{:S(2)}, u32[]{:S(2)}) collective-permute-start(f32[32,128]{1,0:T(8,128)S(1)} %get-tuple-element.53), channel_id=1, source_target_pairs={{0,16},{16,0},{1,17},{17,1},{2,18},{18,2},{3,19},{19,3},{4,20},{20... | collective-permute-start | bytes 49160 | tf_op jit(solution)/shard_map/ppermute | solution.py:442
  72.9 0.9 %shard_map.156 = bf16[128,3072]{1,0:T(8,128)(2,1)} custom-call(bf16[128,3072]{1,0:T(8,128)(2,1)S(1)} %get-tuple-element.51.block_ref), custom_call_target="tpu_custom_call" | custom-call | tf_op jit(solution)/shard_map/pallas_call | solution.py:315
  73.8 1.4 %collective-permute-done.18.partner_ref = f32[32,128]{1,0:T(8,128)S(1)} collective-permute-done((f32[32,128]{1,0:T(8,128)S(1)}, f32[32,128]{1,0:T(8,128)S(1)}, u32[]{:S(2)}, u32[]{:S(2)}) %collective-permute-start.18) | collective-permute-done | bytes 16416 | tf_op jit(solution)/shard_map/ppermute | solution.py:442
  75.2 0.6 shard_map.157
  (8 shorter events, 0.0 us)
Async XLA Ops:
  2.2 28.8 %collective-permute-start = (bf16[512,384]{1,0:T(8,128)(2,1)S(1)}, bf16[512,384]{1,0:T(8,128)(2,1)S(1)}, u32[]{:S(2)}, u32[]{:S(2)}) collective-permute-start(bf16[512,384]{1,0:T(8,128)(2,1)S(1)} %get-tuple-element.33), channel_id=1, source_target_pairs={{0,2},{2,0},{4,6},{6,4},{8,10},{10,8},{12,14},{14,12},{1,3},{3,1},... | collective-permute-start | bytes 1179656 | tf_op jit(solution)/shard_map/ppermute | solution.py:339
  5.3 27.7 %collective-permute-start.1 = (bf16[512,384]{1,0:T(8,128)(2,1)S(1)}, bf16[512,384]{1,0:T(8,128)(2,1)S(1)}, u32[]{:S(2)}, u32[]{:S(2)}) collective-permute-start(bf16[512,384]{1,0:T(8,128)(2,1)S(1)} %get-tuple-element.34), channel_id=1, source_target_pairs={{0,4},{2,6},{4,0},{6,2},{8,12},{10,14},{12,8},{14,10},{1,5},{3,7},... | collective-permute-start | bytes 1179656 | tf_op jit(solution)/shard_map/ppermute | solution.py:339
  6.8 27.1 %collective-permute-start.2 = (bf16[512,384]{1,0:T(8,128)(2,1)S(1)}, bf16[512,384]{1,0:T(8,128)(2,1)S(1)}, u32[]{:S(2)}, u32[]{:S(2)}) collective-permute-start(bf16[512,384]{1,0:T(8,128)(2,1)S(1)} %get-tuple-element.35), channel_id=1, source_target_pairs={{0,6},{2,4},{4,2},{6,0},{8,14},{10,12},{12,10},{14,8},{1,7},{3,5},... | collective-permute-start | bytes 1179656 | tf_op jit(solution)/shard_map/ppermute | solution.py:339
  9.0 17.5 %collective-permute-start.4 = (bf16[128,384]{1,0:T(8,128)(2,1)S(1)}, bf16[128,384]{1,0:T(8,128)(2,1)S(1)}, u32[]{:S(2)}, u32[]{:S(2)}) collective-permute-start(bf16[128,384]{1,0:T(8,128)(2,1)S(1)} %get-tuple-element.37), channel_id=1, source_target_pairs={{0,10},{2,8},{4,14},{6,12},{8,2},{10,0},{12,6},{14,4},{1,11},{3,9}... | collective-permute-start | bytes 294920 | tf_op jit(solution)/shard_map/ppermute | solution.py:357
  13.0 16.4 %collective-permute-start.3 = (bf16[128,384]{1,0:T(8,128)(2,1)S(1)}, bf16[128,384]{1,0:T(8,128)(2,1)S(1)}, u32[]{:S(2)}, u32[]{:S(2)}) collective-permute-start(bf16[128,384]{1,0:T(8,128)(2,1)S(1)} %get-tuple-element.29.refs_9_), channel_id=1, source_target_pairs={{0,8},{2,10},{4,12},{6,14},{8,0},{10,2},{12,4},{14,6},{1,9},{3,11}... | collective-permute-start | bytes 294920 | tf_op jit(solution)/shard_map/ppermute | solution.py:357
  26.5 15.4 %collective-permute-start.5 = (bf16[128,384]{1,0:T(8,128)(2,1)S(1)}, bf16[128,384]{1,0:T(8,128)(2,1)S(1)}, u32[]{:S(2)}, u32[]{:S(2)}) collective-permute-start(bf16[128,384]{1,0:T(8,128)(2,1)S(1)} %get-tuple-element.38), channel_id=1, source_target_pairs={{0,12},{2,14},{4,8},{6,10},{8,4},{10,6},{12,0},{14,2},{1,13},{3,15... | collective-permute-start | bytes 294920 | tf_op jit(solution)/shard_map/ppermute | solution.py:357
  29.3 13.5 %collective-permute-start.6 = (bf16[128,384]{1,0:T(8,128)(2,1)S(1)}, bf16[128,384]{1,0:T(8,128)(2,1)S(1)}, u32[]{:S(2)}, u32[]{:S(2)}) collective-permute-start(bf16[128,384]{1,0:T(8,128)(2,1)S(1)} %get-tuple-element.39), channel_id=1, source_target_pairs={{0,14},{2,12},{4,10},{6,8},{8,6},{10,4},{12,2},{14,0},{1,15},{3,13... | collective-permute-start | bytes 294920 | tf_op jit(solution)/shard_map/ppermute | solution.py:357
  31.0 12.8 %collective-permute-start.7 = (bf16[128,384]{1,0:T(8,128)(2,1)S(1)}, bf16[128,384]{1,0:T(8,128)(2,1)S(1)}, u32[]{:S(2)}, u32[]{:S(2)}) collective-permute-start(bf16[128,384]{1,0:T(8,128)(2,1)S(1)} %get-tuple-element.37), channel_id=1, source_target_pairs={{0,2},{2,0},{4,6},{6,4},{8,10},{10,8},{12,14},{14,12},{1,3},{3,1},... | collective-permute-start | bytes 294920 | tf_op jit(solution)/shard_map/ppermute | solution.py:358
  33.0 10.9 %collective-permute-start.8 = (bf16[128,384]{1,0:T(8,128)(2,1)S(1)}, bf16[128,384]{1,0:T(8,128)(2,1)S(1)}, u32[]{:S(2)}, u32[]{:S(2)}) collective-permute-start(bf16[128,384]{1,0:T(8,128)(2,1)S(1)} %get-tuple-element.38), channel_id=1, source_target_pairs={{0,4},{2,6},{4,0},{6,2},{8,12},{10,14},{12,8},{14,10},{1,5},{3,7},... | collective-permute-start | bytes 294920 | tf_op jit(solution)/shard_map/ppermute | solution.py:358
  33.9 10.0 %collective-permute-start.9 = (bf16[128,384]{1,0:T(8,128)(2,1)S(1)}, bf16[128,384]{1,0:T(8,128)(2,1)S(1)}, u32[]{:S(2)}, u32[]{:S(2)}) collective-permute-start(bf16[128,384]{1,0:T(8,128)(2,1)S(1)} %get-tuple-element.39), channel_id=1, source_target_pairs={{0,6},{2,4},{4,2},{6,0},{8,14},{10,12},{12,10},{14,8},{1,7},{3,5},... | collective-permute-start | bytes 294920 | tf_op jit(solution)/shard_map/ppermute | solution.py:358
  45.8 8.4 %collective-permute-start.11 = (bf16[400,128]{1,0:T(8,128)(2,1)S(1)}, bf16[400,128]{1,0:T(8,128)(2,1)S(1)}, u32[]{:S(2)}, u32[]{:S(2)}) collective-permute-start(bf16[400,128]{1,0:T(8,128)(2,1)S(1)} %get-tuple-element.41), channel_id=1, source_target_pairs={{4,0},{6,2},{0,4},{2,6},{12,8},{14,10},{8,12},{10,14},{5,1},{7,3},... | collective-permute-start | bytes 307208 | tf_op jit(solution)/shard_map/ppermute | solution.py:416
  47.8 7.3 %collective-permute-start.12 = (bf16[400,128]{1,0:T(8,128)(2,1)S(1)}, bf16[400,128]{1,0:T(8,128)(2,1)S(1)}, u32[]{:S(2)}, u32[]{:S(2)}) collective-permute-start(bf16[400,128]{1,0:T(8,128)(2,1)S(1)} %get-tuple-element.42), channel_id=1, source_target_pairs={{6,0},{4,2},{2,4},{0,6},{14,8},{12,10},{10,12},{8,14},{7,1},{5,3},... | collective-permute-start | bytes 307208 | tf_op jit(solution)/shard_map/ppermute | solution.py:416
  48.9 9.6 %collective-permute-start.16 = (bf16[400,128]{1,0:T(8,128)(2,1)S(1)}, bf16[400,128]{1,0:T(8,128)(2,1)S(1)}, u32[]{:S(2)}, u32[]{:S(2)}) collective-permute-start(bf16[400,128]{1,0:T(8,128)(2,1)S(1)} %shard_map.150.refs_0_), channel_id=1, source_target_pairs={{14,0},{12,2},{10,4},{8,6},{6,8},{4,10},{2,12},{0,14},{15,1},{13,3... | collective-permute-start | bytes 307208 | tf_op jit(solution)/shard_map/ppermute | solution.py:411
  50.9 7.7 %collective-permute-start.15 = (bf16[400,128]{1,0:T(8,128)(2,1)S(1)}, bf16[400,128]{1,0:T(8,128)(2,1)S(1)}, u32[]{:S(2)}, u32[]{:S(2)}) collective-permute-start(bf16[400,128]{1,0:T(8,128)(2,1)S(1)} %shard_map.149.refs_0_), channel_id=1, source_target_pairs={{12,0},{14,2},{8,4},{10,6},{4,8},{6,10},{0,12},{2,14},{13,1},{15,3... | collective-permute-start | bytes 307208 | tf_op jit(solution)/shard_map/ppermute | solution.py:411
  52.6 5.9 %collective-permute-start.10 = (bf16[400,128]{1,0:T(8,128)(2,1)S(1)}, bf16[400,128]{1,0:T(8,128)(2,1)S(1)}, u32[]{:S(2)}, u32[]{:S(2)}) collective-permute-start(bf16[400,128]{1,0:T(8,128)(2,1)S(1)} %get-tuple-element.40.refs_0_), channel_id=1, source_target_pairs={{2,0},{0,2},{6,4},{4,6},{10,8},{8,10},{14,12},{12,14},{3,1},{1,3},... | collective-permute-start | bytes 307208 | tf_op jit(solution)/shard_map/ppermute | solution.py:416
  54.2 11.2 %collective-permute-start.14 = (bf16[400,128]{1,0:T(8,128)(2,1)S(1)}, bf16[400,128]{1,0:T(8,128)(2,1)S(1)}, u32[]{:S(2)}, u32[]{:S(2)}) collective-permute-start(bf16[400,128]{1,0:T(8,128)(2,1)S(1)} %shard_map.148.refs_0_), channel_id=1, source_target_pairs={{10,0},{8,2},{14,4},{12,6},{2,8},{0,10},{6,12},{4,14},{11,1},{9,3}... | collective-permute-start | bytes 307208 | tf_op jit(solution)/shard_map/ppermute | solution.py:411
  55.2 10.5 %collective-permute-start.13 = (bf16[400,128]{1,0:T(8,128)(2,1)S(1)}, bf16[400,128]{1,0:T(8,128)(2,1)S(1)}, u32[]{:S(2)}, u32[]{:S(2)}) collective-permute-start(bf16[400,128]{1,0:T(8,128)(2,1)S(1)} %shard_map.147.refs_0_), channel_id=1, source_target_pairs={{8,0},{10,2},{12,4},{14,6},{0,8},{2,10},{4,12},{6,14},{9,1},{11,3}... | collective-permute-start | bytes 307208 | tf_op jit(solution)/shard_map/ppermute | solution.py:411
  67.7 2.4 %collective-permute-start.17 = (bf16[128,3072]{1,0:T(8,128)(2,1)S(1)}, bf16[128,3072]{1,0:T(8,128)(2,1)S(1)}, u32[]{:S(2)}, u32[]{:S(2)}) collective-permute-start(bf16[128,3072]{1,0:T(8,128)(2,1)S(1)} %get-tuple-element.46), channel_id=1, source_target_pairs={{0,1},{1,0},{2,3},{3,2},{4,5},{5,4},{6,7},{7,6},{8,9},{9,8},{10,11... | collective-permute-start | bytes 2359304 | tf_op jit(solution)/shard_map/ppermute | solution.py:427
  71.4 3.8 %collective-permute-start.18 = (f32[32,128]{1,0:T(8,128)S(1)}, f32[32,128]{1,0:T(8,128)S(1)}, u32[]{:S(2)}, u32[]{:S(2)}) collective-permute-start(f32[32,128]{1,0:T(8,128)S(1)} %get-tuple-element.53), channel_id=1, source_target_pairs={{0,16},{16,0},{1,17},{17,1},{2,18},{18,2},{3,19},{19,3},{4,20},{20... | collective-permute-start | bytes 49160 | tf_op jit(solution)/shard_map/ppermute | solution.py:442

commit v6 on v5

--- a/solution.py
+++ b/solution.py
@@ -182,16 +182,10 @@
             outs[s][pl.ds(own_heads * live_count, stat_rows), :] = stat.astype(jnp.bfloat16)
 
 
-def merge_kernel(dims, places_ref, weight_ref, *refs):
-    members, groups, own_heads, depth, live_count, stat_rows, parts = dims
-    sources = members * groups
-    parcels = refs[:sources]
-    sends = refs[sources : sources + parts - 1]
-    own_ref, spread_ref = refs[sources + parts - 1 :]
-    share = own_ref.shape[0]
+def merge_rows(dims, places, parcels, spread_ref):
+    members, groups, own_heads, depth, live_count, stat_rows, _ = dims
     width = own_heads * depth
     position = ring_place(members)
-    places = jnp.concatenate([places_ref[s] for s in range(parts)], axis=0)
     for b in range(members):
         held = [parcels[a * members + b] for a in range(groups)]
         if groups > 1:
@@ -212,9 +206,17 @@
                 placed = dot_f32(places, values[0])
             base = hop(position, b, members) * width + h * depth
             spread_ref[:, pl.ds(pl.multiple_of(base, depth), depth)] = placed.astype(jnp.bfloat16)
-    own_ref[...] = spread_ref[pl.ds(0, share), :]
-    for s in range(1, parts):
-        project(spread_ref[pl.ds(s * share, share), :], weight_ref, sends[s - 1])
+
+
+def merge_kernel(dims, places_ref, weight_ref, *refs):
+    members, groups, *_, parts = dims
+    sources = members * groups
+    parcels, sends, spread_ref = refs[:sources], refs[sources:-1], refs[-1]
+    share = places_ref.shape[1]
+    places = jnp.concatenate([places_ref[s] for s in range(1, parts)], axis=0)
+    merge_rows(dims, places, parcels, spread_ref)
+    for s, send in enumerate(sends):
+        project(spread_ref[pl.ds(s * share, share), :], weight_ref, send)
 
 
 def project(rows, weight_ref, out_ref):
@@ -225,12 +227,14 @@
         out_ref[:, columns] = dot_f32(rows, weight_ref[:, columns]).astype(out_ref.dtype)
 
 
-def project_kernel(rows_ref, weight_ref, input_ref, gate_ref, out_ref):
+def own_kernel(dims, after_ref, places_ref, weight_ref, input_ref, gate_ref, *refs):
+    parcels, out_ref, spread_ref = refs[:-2], refs[-2], refs[-1]
+    merge_rows(dims, places_ref[0], parcels, spread_ref)
     features = weight_ref.shape[1]
     tile = 512 if features % 512 == 0 else features
     for first in range(0, features, tile):
         columns = pl.ds(first, tile)
-        product = dot_f32(rows_ref[...], weight_ref[:, columns])
+        product = dot_f32(spread_ref[...], weight_ref[:, columns])
         out_ref[:, columns] = input_ref[:, columns].astype(jnp.float32) + gate_ref[:, columns] * product
 
 
@@ -334,7 +338,7 @@
         limit=8,
     )
     pairs = list(pairs)
-    pair_order = sorted(range(1, members), key=lambda b: (b < members // 2, b))
+    pair_order = sorted(range(1, members), key=lambda b: (b != members // 2, b))
     for b in pair_order:
         pairs[b] = lax.ppermute(pairs[b], "ctx", route(0, b, False))
     asks = call(
@@ -351,7 +355,7 @@
         ],
         limit=16,
     )
-    far_routes = [(a, b) for a in range(1, groups) for b in range(members)]
+    far_routes = sorted(((a, b) for a in range(1, groups) for b in range(members)), key=lambda r: (r[0], (1 - r[1] if r[1] < 2 else r[1])))
     far_asks = []
     for a, b in far_routes:
         far_asks.append(lax.ppermute(asks[b], "ctx", route(a, b, False)))
@@ -417,19 +421,21 @@
     (parcels[0, 0],) = attend(after, near_asks[:1])
     parcels = [parcels[a, b] for a in range(groups) for b in range(members)]
 
+    dims = (members, groups, own_heads, depth, live_count, stat_rows, parts)
     merged = call(
-        functools.partial(merge_kernel, (members, groups, own_heads, depth, live_count, stat_rows, parts)),
+        functools.partial(merge_kernel, dims),
         (places, weight, *parcels),
-        [shaped((share, features), bf16)] * (parts - 1) + [shaped((share, width), bf16)],
-        scratch=[pltpu.VMEM((count, width), bf16)],
+        [shaped((share, features), bf16)] * (parts - 1),
+        scratch=[pltpu.VMEM(((parts - 1) * share, width), bf16)],
     )
     arrived = [
         lax.ppermute(merged[s - 1], "tp", [(i, (i + s) % parts) for i in range(parts)]) for s in range(1, parts)
     ]
     (own,) = call(
-        project_kernel,
-        (merged[-1], weight, inputs_here, gate),
+        functools.partial(own_kernel, dims),
+        (merged[0], places, weight, inputs_here, gate, *parcels),
         [shaped((share, features), f32)],
+        scratch=[pltpu.VMEM((share, width), bf16)],
         cost=pl.CostEstimate(flops=2 * share * width * features, transcendentals=0, bytes_accessed=1 << 20),
     )
 

time: 76 us -> 76.5 us (level)
    ppermute x4, waiting for transfers between devices: 7.15 us -> 8.31 us  [shards(): lax.ppermute(far, 'ctx', route(*far_routes[n], True))]
  transfers between devices with their start and end apart: 19 -> 19, of which waited for: 6 -> 7; matrix products, arithmetic and copies ran while one was open for 0% -> 0% of each run, Pallas kernels for 19% -> 19%
where the time goes in v6:
time: 76.5 us; the launch traced here: 76.3 us
  starting transfers between devices  30.3 us (40%)
  waiting for transfers between devices  23.2 us (30%)
  Pallas kernels  22 us (29%)
  between operations  0.79 us (1%)
    pallas_call x18, Pallas kernels, call(): pl.pallas_call(kernel, out_shape=outs, in_specs=in_specs or [VMEM] * len(...  22 us
    ppermute x4, waiting for transfers between devices, shards(): far_asks.append(lax.ppermute(asks[b], 'ctx', route(a, b, False)))  13.2 us
    ppermute x4, starting transfers between devices, shards(): far_asks.append(lax.ppermute(asks[b], 'ctx', route(a, b, False)))  8.86 us
    ppermute x4, waiting for transfers between devices, shards(): lax.ppermute(far, 'ctx', route(*far_routes[n], True))  8.31 us
    ppermute x4, starting transfers between devices, shards(): lax.ppermute(far, 'ctx', route(*far_routes[n], True))  6.67 us
    ppermute x3, starting transfers between devices, shards(): parcels[0, b] = lax.ppermute(near[b - 1], 'ctx', route(0, b, True))  4.65 us
    ppermute x3, starting transfers between devices, shards(): pairs[b] = lax.ppermute(pairs[b], 'ctx', route(0, b, False))  4.64 us
    ppermute x3, starting transfers between devices, shards(): lax.ppermute(asks[b], 'ctx', route(0, b, False))  3.84 us
  transfers between devices with their start and end apart: 19, of which 7 were waited for; matrix products, arithmetic and copies ran while one was open for 0% of the time, Pallas kernels for 19%

profile of v6, /device:TPU:0, one launch (start us, length us, event | category | flops | bytes accessed | tf_op | source)
XLA Modules:
  0.0 76.3 jit_solution(14499055529130163076)
XLA Ops:
  0.6 1.6 %shard_map.140 = (bf16[512,384]{1,0:T(8,128)(2,1)S(1)}, bf16[512,384]{1,0:T(8,128)(2,1)S(1)}, bf16[512,384]{1,0:T(8,128)(2,1)S(1)}, bf16[512,384]{1,0:T(8,128)(2,1)S(1)}) custom-call(bf16[256,1536]{1,0:T(8,128)(2,1)} %bitcast.12, bf16[256,1536]{1,0:T(8,128)(2,1)} %bitcast.13), custom_call_target="tpu_custom_call" | custom-call | tf_op jit(solution)/shard_map/pallas_call | solution.py:319
  2.2 3.1 %collective-permute-start = (bf16[512,384]{1,0:T(8,128)(2,1)S(1)}, bf16[512,384]{1,0:T(8,128)(2,1)S(1)}, u32[]{:S(2)}, u32[]{:S(2)}) collective-permute-start(bf16[512,384]{1,0:T(8,128)(2,1)S(1)} %get-tuple-element.31), channel_id=1, source_target_pairs={{0,2},{2,0},{4,6},{6,4},{8,10},{10,8},{12,14},{14,12},{1,3},{3,1},... | collective-permute-start | bytes 1179656 | tf_op jit(solution)/shard_map/ppermute | solution.py:343
  5.3 1.6 %collective-permute-start.1 = (bf16[512,384]{1,0:T(8,128)(2,1)S(1)}, bf16[512,384]{1,0:T(8,128)(2,1)S(1)}, u32[]{:S(2)}, u32[]{:S(2)}) collective-permute-start(bf16[512,384]{1,0:T(8,128)(2,1)S(1)} %get-tuple-element.32), channel_id=1, source_target_pairs={{0,4},{2,6},{4,0},{6,2},{8,12},{10,14},{12,8},{14,10},{1,5},{3,7},... | collective-permute-start | bytes 1179656 | tf_op jit(solution)/shard_map/ppermute | solution.py:343
  6.8 0.0 collective-permute-start.2
  6.8 2.1 %shard_map.141 = (bf16[128,384]{1,0:T(8,128)(2,1)S(1)}, bf16[128,384]{1,0:T(8,128)(2,1)S(1)}, bf16[128,384]{1,0:T(8,128)(2,1)S(1)}, bf16[128,384]{1,0:T(8,128)(2,1)S(1)}) custom-call(s32[1,256]{1,0:T(1,128)} %refs_0_.1, f32[1,128]{1,0:T(1,128)} %bitcast.18, bf16[256,1536]{1,0:T(8,128)(2,1)} %bitcast.14, ...), custom_call_target="tpu_custom_call" | custom-call | tf_op jit(solution)/shard_map/pallas_call | solution.py:319
  9.0 4.0 %collective-permute-start.3 = (bf16[128,384]{1,0:T(8,128)(2,1)S(1)}, bf16[128,384]{1,0:T(8,128)(2,1)S(1)}, u32[]{:S(2)}, u32[]{:S(2)}) collective-permute-start(bf16[128,384]{1,0:T(8,128)(2,1)S(1)} %get-tuple-element.35), channel_id=1, source_target_pairs={{0,10},{2,8},{4,14},{6,12},{8,2},{10,0},{12,6},{14,4},{1,11},{3,9}... | collective-permute-start | bytes 294920 | tf_op jit(solution)/shard_map/ppermute | solution.py:361
  13.0 0.3 collective-permute-start.4
  13.3 13.2 %collective-permute-done.3.refs_9_ = bf16[128,384]{1,0:T(8,128)(2,1)S(1)} collective-permute-done((bf16[128,384]{1,0:T(8,128)(2,1)S(1)}, bf16[128,384]{1,0:T(8,128)(2,1)S(1)}, u32[]{:S(2)}, u32[]{:S(2)}) %collective-permute-start.3) | collective-permute-done | bytes 98336 | tf_op jit(solution)/shard_map/ppermute | solution.py:361
  26.5 2.8 %collective-permute-start.5 = (bf16[128,384]{1,0:T(8,128)(2,1)S(1)}, bf16[128,384]{1,0:T(8,128)(2,1)S(1)}, u32[]{:S(2)}, u32[]{:S(2)}) collective-permute-start(bf16[128,384]{1,0:T(8,128)(2,1)S(1)} %get-tuple-element.36), channel_id=1, source_target_pairs={{0,12},{2,14},{4,8},{6,10},{8,4},{10,6},{12,0},{14,2},{1,13},{3,15... | collective-permute-start | bytes 294920 | tf_op jit(solution)/shard_map/ppermute | solution.py:361
  29.3 1.7 %collective-permute-start.6 = (bf16[128,384]{1,0:T(8,128)(2,1)S(1)}, bf16[128,384]{1,0:T(8,128)(2,1)S(1)}, u32[]{:S(2)}, u32[]{:S(2)}) collective-permute-start(bf16[128,384]{1,0:T(8,128)(2,1)S(1)} %get-tuple-element.37), channel_id=1, source_target_pairs={{0,14},{2,12},{4,10},{6,8},{8,6},{10,4},{12,2},{14,0},{1,15},{3,13... | collective-permute-start | bytes 294920 | tf_op jit(solution)/shard_map/ppermute | solution.py:361
  31.0 0.0 collective-permute-done.pair_ref.refs_2_
  31.0 1.9 %collective-permute-start.7 = (bf16[128,384]{1,0:T(8,128)(2,1)S(1)}, bf16[128,384]{1,0:T(8,128)(2,1)S(1)}, u32[]{:S(2)}, u32[]{:S(2)}) collective-permute-start(bf16[128,384]{1,0:T(8,128)(2,1)S(1)} %get-tuple-element.35), channel_id=1, source_target_pairs={{0,2},{2,0},{4,6},{6,4},{8,10},{10,8},{12,14},{14,12},{1,3},{3,1},... | collective-permute-start | bytes 294920 | tf_op jit(solution)/shard_map/ppermute | solution.py:362
  33.0 0.9 %collective-permute-start.8 = (bf16[128,384]{1,0:T(8,128)(2,1)S(1)}, bf16[128,384]{1,0:T(8,128)(2,1)S(1)}, u32[]{:S(2)}, u32[]{:S(2)}) collective-permute-start(bf16[128,384]{1,0:T(8,128)(2,1)S(1)} %get-tuple-element.36), channel_id=1, source_target_pairs={{0,4},{2,6},{4,0},{6,2},{8,12},{10,14},{12,8},{14,10},{1,5},{3,7},... | collective-permute-start | bytes 294920 | tf_op jit(solution)/shard_map/ppermute | solution.py:362
  33.9 0.0 collective-permute-done.2.pair_ref.refs_4_
  33.9 1.0 %collective-permute-start.9 = (bf16[128,384]{1,0:T(8,128)(2,1)S(1)}, bf16[128,384]{1,0:T(8,128)(2,1)S(1)}, u32[]{:S(2)}, u32[]{:S(2)}) collective-permute-start(bf16[128,384]{1,0:T(8,128)(2,1)S(1)} %get-tuple-element.37), channel_id=1, source_target_pairs={{0,6},{2,4},{4,2},{6,0},{8,14},{10,12},{12,10},{14,8},{1,7},{3,5},... | collective-permute-start | bytes 294920 | tf_op jit(solution)/shard_map/ppermute | solution.py:362
  34.9 4.3 %shard_map.142 = (s32[1,256]{1,0:T(1,128)S(1)}, f32[1,128]{1,0:T(1,128)S(1)}, bf16[1536,3072]{1,0:T(8,128)(2,1)S(1)}, bf16[128,3072]{1,0:T(8,128)(2,1)S(1)}, bf1...) custom-call(s32[1,256]{1,0:T(1,128)} %refs_0_.1, ...), custom_call_target="tpu_custom_call" | custom-call | bytes 22883328 | tf_op jit(solution)/shard_map/pallas_call | solution.py:319
  39.2 0.2 shard_map.143.refs_5_
  39.4 0.2 shard_map.146.refs_8_
  39.6 0.2 shard_map.145.refs_7_
  39.8 0.2 shard_map.144.refs_6_
  40.0 1.0 %shard_map.147.refs_0_ = bf16[400,128]{1,0:T(8,128)(2,1)S(1)} custom-call(s32[1,256]{1,0:T(1,128)S(1)} %get-tuple-element.28.refs_0_.mask_ref, bf16[512,384]{1,0:T(8,128)(2,1)S(1)} %get-tuple-element.26.refs_0_.pair_ref.refs_1_, bf16[512,384]{1,0:T(8,128)(2,1)S(1)} %collective-permute-done.pair_ref.refs_2_, ...), custom_call_target="tpu_custom_call" | custom-call | flops 201326592 | bytes 1048576 | tf_op jit(solution)/shard_map/pallas_call | solution.py:319
  40.9 1.0 %shard_map.148.refs_0_ = bf16[400,128]{1,0:T(8,128)(2,1)S(1)} custom-call(bf16[400,128]{1,0:T(8,128)(2,1)S(1)} %shard_map.147.refs_0_, bf16[512,384]{1,0:T(8,128)(2,1)S(1)} %get-tuple-element.26.refs_0_.pair_ref.refs_1_, bf16[512,384]{1,0:T(8,128)(2,1)S(1)} %collective-permute-done.pair_ref.refs_2_, ...), custom_call_target="tpu_custom_call" | custom-call | flops 201326592 | bytes 1048576 | tf_op jit(solution)/shard_map/pallas_call | solution.py:319
  41.9 1.0 %shard_map.149.refs_0_ = bf16[400,128]{1,0:T(8,128)(2,1)S(1)} custom-call(bf16[400,128]{1,0:T(8,128)(2,1)S(1)} %shard_map.148.refs_0_, bf16[512,384]{1,0:T(8,128)(2,1)S(1)} %get-tuple-element.26.refs_0_.pair_ref.refs_1_, bf16[512,384]{1,0:T(8,128)(2,1)S(1)} %collective-permute-done.pair_ref.refs_2_, ...), custom_call_target="tpu_custom_call" | custom-call | flops 201326592 | bytes 1048576 | tf_op jit(solution)/shard_map/pallas_call | solution.py:319
  42.9 1.0 %shard_map.150.refs_0_ = bf16[400,128]{1,0:T(8,128)(2,1)S(1)} custom-call(bf16[400,128]{1,0:T(8,128)(2,1)S(1)} %shard_map.149.refs_0_, bf16[512,384]{1,0:T(8,128)(2,1)S(1)} %get-tuple-element.26.refs_0_.pair_ref.refs_1_, bf16[512,384]{1,0:T(8,128)(2,1)S(1)} %collective-permute-done.pair_ref.refs_2_, ...), custom_call_target="tpu_custom_call" | custom-call | flops 201326592 | bytes 1048576 | tf_op jit(solution)/shard_map/pallas_call | solution.py:319
  43.8 0.0 collective-permute-done.7.refs_9_
  43.8 0.0 collective-permute-done.8.refs_10_
  43.9 2.0 %shard_map.151 = (bf16[400,128]{1,0:T(8,128)(2,1)S(1)}, bf16[400,128]{1,0:T(8,128)(2,1)S(1)}, bf16[400,128]{1,0:T(8,128)(2,1)S(1)}) custom-call(bf16[400,128]{1,0:T(8,128)(2,1)S(1)} %shard_map.150.refs_0_, bf16[512,384]{1,0:T(8,128)(2,1)S(1)} %get-tuple-element.26.refs_0_.pair_ref.refs_1_, bf16[512,384]{1,0:T(8,128)(2,1)S(1)} %collective-permute-done.pair_ref.refs_2_, ...), custom_call_target="tpu_custom_call" | custom-call | flops 603979776 | bytes 1048576 | tf_op jit(solution)/shard_map/pallas_call | solution.py:319
  45.8 2.0 %collective-permute-start.11 = (bf16[400,128]{1,0:T(8,128)(2,1)S(1)}, bf16[400,128]{1,0:T(8,128)(2,1)S(1)}, u32[]{:S(2)}, u32[]{:S(2)}) collective-permute-start(bf16[400,128]{1,0:T(8,128)(2,1)S(1)} %get-tuple-element.39), channel_id=1, source_target_pairs={{4,0},{6,2},{0,4},{2,6},{12,8},{14,10},{8,12},{10,14},{5,1},{7,3},... | collective-permute-start | bytes 307208 | tf_op jit(solution)/shard_map/ppermute | solution.py:420
  47.8 1.1 %collective-permute-start.12 = (bf16[400,128]{1,0:T(8,128)(2,1)S(1)}, bf16[400,128]{1,0:T(8,128)(2,1)S(1)}, u32[]{:S(2)}, u32[]{:S(2)}) collective-permute-start(bf16[400,128]{1,0:T(8,128)(2,1)S(1)} %get-tuple-element.40), channel_id=1, source_target_pairs={{6,0},{4,2},{2,4},{0,6},{14,8},{12,10},{10,12},{8,14},{7,1},{5,3},... | collective-permute-start | bytes 307208 | tf_op jit(solution)/shard_map/ppermute | solution.py:420
  48.9 2.0 %collective-permute-start.16 = (bf16[400,128]{1,0:T(8,128)(2,1)S(1)}, bf16[400,128]{1,0:T(8,128)(2,1)S(1)}, u32[]{:S(2)}, u32[]{:S(2)}) collective-permute-start(bf16[400,128]{1,0:T(8,128)(2,1)S(1)} %shard_map.150.refs_0_), channel_id=1, source_target_pairs={{14,0},{12,2},{10,4},{8,6},{6,8},{4,10},{2,12},{0,14},{15,1},{13,3... | collective-permute-start | bytes 307208 | tf_op jit(solution)/shard_map/ppermute | solution.py:415
  50.9 1.7 %collective-permute-start.15 = (bf16[400,128]{1,0:T(8,128)(2,1)S(1)}, bf16[400,128]{1,0:T(8,128)(2,1)S(1)}, u32[]{:S(2)}, u32[]{:S(2)}) collective-permute-start(bf16[400,128]{1,0:T(8,128)(2,1)S(1)} %shard_map.149.refs_0_), channel_id=1, source_target_pairs={{12,0},{14,2},{8,4},{10,6},{4,8},{6,10},{0,12},{2,14},{13,1},{15,3... | collective-permute-start | bytes 307208 | tf_op jit(solution)/shard_map/ppermute | solution.py:415
  52.6 1.6 %collective-permute-start.10 = (bf16[400,128]{1,0:T(8,128)(2,1)S(1)}, bf16[400,128]{1,0:T(8,128)(2,1)S(1)}, u32[]{:S(2)}, u32[]{:S(2)}) collective-permute-start(bf16[400,128]{1,0:T(8,128)(2,1)S(1)} %get-tuple-element.38.refs_0_), channel_id=1, source_target_pairs={{2,0},{0,2},{6,4},{4,6},{10,8},{8,10},{14,12},{12,14},{3,1},{1,3},... | collective-permute-start | bytes 307208 | tf_op jit(solution)/shard_map/ppermute | solution.py:420
  54.2 0.7 collective-permute-start.13
  54.9 2.2 %collective-permute-start.14 = (bf16[400,128]{1,0:T(8,128)(2,1)S(1)}, bf16[400,128]{1,0:T(8,128)(2,1)S(1)}, u32[]{:S(2)}, u32[]{:S(2)}) collective-permute-start(bf16[400,128]{1,0:T(8,128)(2,1)S(1)} %shard_map.147.refs_0_), channel_id=1, source_target_pairs={{10,0},{8,2},{14,4},{12,6},{2,8},{0,10},{6,12},{4,14},{11,1},{9,3}... | collective-permute-start | bytes 307208 | tf_op jit(solution)/shard_map/ppermute | solution.py:415
  57.1 1.0 %shard_map.152.refs_0_ = bf16[400,128]{1,0:T(8,128)(2,1)S(1)} custom-call(bf16[400,128]{1,0:T(8,128)(2,1)S(1)} %get-tuple-element.38.refs_0_, bf16[512,384]{1,0:T(8,128)(2,1)S(1)} %get-tuple-element.26.refs_0_.pair_ref.refs_1_, bf16[512,384]{1,0:T(8,128)(2,1)S(1)} %collective-permute-done.pair_ref.refs_2_, ...), custom_call_target="tpu_custom_call" | custom-call | flops 201326592 | bytes 1048576 | tf_op jit(solution)/shard_map/pallas_call | solution.py:319
  58.1 0.3 collective-permute-done.16.refs_7_
  58.4 0.1 collective-permute-done.15.refs_6_
  58.5 6.1 %collective-permute-done.13.refs_4_ = bf16[400,128]{1,0:T(8,128)(2,1)S(1)} collective-permute-done((bf16[400,128]{1,0:T(8,128)(2,1)S(1)}, bf16[400,128]{1,0:T(8,128)(2,1)S(1)}, u32[]{:S(2)}, u32[]{:S(2)}) %collective-permute-start.13) | collective-permute-done | bytes 102432 | tf_op jit(solution)/shard_map/ppermute | solution.py:415
  64.6 1.8 %collective-permute-done.14.refs_5_ = bf16[400,128]{1,0:T(8,128)(2,1)S(1)} collective-permute-done((bf16[400,128]{1,0:T(8,128)(2,1)S(1)}, bf16[400,128]{1,0:T(8,128)(2,1)S(1)}, u32[]{:S(2)}, u32[]{:S(2)}) %collective-permute-start.14) | collective-permute-done | bytes 102432 | tf_op jit(solution)/shard_map/ppermute | solution.py:415
  66.4 1.8 %shard_map.153.after_ref = bf16[128,3072]{1,0:T(8,128)(2,1)S(1)} custom-call(bf16[2,128,128]{2,1,0:T(8,128)(2,1)S(1)} %get-tuple-element.29.places_ref, bf16[1536,3072]{1,0:T(8,128)(2,1)S(1)} %get-tuple-element.30.weight_ref, bf16[400,128]{1,0:T(8,128)(2,1)S(1)} %shard_map.152.refs_0_, bf16[400,128]{1,0:T(8,128)(2,1)S(1)} %collective-permute-done.10.refs_1_, ...), custom_call_target="tpu_custom_call" | custom-call | tf_op jit(solution)/shard_map/pallas_call | solution.py:319
  68.2 0.1 collective-permute-start.17
  68.3 1.9 %shard_map.154.own_ref = f32[128,3072]{1,0:T(8,128)S(1)} custom-call(bf16[128,3072]{1,0:T(8,128)(2,1)S(1)} %shard_map.153.after_ref, bf16[2,128,128]{2,1,0:T(8,128)(2,1)S(1)} %get-tuple-element.29.places_ref, bf16[1536,3072]{1,0:T(8,128)(2,1)S(1)} %get-tuple-element.30.weight_ref, bf16[128,3072]{1,0:T(8,128)(2,1)S(1)} %get-tuple-element.41.input_ref, ...), custom_call_target="tpu_custom_call" | custom-call | flops 1207959552 | bytes 1048576 | tf_op jit(solution)/shard_map/pallas_call | solution.py:319
  70.2 0.4 collective-permute-done.17.refs_0_
  70.6 1.3 %shard_map.155 = (bf16[128,3072]{1,0:T(8,128)(2,1)S(1)}, f32[32,128]{1,0:T(8,128)S(1)}, f32[32,128]{1,0:T(8,128)S(1)}) custom-call(s32[1,256]{1,0:T(1,128)S(1)} %get-tuple-element.28.refs_0_.mask_ref, f32[128,3072]{1,0:T(8,128)S(1)} %shard_map.154.own_ref, bf16[128,3072]{1,0:T(8,128)(2,1)S(1)} %collective-permute-done.17.refs_0_, ...), custom_call_target="tpu_custom_call" | custom-call | tf_op jit(solution)/shard_map/pallas_call | solution.py:319
  71.9 1.6 %collective-permute-start.18 = (f32[32,128]{1,0:T(8,128)S(1)}, f32[32,128]{1,0:T(8,128)S(1)}, u32[]{:S(2)}, u32[]{:S(2)}) collective-permute-start(f32[32,128]{1,0:T(8,128)S(1)} %get-tuple-element.49), channel_id=1, source_target_pairs={{0,16},{16,0},{1,17},{17,1},{2,18},{18,2},{3,19},{19,3},{4,20},{20... | collective-permute-start | bytes 49160 | tf_op jit(solution)/shard_map/ppermute | solution.py:448
  73.4 0.9 %shard_map.156 = bf16[128,3072]{1,0:T(8,128)(2,1)} custom-call(bf16[128,3072]{1,0:T(8,128)(2,1)S(1)} %get-tuple-element.47.block_ref), custom_call_target="tpu_custom_call" | custom-call | tf_op jit(solution)/shard_map/pallas_call | solution.py:319
  74.3 1.3 %collective-permute-done.18.partner_ref = f32[32,128]{1,0:T(8,128)S(1)} collective-permute-done((f32[32,128]{1,0:T(8,128)S(1)}, f32[32,128]{1,0:T(8,128)S(1)}, u32[]{:S(2)}, u32[]{:S(2)}) %collective-permute-start.18) | collective-permute-done | bytes 16416 | tf_op jit(solution)/shard_map/ppermute | solution.py:448
  75.7 0.6 shard_map.157
  (8 shorter events, 0.0 us)
Async XLA Ops:
  2.2 28.8 %collective-permute-start = (bf16[512,384]{1,0:T(8,128)(2,1)S(1)}, bf16[512,384]{1,0:T(8,128)(2,1)S(1)}, u32[]{:S(2)}, u32[]{:S(2)}) collective-permute-start(bf16[512,384]{1,0:T(8,128)(2,1)S(1)} %get-tuple-element.31), channel_id=1, source_target_pairs={{0,2},{2,0},{4,6},{6,4},{8,10},{10,8},{12,14},{14,12},{1,3},{3,1},... | collective-permute-start | bytes 1179656 | tf_op jit(solution)/shard_map/ppermute | solution.py:343
  5.3 27.7 %collective-permute-start.1 = (bf16[512,384]{1,0:T(8,128)(2,1)S(1)}, bf16[512,384]{1,0:T(8,128)(2,1)S(1)}, u32[]{:S(2)}, u32[]{:S(2)}) collective-permute-start(bf16[512,384]{1,0:T(8,128)(2,1)S(1)} %get-tuple-element.32), channel_id=1, source_target_pairs={{0,4},{2,6},{4,0},{6,2},{8,12},{10,14},{12,8},{14,10},{1,5},{3,7},... | collective-permute-start | bytes 1179656 | tf_op jit(solution)/shard_map/ppermute | solution.py:343
  6.8 27.1 %collective-permute-start.2 = (bf16[512,384]{1,0:T(8,128)(2,1)S(1)}, bf16[512,384]{1,0:T(8,128)(2,1)S(1)}, u32[]{:S(2)}, u32[]{:S(2)}) collective-permute-start(bf16[512,384]{1,0:T(8,128)(2,1)S(1)} %get-tuple-element.33), channel_id=1, source_target_pairs={{0,6},{2,4},{4,2},{6,0},{8,14},{10,12},{12,10},{14,8},{1,7},{3,5},... | collective-permute-start | bytes 1179656 | tf_op jit(solution)/shard_map/ppermute | solution.py:343
  9.0 17.5 %collective-permute-start.3 = (bf16[128,384]{1,0:T(8,128)(2,1)S(1)}, bf16[128,384]{1,0:T(8,128)(2,1)S(1)}, u32[]{:S(2)}, u32[]{:S(2)}) collective-permute-start(bf16[128,384]{1,0:T(8,128)(2,1)S(1)} %get-tuple-element.35), channel_id=1, source_target_pairs={{0,10},{2,8},{4,14},{6,12},{8,2},{10,0},{12,6},{14,4},{1,11},{3,9}... | collective-permute-start | bytes 294920 | tf_op jit(solution)/shard_map/ppermute | solution.py:361
  13.0 16.4 %collective-permute-start.4 = (bf16[128,384]{1,0:T(8,128)(2,1)S(1)}, bf16[128,384]{1,0:T(8,128)(2,1)S(1)}, u32[]{:S(2)}, u32[]{:S(2)}) collective-permute-start(bf16[128,384]{1,0:T(8,128)(2,1)S(1)} %get-tuple-element.27.refs_9_), channel_id=1, source_target_pairs={{0,8},{2,10},{4,12},{6,14},{8,0},{10,2},{12,4},{14,6},{1,9},{3,11}... | collective-permute-start | bytes 294920 | tf_op jit(solution)/shard_map/ppermute | solution.py:361
  26.5 15.4 %collective-permute-start.5 = (bf16[128,384]{1,0:T(8,128)(2,1)S(1)}, bf16[128,384]{1,0:T(8,128)(2,1)S(1)}, u32[]{:S(2)}, u32[]{:S(2)}) collective-permute-start(bf16[128,384]{1,0:T(8,128)(2,1)S(1)} %get-tuple-element.36), channel_id=1, source_target_pairs={{0,12},{2,14},{4,8},{6,10},{8,4},{10,6},{12,0},{14,2},{1,13},{3,15... | collective-permute-start | bytes 294920 | tf_op jit(solution)/shard_map/ppermute | solution.py:361
  29.3 13.5 %collective-permute-start.6 = (bf16[128,384]{1,0:T(8,128)(2,1)S(1)}, bf16[128,384]{1,0:T(8,128)(2,1)S(1)}, u32[]{:S(2)}, u32[]{:S(2)}) collective-permute-start(bf16[128,384]{1,0:T(8,128)(2,1)S(1)} %get-tuple-element.37), channel_id=1, source_target_pairs={{0,14},{2,12},{4,10},{6,8},{8,6},{10,4},{12,2},{14,0},{1,15},{3,13... | collective-permute-start | bytes 294920 | tf_op jit(solution)/shard_map/ppermute | solution.py:361
  31.0 12.8 %collective-permute-start.7 = (bf16[128,384]{1,0:T(8,128)(2,1)S(1)}, bf16[128,384]{1,0:T(8,128)(2,1)S(1)}, u32[]{:S(2)}, u32[]{:S(2)}) collective-permute-start(bf16[128,384]{1,0:T(8,128)(2,1)S(1)} %get-tuple-element.35), channel_id=1, source_target_pairs={{0,2},{2,0},{4,6},{6,4},{8,10},{10,8},{12,14},{14,12},{1,3},{3,1},... | collective-permute-start | bytes 294920 | tf_op jit(solution)/shard_map/ppermute | solution.py:362
  33.0 10.9 %collective-permute-start.8 = (bf16[128,384]{1,0:T(8,128)(2,1)S(1)}, bf16[128,384]{1,0:T(8,128)(2,1)S(1)}, u32[]{:S(2)}, u32[]{:S(2)}) collective-permute-start(bf16[128,384]{1,0:T(8,128)(2,1)S(1)} %get-tuple-element.36), channel_id=1, source_target_pairs={{0,4},{2,6},{4,0},{6,2},{8,12},{10,14},{12,8},{14,10},{1,5},{3,7},... | collective-permute-start | bytes 294920 | tf_op jit(solution)/shard_map/ppermute | solution.py:362
  33.9 9.9 %collective-permute-start.9 = (bf16[128,384]{1,0:T(8,128)(2,1)S(1)}, bf16[128,384]{1,0:T(8,128)(2,1)S(1)}, u32[]{:S(2)}, u32[]{:S(2)}) collective-permute-start(bf16[128,384]{1,0:T(8,128)(2,1)S(1)} %get-tuple-element.37), channel_id=1, source_target_pairs={{0,6},{2,4},{4,2},{6,0},{8,14},{10,12},{12,10},{14,8},{1,7},{3,5},... | collective-permute-start | bytes 294920 | tf_op jit(solution)/shard_map/ppermute | solution.py:362
  45.8 8.4 %collective-permute-start.11 = (bf16[400,128]{1,0:T(8,128)(2,1)S(1)}, bf16[400,128]{1,0:T(8,128)(2,1)S(1)}, u32[]{:S(2)}, u32[]{:S(2)}) collective-permute-start(bf16[400,128]{1,0:T(8,128)(2,1)S(1)} %get-tuple-element.39), channel_id=1, source_target_pairs={{4,0},{6,2},{0,4},{2,6},{12,8},{14,10},{8,12},{10,14},{5,1},{7,3},... | collective-permute-start | bytes 307208 | tf_op jit(solution)/shard_map/ppermute | solution.py:420
  47.8 7.1 %collective-permute-start.12 = (bf16[400,128]{1,0:T(8,128)(2,1)S(1)}, bf16[400,128]{1,0:T(8,128)(2,1)S(1)}, u32[]{:S(2)}, u32[]{:S(2)}) collective-permute-start(bf16[400,128]{1,0:T(8,128)(2,1)S(1)} %get-tuple-element.40), channel_id=1, source_target_pairs={{6,0},{4,2},{2,4},{0,6},{14,8},{12,10},{10,12},{8,14},{7,1},{5,3},... | collective-permute-start | bytes 307208 | tf_op jit(solution)/shard_map/ppermute | solution.py:420
  48.9 9.5 %collective-permute-start.16 = (bf16[400,128]{1,0:T(8,128)(2,1)S(1)}, bf16[400,128]{1,0:T(8,128)(2,1)S(1)}, u32[]{:S(2)}, u32[]{:S(2)}) collective-permute-start(bf16[400,128]{1,0:T(8,128)(2,1)S(1)} %shard_map.150.refs_0_), channel_id=1, source_target_pairs={{14,0},{12,2},{10,4},{8,6},{6,8},{4,10},{2,12},{0,14},{15,1},{13,3... | collective-permute-start | bytes 307208 | tf_op jit(solution)/shard_map/ppermute | solution.py:415
  50.9 7.6 %collective-permute-start.15 = (bf16[400,128]{1,0:T(8,128)(2,1)S(1)}, bf16[400,128]{1,0:T(8,128)(2,1)S(1)}, u32[]{:S(2)}, u32[]{:S(2)}) collective-permute-start(bf16[400,128]{1,0:T(8,128)(2,1)S(1)} %shard_map.149.refs_0_), channel_id=1, source_target_pairs={{12,0},{14,2},{8,4},{10,6},{4,8},{6,10},{0,12},{2,14},{13,1},{15,3... | collective-permute-start | bytes 307208 | tf_op jit(solution)/shard_map/ppermute | solution.py:415
  52.6 5.5 %collective-permute-start.10 = (bf16[400,128]{1,0:T(8,128)(2,1)S(1)}, bf16[400,128]{1,0:T(8,128)(2,1)S(1)}, u32[]{:S(2)}, u32[]{:S(2)}) collective-permute-start(bf16[400,128]{1,0:T(8,128)(2,1)S(1)} %get-tuple-element.38.refs_0_), channel_id=1, source_target_pairs={{2,0},{0,2},{6,4},{4,6},{10,8},{8,10},{14,12},{12,14},{3,1},{1,3},... | collective-permute-start | bytes 307208 | tf_op jit(solution)/shard_map/ppermute | solution.py:420
  54.2 10.4 %collective-permute-start.13 = (bf16[400,128]{1,0:T(8,128)(2,1)S(1)}, bf16[400,128]{1,0:T(8,128)(2,1)S(1)}, u32[]{:S(2)}, u32[]{:S(2)}) collective-permute-start(bf16[400,128]{1,0:T(8,128)(2,1)S(1)} %shard_map.148.refs_0_), channel_id=1, source_target_pairs={{8,0},{10,2},{12,4},{14,6},{0,8},{2,10},{4,12},{6,14},{9,1},{11,3}... | collective-permute-start | bytes 307208 | tf_op jit(solution)/shard_map/ppermute | solution.py:415
  54.9 11.5 %collective-permute-start.14 = (bf16[400,128]{1,0:T(8,128)(2,1)S(1)}, bf16[400,128]{1,0:T(8,128)(2,1)S(1)}, u32[]{:S(2)}, u32[]{:S(2)}) collective-permute-start(bf16[400,128]{1,0:T(8,128)(2,1)S(1)} %shard_map.147.refs_0_), channel_id=1, source_target_pairs={{10,0},{8,2},{14,4},{12,6},{2,8},{0,10},{6,12},{4,14},{11,1},{9,3}... | collective-permute-start | bytes 307208 | tf_op jit(solution)/shard_map/ppermute | solution.py:415
  68.2 2.4 %collective-permute-start.17 = (bf16[128,3072]{1,0:T(8,128)(2,1)S(1)}, bf16[128,3072]{1,0:T(8,128)(2,1)S(1)}, u32[]{:S(2)}, u32[]{:S(2)}) collective-permute-start(bf16[128,3072]{1,0:T(8,128)(2,1)S(1)} %shard_map.153.after_ref), channel_id=1, source_target_pairs={{0,1},{1,0},{2,3},{3,2},{4,5},{5,4},{6,7},{7,6},{8,9},{9,8},{10,11... | collective-permute-start | bytes 2359304 | tf_op jit(solution)/shard_map/ppermute | solution.py:432
  71.9 3.8 %collective-permute-start.18 = (f32[32,128]{1,0:T(8,128)S(1)}, f32[32,128]{1,0:T(8,128)S(1)}, u32[]{:S(2)}, u32[]{:S(2)}) collective-permute-start(f32[32,128]{1,0:T(8,128)S(1)} %get-tuple-element.49), channel_id=1, source_target_pairs={{0,16},{16,0},{1,17},{17,1},{2,18},{18,2},{3,19},{19,3},{4,20},{20... | collective-permute-start | bytes 49160 | tf_op jit(solution)/shard_map/ppermute | solution.py:448

commit v7 on v6

--- a/solution.py
+++ b/solution.py
@@ -359,7 +359,9 @@
     far_asks = []
     for a, b in far_routes:
         far_asks.append(lax.ppermute(asks[b], "ctx", route(a, b, False)))
-    near_asks = [asks[0]] + [lax.ppermute(asks[b], "ctx", route(0, b, False)) for b in range(1, members)]
+    near_asks = list(asks)
+    for b in pair_order:
+        near_asks[b] = lax.ppermute(asks[b], "ctx", route(0, b, False))
 
     wanted = (
         replay_mask,
@@ -414,10 +416,10 @@
         after = far
         parcels[far_routes[n]] = lax.ppermute(far, "ctx", route(*far_routes[n], True))
     if members > 1:
-        near = attend(after, near_asks[1:])
+        near = attend(after, [near_asks[b] for b in pair_order])
         after = near[0]
-        for b in range(1, members):
-            parcels[0, b] = lax.ppermute(near[b - 1], "ctx", route(0, b, True))
+        for n, b in enumerate(pair_order):
+            parcels[0, b] = lax.ppermute(near[n], "ctx", route(0, b, True))
     (parcels[0, 0],) = attend(after, near_asks[:1])
     parcels = [parcels[a, b] for a in range(groups) for b in range(members)]
 

time: 76.5 us -> 76.3 us (level)
    ppermute x6, starting transfers between devices: 8.49 us -> 7.31 us  [the longest x3 3.84 us: shards(): near_asks[b] = lax.ppermute(asks[b], 'ctx', route(0, b, False))]
    ppermute x4, starting transfers between devices: 6.67 us -> 7.65 us  [shards(): lax.ppermute(far, 'ctx', route(*far_routes[n], True))]
  transfers between devices with their start and end apart: 19 -> 19, of which waited for: 7 -> 8; matrix products, arithmetic and copies ran while one was open for 0% -> 0% of each run, Pallas kernels for 19% -> 19%
where the time goes in v7:
time: 76.3 us; the launch traced here: 76.1 us
  starting transfers between devices  30.1 us (39%)
  waiting for transfers between devices  23.2 us (30%)
  Pallas kernels  22 us (29%)
  between operations  0.78 us (1%)
    pallas_call x18, Pallas kernels, call(): pl.pallas_call(kernel, out_shape=outs, in_specs=in_specs or [VMEM] * len(...  22 us
    ppermute x4, waiting for transfers between devices, shards(): far_asks.append(lax.ppermute(asks[b], 'ctx', route(a, b, False)))  13.2 us
    ppermute x4, starting transfers between devices, shards(): far_asks.append(lax.ppermute(asks[b], 'ctx', route(a, b, False)))  8.86 us
    ppermute x4, waiting for transfers between devices, shards(): lax.ppermute(far, 'ctx', route(*far_routes[n], True))  8.06 us
    ppermute x4, starting transfers between devices, shards(): lax.ppermute(far, 'ctx', route(*far_routes[n], True))  7.65 us
    ppermute x3, starting transfers between devices, shards(): pairs[b] = lax.ppermute(pairs[b], 'ctx', route(0, b, False))  4.64 us
    ppermute x3, starting transfers between devices, shards(): near_asks[b] = lax.ppermute(asks[b], 'ctx', route(0, b, False))  3.84 us
    ppermute x3, starting transfers between devices, shards(): parcels[0, b] = lax.ppermute(near[n], 'ctx', route(0, b, True))  3.47 us
  transfers between devices with their start and end apart: 19, of which 8 were waited for; matrix products, arithmetic and copies ran while one was open for 0% of the time, Pallas kernels for 19%

profile of v7, /device:TPU:0, one launch (start us, length us, event | category | flops | bytes accessed | tf_op | source)
XLA Modules:
  0.0 76.1 jit_solution(304862017060389688)
XLA Ops:
  0.6 1.6 %shard_map.140 = (bf16[512,384]{1,0:T(8,128)(2,1)S(1)}, bf16[512,384]{1,0:T(8,128)(2,1)S(1)}, bf16[512,384]{1,0:T(8,128)(2,1)S(1)}, bf16[512,384]{1,0:T(8,128)(2,1)S(1)}) custom-call(bf16[256,1536]{1,0:T(8,128)(2,1)} %bitcast.12, bf16[256,1536]{1,0:T(8,128)(2,1)} %bitcast.13), custom_call_target="tpu_custom_call" | custom-call | tf_op jit(solution)/shard_map/pallas_call | solution.py:319
  2.2 3.1 %collective-permute-start = (bf16[512,384]{1,0:T(8,128)(2,1)S(1)}, bf16[512,384]{1,0:T(8,128)(2,1)S(1)}, u32[]{:S(2)}, u32[]{:S(2)}) collective-permute-start(bf16[512,384]{1,0:T(8,128)(2,1)S(1)} %get-tuple-element.31), channel_id=1, source_target_pairs={{0,2},{2,0},{4,6},{6,4},{8,10},{10,8},{12,14},{14,12},{1,3},{3,1},... | collective-permute-start | bytes 1179656 | tf_op jit(solution)/shard_map/ppermute | solution.py:343
  5.3 1.6 %collective-permute-start.1 = (bf16[512,384]{1,0:T(8,128)(2,1)S(1)}, bf16[512,384]{1,0:T(8,128)(2,1)S(1)}, u32[]{:S(2)}, u32[]{:S(2)}) collective-permute-start(bf16[512,384]{1,0:T(8,128)(2,1)S(1)} %get-tuple-element.32), channel_id=1, source_target_pairs={{0,4},{2,6},{4,0},{6,2},{8,12},{10,14},{12,8},{14,10},{1,5},{3,7},... | collective-permute-start | bytes 1179656 | tf_op jit(solution)/shard_map/ppermute | solution.py:343
  6.8 0.0 collective-permute-start.2
  6.8 2.1 %shard_map.141 = (bf16[128,384]{1,0:T(8,128)(2,1)S(1)}, bf16[128,384]{1,0:T(8,128)(2,1)S(1)}, bf16[128,384]{1,0:T(8,128)(2,1)S(1)}, bf16[128,384]{1,0:T(8,128)(2,1)S(1)}) custom-call(s32[1,256]{1,0:T(1,128)} %refs_0_.1, f32[1,128]{1,0:T(1,128)} %bitcast.18, bf16[256,1536]{1,0:T(8,128)(2,1)} %bitcast.14, ...), custom_call_target="tpu_custom_call" | custom-call | tf_op jit(solution)/shard_map/pallas_call | solution.py:319
  9.0 4.0 %collective-permute-start.3 = (bf16[128,384]{1,0:T(8,128)(2,1)S(1)}, bf16[128,384]{1,0:T(8,128)(2,1)S(1)}, u32[]{:S(2)}, u32[]{:S(2)}) collective-permute-start(bf16[128,384]{1,0:T(8,128)(2,1)S(1)} %get-tuple-element.35), channel_id=1, source_target_pairs={{0,10},{2,8},{4,14},{6,12},{8,2},{10,0},{12,6},{14,4},{1,11},{3,9}... | collective-permute-start | bytes 294920 | tf_op jit(solution)/shard_map/ppermute | solution.py:361
  13.0 0.3 collective-permute-start.4
  13.3 13.2 %collective-permute-done.3.refs_9_ = bf16[128,384]{1,0:T(8,128)(2,1)S(1)} collective-permute-done((bf16[128,384]{1,0:T(8,128)(2,1)S(1)}, bf16[128,384]{1,0:T(8,128)(2,1)S(1)}, u32[]{:S(2)}, u32[]{:S(2)}) %collective-permute-start.3) | collective-permute-done | bytes 98336 | tf_op jit(solution)/shard_map/ppermute | solution.py:361
  26.5 2.8 %collective-permute-start.5 = (bf16[128,384]{1,0:T(8,128)(2,1)S(1)}, bf16[128,384]{1,0:T(8,128)(2,1)S(1)}, u32[]{:S(2)}, u32[]{:S(2)}) collective-permute-start(bf16[128,384]{1,0:T(8,128)(2,1)S(1)} %get-tuple-element.36), channel_id=1, source_target_pairs={{0,12},{2,14},{4,8},{6,10},{8,4},{10,6},{12,0},{14,2},{1,13},{3,15... | collective-permute-start | bytes 294920 | tf_op jit(solution)/shard_map/ppermute | solution.py:361
  29.3 1.7 %collective-permute-start.6 = (bf16[128,384]{1,0:T(8,128)(2,1)S(1)}, bf16[128,384]{1,0:T(8,128)(2,1)S(1)}, u32[]{:S(2)}, u32[]{:S(2)}) collective-permute-start(bf16[128,384]{1,0:T(8,128)(2,1)S(1)} %get-tuple-element.37), channel_id=1, source_target_pairs={{0,14},{2,12},{4,10},{6,8},{8,6},{10,4},{12,2},{14,0},{1,15},{3,13... | collective-permute-start | bytes 294920 | tf_op jit(solution)/shard_map/ppermute | solution.py:361
  31.0 0.0 collective-permute-done.pair_ref.refs_2_
  31.0 1.9 %collective-permute-start.8 = (bf16[128,384]{1,0:T(8,128)(2,1)S(1)}, bf16[128,384]{1,0:T(8,128)(2,1)S(1)}, u32[]{:S(2)}, u32[]{:S(2)}) collective-permute-start(bf16[128,384]{1,0:T(8,128)(2,1)S(1)} %get-tuple-element.35), channel_id=1, source_target_pairs={{0,2},{2,0},{4,6},{6,4},{8,10},{10,8},{12,14},{14,12},{1,3},{3,1},... | collective-permute-start | bytes 294920 | tf_op jit(solution)/shard_map/ppermute | solution.py:364
  33.0 0.9 %collective-permute-start.7 = (bf16[128,384]{1,0:T(8,128)(2,1)S(1)}, bf16[128,384]{1,0:T(8,128)(2,1)S(1)}, u32[]{:S(2)}, u32[]{:S(2)}) collective-permute-start(bf16[128,384]{1,0:T(8,128)(2,1)S(1)} %get-tuple-element.36), channel_id=1, source_target_pairs={{0,4},{2,6},{4,0},{6,2},{8,12},{10,14},{12,8},{14,10},{1,5},{3,7},... | collective-permute-start | bytes 294920 | tf_op jit(solution)/shard_map/ppermute | solution.py:364
  33.9 0.0 collective-permute-done.2.pair_ref.refs_4_
  33.9 1.0 %collective-permute-start.9 = (bf16[128,384]{1,0:T(8,128)(2,1)S(1)}, bf16[128,384]{1,0:T(8,128)(2,1)S(1)}, u32[]{:S(2)}, u32[]{:S(2)}) collective-permute-start(bf16[128,384]{1,0:T(8,128)(2,1)S(1)} %get-tuple-element.37), channel_id=1, source_target_pairs={{0,6},{2,4},{4,2},{6,0},{8,14},{10,12},{12,10},{14,8},{1,7},{3,5},... | collective-permute-start | bytes 294920 | tf_op jit(solution)/shard_map/ppermute | solution.py:364
  34.9 4.3 %shard_map.142 = (s32[1,256]{1,0:T(1,128)S(1)}, f32[1,128]{1,0:T(1,128)S(1)}, bf16[1536,3072]{1,0:T(8,128)(2,1)S(1)}, bf16[128,3072]{1,0:T(8,128)(2,1)S(1)}, bf1...) custom-call(s32[1,256]{1,0:T(1,128)} %refs_0_.1, ...), custom_call_target="tpu_custom_call" | custom-call | bytes 22883328 | tf_op jit(solution)/shard_map/pallas_call | solution.py:319
  39.2 0.2 shard_map.143.refs_5_
  39.4 0.2 shard_map.146.refs_8_
  39.6 0.2 shard_map.145.refs_7_
  39.8 0.2 shard_map.144.refs_6_
  40.0 1.0 %shard_map.147.refs_0_ = bf16[400,128]{1,0:T(8,128)(2,1)S(1)} custom-call(s32[1,256]{1,0:T(1,128)S(1)} %get-tuple-element.28.refs_0_.mask_ref, bf16[512,384]{1,0:T(8,128)(2,1)S(1)} %get-tuple-element.26.refs_0_.pair_ref.refs_1_, bf16[512,384]{1,0:T(8,128)(2,1)S(1)} %collective-permute-done.pair_ref.refs_2_, ...), custom_call_target="tpu_custom_call" | custom-call | flops 201326592 | bytes 1048576 | tf_op jit(solution)/shard_map/pallas_call | solution.py:319
  40.9 1.0 %shard_map.148.refs_0_ = bf16[400,128]{1,0:T(8,128)(2,1)S(1)} custom-call(bf16[400,128]{1,0:T(8,128)(2,1)S(1)} %shard_map.147.refs_0_, bf16[512,384]{1,0:T(8,128)(2,1)S(1)} %get-tuple-element.26.refs_0_.pair_ref.refs_1_, bf16[512,384]{1,0:T(8,128)(2,1)S(1)} %collective-permute-done.pair_ref.refs_2_, ...), custom_call_target="tpu_custom_call" | custom-call | flops 201326592 | bytes 1048576 | tf_op jit(solution)/shard_map/pallas_call | solution.py:319
  41.9 0.0 collective-permute-done.5.refs_9_
  41.9 1.0 %shard_map.149.refs_0_ = bf16[400,128]{1,0:T(8,128)(2,1)S(1)} custom-call(bf16[400,128]{1,0:T(8,128)(2,1)S(1)} %shard_map.148.refs_0_, bf16[512,384]{1,0:T(8,128)(2,1)S(1)} %get-tuple-element.26.refs_0_.pair_ref.refs_1_, bf16[512,384]{1,0:T(8,128)(2,1)S(1)} %collective-permute-done.pair_ref.refs_2_, ...), custom_call_target="tpu_custom_call" | custom-call | flops 201326592 | bytes 1048576 | tf_op jit(solution)/shard_map/pallas_call | solution.py:319
  42.9 0.0 collective-permute-done.6.refs_9_
  42.9 1.0 %shard_map.150.refs_0_ = bf16[400,128]{1,0:T(8,128)(2,1)S(1)} custom-call(bf16[400,128]{1,0:T(8,128)(2,1)S(1)} %shard_map.149.refs_0_, bf16[512,384]{1,0:T(8,128)(2,1)S(1)} %get-tuple-element.26.refs_0_.pair_ref.refs_1_, bf16[512,384]{1,0:T(8,128)(2,1)S(1)} %collective-permute-done.pair_ref.refs_2_, ...), custom_call_target="tpu_custom_call" | custom-call | flops 201326592 | bytes 1048576 | tf_op jit(solution)/shard_map/pallas_call | solution.py:319
  43.9 2.0 %shard_map.151 = (bf16[400,128]{1,0:T(8,128)(2,1)S(1)}, bf16[400,128]{1,0:T(8,128)(2,1)S(1)}, bf16[400,128]{1,0:T(8,128)(2,1)S(1)}) custom-call(bf16[400,128]{1,0:T(8,128)(2,1)S(1)} %shard_map.150.refs_0_, bf16[512,384]{1,0:T(8,128)(2,1)S(1)} %get-tuple-element.26.refs_0_.pair_ref.refs_1_, bf16[512,384]{1,0:T(8,128)(2,1)S(1)} %collective-permute-done.pair_ref.refs_2_, ...), custom_call_target="tpu_custom_call" | custom-call | flops 603979776 | bytes 1048576 | tf_op jit(solution)/shard_map/pallas_call | solution.py:319
  45.8 1.6 %collective-permute-start.10 = (bf16[400,128]{1,0:T(8,128)(2,1)S(1)}, bf16[400,128]{1,0:T(8,128)(2,1)S(1)}, u32[]{:S(2)}, u32[]{:S(2)}) collective-permute-start(bf16[400,128]{1,0:T(8,128)(2,1)S(1)} %get-tuple-element.39), channel_id=1, source_target_pairs={{2,0},{0,2},{6,4},{4,6},{10,8},{8,10},{14,12},{12,14},{3,1},{1,3},... | collective-permute-start | bytes 307208 | tf_op jit(solution)/shard_map/ppermute | solution.py:422
  47.5 1.8 %collective-permute-start.12 = (bf16[400,128]{1,0:T(8,128)(2,1)S(1)}, bf16[400,128]{1,0:T(8,128)(2,1)S(1)}, u32[]{:S(2)}, u32[]{:S(2)}) collective-permute-start(bf16[400,128]{1,0:T(8,128)(2,1)S(1)} %get-tuple-element.40), channel_id=1, source_target_pairs={{6,0},{4,2},{2,4},{0,6},{14,8},{12,10},{10,12},{8,14},{7,1},{5,3},... | collective-permute-start | bytes 307208 | tf_op jit(solution)/shard_map/ppermute | solution.py:422
  49.3 3.1 %collective-permute-start.16 = (bf16[400,128]{1,0:T(8,128)(2,1)S(1)}, bf16[400,128]{1,0:T(8,128)(2,1)S(1)}, u32[]{:S(2)}, u32[]{:S(2)}) collective-permute-start(bf16[400,128]{1,0:T(8,128)(2,1)S(1)} %shard_map.150.refs_0_), channel_id=1, source_target_pairs={{14,0},{12,2},{10,4},{8,6},{6,8},{4,10},{2,12},{0,14},{15,1},{13,3... | collective-permute-start | bytes 307208 | tf_op jit(solution)/shard_map/ppermute | solution.py:417
  52.4 0.8 collective-permute-start.15
  53.1 3.6 %collective-permute-start.13 = (bf16[400,128]{1,0:T(8,128)(2,1)S(1)}, bf16[400,128]{1,0:T(8,128)(2,1)S(1)}, u32[]{:S(2)}, u32[]{:S(2)}) collective-permute-start(bf16[400,128]{1,0:T(8,128)(2,1)S(1)} %shard_map.148.refs_0_), channel_id=1, source_target_pairs={{8,0},{10,2},{12,4},{14,6},{0,8},{2,10},{4,12},{6,14},{9,1},{11,3}... | collective-permute-start | bytes 307208 | tf_op jit(solution)/shard_map/ppermute | solution.py:417
  56.8 0.2 collective-permute-start.14
  57.0 1.0 %shard_map.152.refs_0_ = bf16[400,128]{1,0:T(8,128)(2,1)S(1)} custom-call(bf16[400,128]{1,0:T(8,128)(2,1)S(1)} %get-tuple-element.38.refs_0_, bf16[512,384]{1,0:T(8,128)(2,1)S(1)} %get-tuple-element.26.refs_0_.pair_ref.refs_1_, bf16[512,384]{1,0:T(8,128)(2,1)S(1)} %collective-permute-done.pair_ref.refs_2_, ...), custom_call_target="tpu_custom_call" | custom-call | flops 201326592 | bytes 1048576 | tf_op jit(solution)/shard_map/pallas_call | solution.py:319
  57.9 0.2 collective-permute-done.11.refs_2_
  58.2 0.2 collective-permute-done.16.refs_7_
  58.4 1.4 %collective-permute-done.15.refs_6_ = bf16[400,128]{1,0:T(8,128)(2,1)S(1)} collective-permute-done((bf16[400,128]{1,0:T(8,128)(2,1)S(1)}, bf16[400,128]{1,0:T(8,128)(2,1)S(1)}, u32[]{:S(2)}, u32[]{:S(2)}) %collective-permute-start.15) | collective-permute-done | bytes 102432 | tf_op jit(solution)/shard_map/ppermute | solution.py:417
  59.8 5.4 %collective-permute-done.13.refs_4_ = bf16[400,128]{1,0:T(8,128)(2,1)S(1)} collective-permute-done((bf16[400,128]{1,0:T(8,128)(2,1)S(1)}, bf16[400,128]{1,0:T(8,128)(2,1)S(1)}, u32[]{:S(2)}, u32[]{:S(2)}) %collective-permute-start.13) | collective-permute-done | bytes 102432 | tf_op jit(solution)/shard_map/ppermute | solution.py:417
  65.2 1.0 %collective-permute-done.14.refs_5_ = bf16[400,128]{1,0:T(8,128)(2,1)S(1)} collective-permute-done((bf16[400,128]{1,0:T(8,128)(2,1)S(1)}, bf16[400,128]{1,0:T(8,128)(2,1)S(1)}, u32[]{:S(2)}, u32[]{:S(2)}) %collective-permute-start.14) | collective-permute-done | bytes 102432 | tf_op jit(solution)/shard_map/ppermute | solution.py:417
  66.2 1.8 %shard_map.153.after_ref = bf16[128,3072]{1,0:T(8,128)(2,1)S(1)} custom-call(bf16[2,128,128]{2,1,0:T(8,128)(2,1)S(1)} %get-tuple-element.29.places_ref, bf16[1536,3072]{1,0:T(8,128)(2,1)S(1)} %get-tuple-element.30.weight_ref, bf16[400,128]{1,0:T(8,128)(2,1)S(1)} %shard_map.152.refs_0_, bf16[400,128]{1,0:T(8,128)(2,1)S(1)} %collective-permute-done.10.refs_1_, ...), custom_call_target="tpu_custom_call" | custom-call | tf_op jit(solution)/shard_map/pallas_call | solution.py:319
  68.0 0.1 collective-permute-start.17
  68.1 1.9 %shard_map.154.own_ref = f32[128,3072]{1,0:T(8,128)S(1)} custom-call(bf16[128,3072]{1,0:T(8,128)(2,1)S(1)} %shard_map.153.after_ref, bf16[2,128,128]{2,1,0:T(8,128)(2,1)S(1)} %get-tuple-element.29.places_ref, bf16[1536,3072]{1,0:T(8,128)(2,1)S(1)} %get-tuple-element.30.weight_ref, bf16[128,3072]{1,0:T(8,128)(2,1)S(1)} %get-tuple-element.41.input_ref, ...), custom_call_target="tpu_custom_call" | custom-call | flops 1207959552 | bytes 1048576 | tf_op jit(solution)/shard_map/pallas_call | solution.py:319
  70.0 0.4 collective-permute-done.17.refs_0_
  70.4 1.3 %shard_map.155 = (bf16[128,3072]{1,0:T(8,128)(2,1)S(1)}, f32[32,128]{1,0:T(8,128)S(1)}, f32[32,128]{1,0:T(8,128)S(1)}) custom-call(s32[1,256]{1,0:T(1,128)S(1)} %get-tuple-element.28.refs_0_.mask_ref, f32[128,3072]{1,0:T(8,128)S(1)} %shard_map.154.own_ref, bf16[128,3072]{1,0:T(8,128)(2,1)S(1)} %collective-permute-done.17.refs_0_, ...), custom_call_target="tpu_custom_call" | custom-call | tf_op jit(solution)/shard_map/pallas_call | solution.py:319
  71.7 1.6 %collective-permute-start.18 = (f32[32,128]{1,0:T(8,128)S(1)}, f32[32,128]{1,0:T(8,128)S(1)}, u32[]{:S(2)}, u32[]{:S(2)}) collective-permute-start(f32[32,128]{1,0:T(8,128)S(1)} %get-tuple-element.49), channel_id=1, source_target_pairs={{0,16},{16,0},{1,17},{17,1},{2,18},{18,2},{3,19},{19,3},{4,20},{20... | collective-permute-start | bytes 49160 | tf_op jit(solution)/shard_map/ppermute | solution.py:450
  73.2 0.9 %shard_map.156 = bf16[128,3072]{1,0:T(8,128)(2,1)} custom-call(bf16[128,3072]{1,0:T(8,128)(2,1)S(1)} %get-tuple-element.47.block_ref), custom_call_target="tpu_custom_call" | custom-call | tf_op jit(solution)/shard_map/pallas_call | solution.py:319
  74.1 1.3 %collective-permute-done.18.partner_ref = f32[32,128]{1,0:T(8,128)S(1)} collective-permute-done((f32[32,128]{1,0:T(8,128)S(1)}, f32[32,128]{1,0:T(8,128)S(1)}, u32[]{:S(2)}, u32[]{:S(2)}) %collective-permute-start.18) | collective-permute-done | bytes 16416 | tf_op jit(solution)/shard_map/ppermute | solution.py:450
  75.5 0.6 shard_map.157
  (8 shorter events, 0.0 us)
Async XLA Ops:
  2.2 28.8 %collective-permute-start = (bf16[512,384]{1,0:T(8,128)(2,1)S(1)}, bf16[512,384]{1,0:T(8,128)(2,1)S(1)}, u32[]{:S(2)}, u32[]{:S(2)}) collective-permute-start(bf16[512,384]{1,0:T(8,128)(2,1)S(1)} %get-tuple-element.31), channel_id=1, source_target_pairs={{0,2},{2,0},{4,6},{6,4},{8,10},{10,8},{12,14},{14,12},{1,3},{3,1},... | collective-permute-start | bytes 1179656 | tf_op jit(solution)/shard_map/ppermute | solution.py:343
  5.3 27.7 %collective-permute-start.1 = (bf16[512,384]{1,0:T(8,128)(2,1)S(1)}, bf16[512,384]{1,0:T(8,128)(2,1)S(1)}, u32[]{:S(2)}, u32[]{:S(2)}) collective-permute-start(bf16[512,384]{1,0:T(8,128)(2,1)S(1)} %get-tuple-element.32), channel_id=1, source_target_pairs={{0,4},{2,6},{4,0},{6,2},{8,12},{10,14},{12,8},{14,10},{1,5},{3,7},... | collective-permute-start | bytes 1179656 | tf_op jit(solution)/shard_map/ppermute | solution.py:343
  6.8 27.1 %collective-permute-start.2 = (bf16[512,384]{1,0:T(8,128)(2,1)S(1)}, bf16[512,384]{1,0:T(8,128)(2,1)S(1)}, u32[]{:S(2)}, u32[]{:S(2)}) collective-permute-start(bf16[512,384]{1,0:T(8,128)(2,1)S(1)} %get-tuple-element.33), channel_id=1, source_target_pairs={{0,6},{2,4},{4,2},{6,0},{8,14},{10,12},{12,10},{14,8},{1,7},{3,5},... | collective-permute-start | bytes 1179656 | tf_op jit(solution)/shard_map/ppermute | solution.py:343
  9.0 17.5 %collective-permute-start.3 = (bf16[128,384]{1,0:T(8,128)(2,1)S(1)}, bf16[128,384]{1,0:T(8,128)(2,1)S(1)}, u32[]{:S(2)}, u32[]{:S(2)}) collective-permute-start(bf16[128,384]{1,0:T(8,128)(2,1)S(1)} %get-tuple-element.35), channel_id=1, source_target_pairs={{0,10},{2,8},{4,14},{6,12},{8,2},{10,0},{12,6},{14,4},{1,11},{3,9}... | collective-permute-start | bytes 294920 | tf_op jit(solution)/shard_map/ppermute | solution.py:361
  13.0 16.4 %collective-permute-start.4 = (bf16[128,384]{1,0:T(8,128)(2,1)S(1)}, bf16[128,384]{1,0:T(8,128)(2,1)S(1)}, u32[]{:S(2)}, u32[]{:S(2)}) collective-permute-start(bf16[128,384]{1,0:T(8,128)(2,1)S(1)} %get-tuple-element.27.refs_9_), channel_id=1, source_target_pairs={{0,8},{2,10},{4,12},{6,14},{8,0},{10,2},{12,4},{14,6},{1,9},{3,11}... | collective-permute-start | bytes 294920 | tf_op jit(solution)/shard_map/ppermute | solution.py:361
  26.5 15.4 %collective-permute-start.5 = (bf16[128,384]{1,0:T(8,128)(2,1)S(1)}, bf16[128,384]{1,0:T(8,128)(2,1)S(1)}, u32[]{:S(2)}, u32[]{:S(2)}) collective-permute-start(bf16[128,384]{1,0:T(8,128)(2,1)S(1)} %get-tuple-element.36), channel_id=1, source_target_pairs={{0,12},{2,14},{4,8},{6,10},{8,4},{10,6},{12,0},{14,2},{1,13},{3,15... | collective-permute-start | bytes 294920 | tf_op jit(solution)/shard_map/ppermute | solution.py:361
  29.3 13.5 %collective-permute-start.6 = (bf16[128,384]{1,0:T(8,128)(2,1)S(1)}, bf16[128,384]{1,0:T(8,128)(2,1)S(1)}, u32[]{:S(2)}, u32[]{:S(2)}) collective-permute-start(bf16[128,384]{1,0:T(8,128)(2,1)S(1)} %get-tuple-element.37), channel_id=1, source_target_pairs={{0,14},{2,12},{4,10},{6,8},{8,6},{10,4},{12,2},{14,0},{1,15},{3,13... | collective-permute-start | bytes 294920 | tf_op jit(solution)/shard_map/ppermute | solution.py:361
  31.0 12.8 %collective-permute-start.8 = (bf16[128,384]{1,0:T(8,128)(2,1)S(1)}, bf16[128,384]{1,0:T(8,128)(2,1)S(1)}, u32[]{:S(2)}, u32[]{:S(2)}) collective-permute-start(bf16[128,384]{1,0:T(8,128)(2,1)S(1)} %get-tuple-element.35), channel_id=1, source_target_pairs={{0,2},{2,0},{4,6},{6,4},{8,10},{10,8},{12,14},{14,12},{1,3},{3,1},... | collective-permute-start | bytes 294920 | tf_op jit(solution)/shard_map/ppermute | solution.py:364
  33.0 10.9 %collective-permute-start.7 = (bf16[128,384]{1,0:T(8,128)(2,1)S(1)}, bf16[128,384]{1,0:T(8,128)(2,1)S(1)}, u32[]{:S(2)}, u32[]{:S(2)}) collective-permute-start(bf16[128,384]{1,0:T(8,128)(2,1)S(1)} %get-tuple-element.36), channel_id=1, source_target_pairs={{0,4},{2,6},{4,0},{6,2},{8,12},{10,14},{12,8},{14,10},{1,5},{3,7},... | collective-permute-start | bytes 294920 | tf_op jit(solution)/shard_map/ppermute | solution.py:364
  33.9 10.0 %collective-permute-start.9 = (bf16[128,384]{1,0:T(8,128)(2,1)S(1)}, bf16[128,384]{1,0:T(8,128)(2,1)S(1)}, u32[]{:S(2)}, u32[]{:S(2)}) collective-permute-start(bf16[128,384]{1,0:T(8,128)(2,1)S(1)} %get-tuple-element.37), channel_id=1, source_target_pairs={{0,6},{2,4},{4,2},{6,0},{8,14},{10,12},{12,10},{14,8},{1,7},{3,5},... | collective-permute-start | bytes 294920 | tf_op jit(solution)/shard_map/ppermute | solution.py:364
  45.8 7.3 %collective-permute-start.10 = (bf16[400,128]{1,0:T(8,128)(2,1)S(1)}, bf16[400,128]{1,0:T(8,128)(2,1)S(1)}, u32[]{:S(2)}, u32[]{:S(2)}) collective-permute-start(bf16[400,128]{1,0:T(8,128)(2,1)S(1)} %get-tuple-element.39), channel_id=1, source_target_pairs={{2,0},{0,2},{6,4},{4,6},{10,8},{8,10},{14,12},{12,14},{3,1},{1,3},... | collective-permute-start | bytes 307208 | tf_op jit(solution)/shard_map/ppermute | solution.py:422
  47.5 9.3 %collective-permute-start.12 = (bf16[400,128]{1,0:T(8,128)(2,1)S(1)}, bf16[400,128]{1,0:T(8,128)(2,1)S(1)}, u32[]{:S(2)}, u32[]{:S(2)}) collective-permute-start(bf16[400,128]{1,0:T(8,128)(2,1)S(1)} %get-tuple-element.40), channel_id=1, source_target_pairs={{6,0},{4,2},{2,4},{0,6},{14,8},{12,10},{10,12},{8,14},{7,1},{5,3},... | collective-permute-start | bytes 307208 | tf_op jit(solution)/shard_map/ppermute | solution.py:422
  49.3 9.1 %collective-permute-start.16 = (bf16[400,128]{1,0:T(8,128)(2,1)S(1)}, bf16[400,128]{1,0:T(8,128)(2,1)S(1)}, u32[]{:S(2)}, u32[]{:S(2)}) collective-permute-start(bf16[400,128]{1,0:T(8,128)(2,1)S(1)} %shard_map.150.refs_0_), channel_id=1, source_target_pairs={{14,0},{12,2},{10,4},{8,6},{6,8},{4,10},{2,12},{0,14},{15,1},{13,3... | collective-permute-start | bytes 307208 | tf_op jit(solution)/shard_map/ppermute | solution.py:417
  52.4 7.4 %collective-permute-start.15 = (bf16[400,128]{1,0:T(8,128)(2,1)S(1)}, bf16[400,128]{1,0:T(8,128)(2,1)S(1)}, u32[]{:S(2)}, u32[]{:S(2)}) collective-permute-start(bf16[400,128]{1,0:T(8,128)(2,1)S(1)} %shard_map.149.refs_0_), channel_id=1, source_target_pairs={{12,0},{14,2},{8,4},{10,6},{4,8},{6,10},{0,12},{2,14},{13,1},{15,3... | collective-permute-start | bytes 307208 | tf_op jit(solution)/shard_map/ppermute | solution.py:417
  53.1 5.0 %collective-permute-start.11 = (bf16[400,128]{1,0:T(8,128)(2,1)S(1)}, bf16[400,128]{1,0:T(8,128)(2,1)S(1)}, u32[]{:S(2)}, u32[]{:S(2)}) collective-permute-start(bf16[400,128]{1,0:T(8,128)(2,1)S(1)} %get-tuple-element.38.refs_0_), channel_id=1, source_target_pairs={{4,0},{6,2},{0,4},{2,6},{12,8},{14,10},{8,12},{10,14},{5,1},{7,3},... | collective-permute-start | bytes 307208 | tf_op jit(solution)/shard_map/ppermute | solution.py:422
  53.1 12.1 %collective-permute-start.13 = (bf16[400,128]{1,0:T(8,128)(2,1)S(1)}, bf16[400,128]{1,0:T(8,128)(2,1)S(1)}, u32[]{:S(2)}, u32[]{:S(2)}) collective-permute-start(bf16[400,128]{1,0:T(8,128)(2,1)S(1)} %shard_map.148.refs_0_), channel_id=1, source_target_pairs={{8,0},{10,2},{12,4},{14,6},{0,8},{2,10},{4,12},{6,14},{9,1},{11,3}... | collective-permute-start | bytes 307208 | tf_op jit(solution)/shard_map/ppermute | solution.py:417
  56.8 9.5 %collective-permute-start.14 = (bf16[400,128]{1,0:T(8,128)(2,1)S(1)}, bf16[400,128]{1,0:T(8,128)(2,1)S(1)}, u32[]{:S(2)}, u32[]{:S(2)}) collective-permute-start(bf16[400,128]{1,0:T(8,128)(2,1)S(1)} %shard_map.147.refs_0_), channel_id=1, source_target_pairs={{10,0},{8,2},{14,4},{12,6},{2,8},{0,10},{6,12},{4,14},{11,1},{9,3}... | collective-permute-start | bytes 307208 | tf_op jit(solution)/shard_map/ppermute | solution.py:417
  68.0 2.4 %collective-permute-start.17 = (bf16[128,3072]{1,0:T(8,128)(2,1)S(1)}, bf16[128,3072]{1,0:T(8,128)(2,1)S(1)}, u32[]{:S(2)}, u32[]{:S(2)}) collective-permute-start(bf16[128,3072]{1,0:T(8,128)(2,1)S(1)} %shard_map.153.after_ref), channel_id=1, source_target_pairs={{0,1},{1,0},{2,3},{3,2},{4,5},{5,4},{6,7},{7,6},{8,9},{9,8},{10,11... | collective-permute-start | bytes 2359304 | tf_op jit(solution)/shard_map/ppermute | solution.py:434
  71.7 3.8 %collective-permute-start.18 = (f32[32,128]{1,0:T(8,128)S(1)}, f32[32,128]{1,0:T(8,128)S(1)}, u32[]{:S(2)}, u32[]{:S(2)}) collective-permute-start(f32[32,128]{1,0:T(8,128)S(1)} %get-tuple-element.49), channel_id=1, source_target_pairs={{0,16},{16,0},{1,17},{17,1},{2,18},{18,2},{3,19},{19,3},{4,20},{20... | collective-permute-start | bytes 49160 | tf_op jit(solution)/shard_map/ppermute | solution.py:450
